TPU v7x, 32 devices: a whole 2x2x4 slice. The times are simulated.
32 devices in a mesh: img: 4 (over x, core), cls: 4 (over z), tpl: 2 (over y).
Axes of the slice: x: 2, y: 2, z: 4, core: 2. Of those that a mesh axis runs over, the one named last changes fastest.
Arguments:
- images: bfloat16 [2048, 1280], P(('img', 'tpl')), may hold values from -5 to 5
- labels: int32 [2048], P(('img', 'tpl')), may hold values from 0 to 1023
- templates: bfloat16 [8, 1024, 1280], P('tpl', ('cls', 'img')), may hold values from -0.125 to 0.125
- projection: bfloat16 [1280, 1280], P('img', 'cls'), may hold values from -0.08441157 to 0.08441157
Outputs:
- grad_templates: bfloat16 [8, 1024, 1280], P('tpl', ('cls', 'img'))
- grad_projection: float32 [1280, 1280], P('img', 'cls')
All inputs are finite; a program needn't handle non-finite values.
Results may differ from a plain program's by a relative error of at most 0.011.
Values may be sent and summed in bfloat16 or wider, within the bound.
No kernel may reach another device: no remote copies, remote signals or barrier semaphores. Data moves between devices by JAX's collectives and lax.ppermute only.
A program may use at most 64 MiB of HBM per device.

v0:
```python
import jax
import jax.numpy as jnp
from jax import lax
from jax.sharding import PartitionSpec as P

logit_scale = 50.0
epsilon = 1e-06


def inverse_norm(values):
    return lax.rsqrt(jnp.sum(values * values, axis=-1, keepdims=True) + epsilon)


def body(images, labels, templates, projection):
    tpl_count = templates.shape[0]
    cls_count = templates.shape[1]
    feat_width = templates.shape[2]
    tpl_total = tpl_count * lax.axis_size("tpl")
    img_count = lax.axis_size("img")
    wide_proj = lax.all_gather(projection, "cls", axis=1, tiled=True)
    full_proj = lax.all_gather(wide_proj, "img", axis=0, tiled=True)
    flat_tpl = templates.reshape(tpl_count * cls_count, feat_width)
    text_z = jnp.dot(flat_tpl, full_proj, preferred_element_type=jnp.float32)
    text_rz = inverse_norm(text_z)
    text_u = text_z * text_rz
    u_three = text_u.reshape(tpl_count, cls_count, feat_width)
    local_sum = jnp.sum(u_three, axis=0)
    mean_emb = lax.psum(local_sum, "tpl") / tpl_total
    mean_rn = inverse_norm(mean_emb)
    class_w = mean_emb * mean_rn
    class_b = class_w.astype(jnp.bfloat16)
    img_f = images.astype(jnp.float32)
    img_b = (img_f * inverse_norm(img_f)).astype(jnp.bfloat16)
    class_panel = lax.all_gather(class_b, "img", axis=0, tiled=True)
    scores = logit_scale * jnp.einsum(
        "cd,nd->cn", class_panel, img_b, preferred_element_type=jnp.float32
    )
    exp_scores = jnp.exp(scores)
    totals = lax.psum(jnp.sum(exp_scores, axis=0), "cls")
    first_id = lax.axis_index("cls") * img_count * cls_count
    class_ids = first_id + lax.broadcasted_iota(jnp.int32, (class_panel.shape[0], 1), 0)
    one_hot = (labels[None, :] == class_ids).astype(jnp.float32)
    grad_logit = (exp_scores / totals[None, :] - one_hot).astype(jnp.bfloat16)
    spread = lax.psum_scatter(
        logit_scale * jnp.dot(grad_logit, img_b, preferred_element_type=jnp.float32),
        "img",
        scatter_dimension=0,
        tiled=True,
    )
    class_g = lax.psum(spread, "tpl")
    dot_wg = jnp.sum(class_w * class_g, axis=1, keepdims=True)
    grad_mean = (class_g - class_w * dot_wg) * mean_rn
    per_u = grad_mean / tpl_total
    inner_prod = jnp.sum(u_three * per_u[None], axis=2, keepdims=True)
    grad_z = (
        (per_u[None] - u_three * inner_prod) * text_rz.reshape(tpl_count, cls_count, 1)
    ).astype(jnp.bfloat16)
    grad_flat = grad_z.reshape(tpl_count * cls_count, feat_width)
    grad_tpl = lax.dot_general(
        grad_flat, full_proj, (((1,), (1,)), ((), ())), preferred_element_type=jnp.float32
    )
    grad_templates = grad_tpl.astype(jnp.bfloat16).reshape(tpl_count, cls_count, feat_width)
    tpl_columns = lax.all_to_all(flat_tpl, "img", split_axis=1, concat_axis=0, tiled=True)
    partial_proj = lax.dot_general(
        tpl_columns,
        lax.all_gather(grad_flat, "img", axis=0, tiled=True),
        (((0,), (0,)), ((), ())),
        preferred_element_type=jnp.float32,
    )
    shared_proj = lax.psum_scatter(
        partial_proj.astype(jnp.bfloat16), "cls", scatter_dimension=1, tiled=True
    )
    grad_projection = lax.psum(shared_proj, "tpl").astype(jnp.float32)
    return (grad_templates, grad_projection)


def solution(mesh):
    in_specs = (
        P(("img", "tpl"), None),
        P(("img", "tpl")),
        P("tpl", ("cls", "img"), None),
        P("img", "cls"),
    )
    out_specs = (P("tpl", ("cls", "img"), None), P("img", "cls"))
    return jax.shard_map(body, mesh=mesh, in_specs=in_specs, out_specs=out_specs, check_vma=False)
```

profile of v0, /device:TPU:0, one launch (start us, length us, event | category | flops | bytes accessed | tf_op | source)
XLA Modules:
  0.0 261.0 jit_solution(5731900698816479913)
XLA Ops:
  7.2 1.1 copy.10
  8.3 23.5 %all_gather.12 = bf16[320,1280]{0,1:T(8,128)(2,1)S(1)} all-gather(bf16[320,320]{0,1:T(8,128)(2,1)S(1)} %copy.10), channel_id=1, replica_groups=mesh['img'=4,'cls'=4,'tpl'=2] {'cls'}, dimensions={1}, use_global_device_ids=true | all-gather | bytes 1024000 | tf_op jit(solution)/shard_map/all_gather | solution.py:20
  31.8 1.3 copy.11
  33.2 0.2 fusion.1
  33.4 29.0 %all-gather.3.cloned.1.call-done = bf16[1280,1280]{1,0:T(8,128)(2,1)} async-done(((bf16[320,1280]{1,0:T(8,128)(2,1)}), bf16[1280,1280]{1,0:T(8,128)(2,1)}) %all-gather.3.cloned.1.call-update) | async-done | bytes 3276816 | tf_op jit(solution)/shard_map/all_gather | solution.py:21
  62.4 3.0 %multiply_reduce_fusion = (f32[256]{0:T(256)S(1)}, f32[256,1280]{1,0:T(8,128)S(1)}) fusion(bf16[256,1280]{1,0:T(8,128)(2,1)S(1)} %bitcast.29, bf16[1280,1280]{1,0:T(8,128)(2,1)} %all-gather.3.cloned.1.call-done), kind=kOutput, calls=%fused_computation.13 | convolution fusion | flops 839515904 | bytes 5243904 | tf_op jit(solution)/shard_map/dot_general | solution.py:23
  65.5 0.2 broadcast_multiply_fusion
  65.7 0.8 reduce_sum.64
  66.6 24.4 %all-reduce.4.cloned.1.call-done = f32[64,1280]{1,0:T(8,128)} async-done(((f32[64,1280]{1,0:T(8,128)}), f32[64,1280]{1,0:T(8,128)}) %all-reduce.4.cloned.1.call-update) | async-done | bytes 327696 | tf_op jit(solution)/shard_map/psum | solution.py:28
  91.0 1.1 multiply_reduce_fusion.2
  92.1 1.1 multiply_convert_fusion
  93.2 7.9 %all_gather.14 = bf16[256,1280]{1,0:T(8,128)(2,1)S(1)} all-gather(bf16[64,1280]{1,0:T(8,128)(2,1)S(1)} %multiply_convert_fusion), channel_id=1, replica_groups=mesh['img'=4,'cls'=4,'tpl'=2] {'img'}, dimensions={0}, use_global_device_ids=true | all-gather | bytes 819200 | tf_op jit(solution)/shard_map/all_gather | solution.py:34
  101.1 0.5 fusion.12
  101.5 11.7 %psum.29 = f32[256]{0:T(256)S(1)} all-reduce(f32[256]{0:T(256)S(1)} %get-tuple-element.6), channel_id=1, replica_groups=mesh['img'=4,'cls'=4,'tpl'=2] {'cls'}, use_global_device_ids=true, to_apply=%region_6.0 | all-reduce | flops 256 | bytes 2048 | tf_op jit(solution)/shard_map/psum | solution.py:39
  113.2 1.5 convolution_multiply_fusion
  114.8 23.3 %reduce-scatter.5.cloned.1.call-done = f32[64,1280]{1,0:T(8,128)} async-done(((f32[256,1280]{1,0:T(8,128)}), f32[64,1280]{1,0:T(8,128)}) %reduce-scatter.5.cloned.1.call-update) | async-done | bytes 327696 | tf_op jit(solution)/shard_map/reduce_scatter | solution.py:44
  138.2 26.4 %all-reduce.6.cloned.1.call-done = f32[64,1280]{1,0:T(8,128)} async-done(((f32[64,1280]{1,0:T(8,128)}), f32[64,1280]{1,0:T(8,128)}) %all-reduce.6.cloned.1.call-update) | async-done | bytes 327696 | tf_op jit(solution)/shard_map/psum | solution.py:50
  164.6 1.2 multiply_reduce_fusion.1
  165.8 1.1 multiply_multiply_fusion
  166.9 0.3 fusion.3
  167.2 1.1 fusion.5
  168.4 0.9 all_to_all.14
  169.3 0.6 copy.12
  169.9 17.5 %all_to_all.19 = bf16[256,4,320]{0,2,1:T(8,128)(2,1)S(1)} all-to-all(bf16[256,4,320]{0,2,1:T(8,128)(2,1)S(1)} %copy.12), channel_id=1, replica_groups=mesh['img'=4,'cls'=4,'tpl'=2] {'img'}, dimensions={1} | all-to-all | bytes 1310720 | tf_op jit(solution)/shard_map/all_to_all | solution.py:63
  187.5 10.8 %all-gather.5.cloned.1.call-done = bf16[1024,1280]{1,0:T(8,128)(2,1)} async-done(((bf16[256,1280]{1,0:T(8,128)(2,1)}), bf16[1024,1280]{1,0:T(8,128)(2,1)}) %all-gather.5.cloned.1.call-update) | async-done | bytes 2621456 | tf_op jit(solution)/shard_map/all_gather | solution.py:66
  198.3 2.7 %fusion = bf16[320,1280]{1,0:T(8,128)(2,1)S(1)} fusion(bf16[1024,320]{0,1:T(8,128)(2,1)S(1)} %bitcast.30, bf16[1024,1280]{1,0:T(8,128)(2,1)} %all-gather.5.cloned.1.call-done), kind=kOutput, calls=%fused_computation.3 | convolution fusion | flops 839270400 | bytes 4096000 | tf_op jit(solution)/shard_map/dot_general | solution.py:64
  201.0 1.3 copy.14
  202.4 25.5 %reduce-scatter.7.cloned.1.call-done = bf16[320,320]{1,0:T(8,128)(2,1)} async-done(((bf16[1280,320]{1,0:T(8,128)(2,1)}), bf16[320,320]{1,0:T(8,128)(2,1)}) %reduce-scatter.7.cloned.1.call-update) | async-done | bytes 204816
  227.9 1.8 copy.15
  229.7 3.8 %convolution_convert_fusion.1 = bf16[256,1280]{1,0:T(8,128)(2,1)} fusion(bf16[256,1280]{1,0:T(8,128)(2,1)S(1)} %copy-done.1, bf16[1280,1280]{1,0:T(8,128)(2,1)} %all-gather.3.cloned.1.call-done), kind=kOutput, calls=%fused_computation.2 | convolution fusion | flops 839188480 | bytes 4587520 | tf_op jit(solution)/shard_map/dot_general | solution.py:59
  233.5 18.9 %all-reduce.8.cloned.1.call-done = bf16[320,320]{1,0:T(8,128)(2,1)} async-done(((bf16[320,320]{1,0:T(8,128)(2,1)}), bf16[320,320]{1,0:T(8,128)(2,1)}) %all-reduce.8.cloned.1.call-update) | async-done | bytes 204816 | tf_op jit(solution)/shard_map/psum | solution.py:73
  252.4 1.8 convert_element_type.40
  (31 shorter events, 0.5 us)
Async XLA Ops:
  7.2 55.3 %all-gather.3.cloned.1.call-start = ((), (), s32[]{:S(2)}) async-start(), calls=%async_computation.3 | async-start | bytes 4096000 | tf_op jit(solution)/shard_map/all_gather | solution.py:21
  31.8 1.4 copy-start.2
  31.8 30.6 %copy-start.3 = (bf16[4,64,1280]{2,1,0:T(8,128)(2,1)S(1)}, bf16[4,64,1280]{2,1,0:T(8,128)(2,1)}, u32[]{:S(2)}) copy-start(bf16[4,64,1280]{2,1,0:T(8,128)(2,1)} %param.6) | copy-start | bytes 1966084
  33.1 57.9 %all-reduce.4.cloned.1.call-start = ((), (), s32[]{:S(2)}) async-start(), calls=%async_computation.4 | async-start | bytes 655360 | tf_op jit(solution)/shard_map/psum | solution.py:28
  66.5 71.6 %reduce-scatter.5.cloned.1.call-start = ((), (), s32[]{:S(2)}) async-start(), calls=%async_computation.5 | async-start | bytes 1638400 | tf_op jit(solution)/shard_map/reduce_scatter | solution.py:44
  93.2 20.1 %copy-start.5 = (s32[256]{0:T(256)S(1)}, s32[256]{0:T(256)}, u32[]{:S(2)}) copy-start(s32[256]{0:T(256)} %param.5) | copy-start | bytes 3076
  114.7 49.9 %copy-start = (f32[64,1280]{1,0:T(8,128)S(1)}, f32[64,1280]{1,0:T(8,128)}, u32[]{:S(2)}) copy-start(f32[64,1280]{1,0:T(8,128)} %all-reduce.4.cloned.1.call-done) | copy-start | bytes 983044
  114.8 49.8 %all-reduce.6.cloned.1.call-start = ((), (), s32[]{:S(2)}) async-start(), calls=%async_computation.6 | async-start | bytes 655360 | tf_op jit(solution)/shard_map/psum | solution.py:50
  138.1 60.2 %all-gather.5.cloned.1.call-start = ((), (), s32[]{:S(2)}) async-start(), calls=%async_computation.7 | async-start | bytes 3276800 | tf_op jit(solution)/shard_map/all_gather | solution.py:66
  167.2 1.2 copy-start.4
  168.4 59.5 %reduce-scatter.7.cloned.1.call-start = ((), (), s32[]{:S(2)}) async-start(), calls=%async_computation.9 | async-start | bytes 1228800
  202.3 27.4 %copy-start.1 = (bf16[256,1280]{1,0:T(8,128)(2,1)S(1)}, bf16[256,1280]{1,0:T(8,128)(2,1)}, u32[]{:S(2)}) copy-start(bf16[256,1280]{1,0:T(8,128)(2,1)} %fusion.5) | copy-start | bytes 1966084
  202.4 50.0 %all-reduce.8.cloned.1.call-start = ((), (), s32[]{:S(2)}) async-start(), calls=%async_computation.8 | async-start | bytes 491520 | tf_op jit(solution)/shard_map/psum | solution.py:73
Sparse Core Ops, SparseCore 0:
  33.2 29.1 all-gather.2
  66.6 24.3 all-reduce.3
  114.9 23.1 reduce-scatter.4
  140.2 24.3 all-reduce.5
  168.5 29.7 all-gather.4
  202.5 25.3 reduce-scatter.6
  230.7 21.6 all-reduce.7
where the time goes:
time: 262 us; the launch traced here: 261 us
  waiting for transfers between devices  158 us (60%)
  blocking collectives  60.5 us (23%)
  between operations  14.3 us (5%)
  matrix products  11.6 us (4%)
  other arithmetic  8.86 us (3%)
  local copies, waits for them, and re-layouts  7.09 us (3%)
    all_gather x1, waiting for transfers between devices, body(): full_proj = lax.all_gather(wide_proj, 'img', axis=0, tiled=True)  29 us
    psum x1, waiting for transfers between devices, body(): class_g = lax.psum(spread, 'tpl')  26.4 us
    unnamed x8, waiting for transfers between devices  25.6 us
    psum x1, waiting for transfers between devices, body(): mean_emb = lax.psum(local_sum, 'tpl') / tpl_total  24.4 us
    all_gather x1, blocking collectives, body(): wide_proj = lax.all_gather(projection, 'cls', axis=1, tiled=True)  23.5 us
    reduce_scatter x1, waiting for transfers between devices, body(): lax.psum_scatter(logit_scale * jnp.dot(grad_logit, img_b, preferred_eleme...  23.3 us
    psum x1, waiting for transfers between devices, body(): grad_projection = lax.psum(shared_proj, 'tpl').astype(jnp.float32)  18.9 us
    all_to_all x1, blocking collectives, body(): lax.all_to_all(flat_tpl, 'img', split_axis=1, concat_axis=0, tiled=True)  17.5 us
  transfers between devices with their start and end apart: 7, of which 7 were waited for; matrix products, arithmetic and copies ran while one was open for 2% of the time, Pallas kernels for 0%

commit v1 on v0

--- a/solution.py
+++ b/solution.py
@@ -1,17 +1,25 @@
+import functools
+
 import jax
 import jax.numpy as jnp
 from jax import lax
+from jax.experimental import pallas as pl
+from jax.experimental.pallas import tpu as pltpu
 from jax.sharding import PartitionSpec as P
 
 logit_scale = 50.0
 epsilon = 1e-06
+MIB = 1 << 20
+VM = pl.BlockSpec(memory_space=pltpu.VMEM)
+HB = pl.BlockSpec(memory_space=pl.ANY)
+SM = pl.BlockSpec(memory_space=pltpu.SMEM)
 
 
 def inverse_norm(values):
     return lax.rsqrt(jnp.sum(values * values, axis=-1, keepdims=True) + epsilon)
 
 
-def body(images, labels, templates, projection):
+def general_body(images, labels, templates, projection):
     tpl_count = templates.shape[0]
     cls_count = templates.shape[1]
     feat_width = templates.shape[2]
@@ -74,7 +82,261 @@
     return (grad_templates, grad_projection)
 
 
+def sds(shape, dtype):
+    return jax.ShapeDtypeStruct(shape, dtype)
+
+
+def swap(x, axis, mask):
+    n = lax.axis_size(axis)
+    return lax.ppermute(x, axis, [(i, i ^ mask) for i in range(n)])
+
+
+def params(mib):
+    return pltpu.CompilerParams(vmem_limit_bytes=mib * MIB)
+
+
+def load_projection(me_ref, piece_refs, full_ref, sem):
+    copies = []
+    for k, piece in enumerate(piece_refs):
+        copy = pltpu.make_async_copy(piece, full_ref.at[me_ref[0] ^ k], sem.at[k])
+        copy.start()
+        copies.append(copy)
+    for copy in copies:
+        copy.wait()
+
+
+def text_kernel(n_img, n_tpl, me_ref, tpl_ref, *rest):
+    pieces = rest[:n_img]
+    u_ref, rz_ref, sum_ref, send_ref, full_ref, sem = rest[n_img:]
+    load_projection(me_ref, pieces, full_ref, sem)
+    feat = tpl_ref.shape[1]
+    full = full_ref[...].reshape(feat, feat)
+    z = jnp.dot(tpl_ref[...], full, preferred_element_type=jnp.float32)
+    rz = inverse_norm(z)
+    u = z * rz
+    u_ref[...] = u
+    rz_ref[...] = rz
+    rows = u.shape[0] // n_tpl
+    total = u[:rows]
+    for t in range(1, n_tpl):
+        total = total + u[t * rows : (t + 1) * rows]
+    sum_ref[...] = total
+    send_ref[...] = total.astype(jnp.bfloat16)
+
+
+def score_kernel(tpl_total, n_piece, n_other, sum_ref, *rest):
+    others = rest[:n_other]
+    images = rest[n_other : n_other + n_piece]
+    w_ref, rn_ref, e_ref, tot_ref = rest[n_other + n_piece :]
+    mean = sum_ref[...]
+    for other in others:
+        mean = mean + other[...].astype(jnp.float32)
+    mean = mean / tpl_total
+    rn = inverse_norm(mean)
+    w = mean * rn
+    w_ref[...] = w
+    rn_ref[...] = rn
+    wb = w.astype(jnp.bfloat16)
+    for k, image in enumerate(images):
+        scores = logit_scale * lax.dot_general(
+            wb, image[...], (((1,), (1,)), ((), ())), preferred_element_type=jnp.float32
+        )
+        e = jnp.exp(scores)
+        e_ref[k] = e
+        tot_ref[k : k + 1] = jnp.sum(e, axis=0, keepdims=True)
+
+
+def grad_kernel(tpl_total, n_tpl, n_piece, n_tot, first_ref, *rest):
+    tots = rest[:n_tot]
+    images = rest[n_tot : n_tot + n_piece]
+    e_ref, lab_ref, w_ref, rn_ref, u_ref, rz_ref, gz_ref = rest[n_tot + n_piece :]
+    totals = tots[0][...]
+    for other in tots[1:]:
+        totals = totals + other[...]
+    inv = 1.0 / totals
+    rows, feat = w_ref.shape
+    acc = jnp.zeros((rows, feat), jnp.float32)
+    ids = first_ref[0] + lax.broadcasted_iota(jnp.int32, (rows, e_ref.shape[2]), 0)
+    for k, image in enumerate(images):
+        hot = (lab_ref[k : k + 1, :] == ids).astype(jnp.float32)
+        gl = (e_ref[k] * inv[k : k + 1] - hot).astype(jnp.bfloat16)
+        acc = acc + jnp.dot(gl, image[...], preferred_element_type=jnp.float32)
+    g = logit_scale * acc
+    w = w_ref[...]
+    dot_wg = jnp.sum(w * g, axis=1, keepdims=True)
+    per_u = (g - w * dot_wg) * rn_ref[...] / tpl_total
+    for t in range(n_tpl):
+        sl = slice(t * rows, (t + 1) * rows)
+        u = u_ref[sl]
+        inner = jnp.sum(u * per_u, axis=1, keepdims=True)
+        gz_ref[sl] = ((per_u - u * inner) * rz_ref[sl]).astype(jnp.bfloat16)
+
+
+def back_kernel(n_img, me_ref, gz_ref, *rest):
+    pieces = rest[:n_img]
+    out_ref, full_ref, sem = rest[n_img:]
+    load_projection(me_ref, pieces, full_ref, sem)
+    feat = gz_ref.shape[1]
+    full = full_ref[...].reshape(feat, feat)
+    out_ref[...] = lax.dot_general(
+        gz_ref[...], full, (((1,), (1,)), ((), ())), preferred_element_type=jnp.float32
+    ).astype(jnp.bfloat16)
+
+
+def outer_kernel(n_img, n_cls, *rest):
+    tpl = rest[:n_img]
+    grads = rest[n_img : 2 * n_img]
+    out_ref = rest[2 * n_img]
+    acc = jnp.dot(tpl[0][...], grads[0][...], preferred_element_type=jnp.float32)
+    for k in range(1, n_img):
+        acc = acc + jnp.dot(tpl[k][...], grads[k][...], preferred_element_type=jnp.float32)
+    width = acc.shape[1] // n_cls
+    for j in range(n_cls):
+        out_ref[j] = acc[:, j * width : (j + 1) * width].astype(jnp.bfloat16)
+
+
+def body(images, labels, templates, projection):
+    tpl_count, cls_count, feat = templates.shape
+    n_tpl, n_img, n_cls = (lax.axis_size(a) for a in ("tpl", "img", "cls"))
+    tpl_total = tpl_count * n_tpl
+    flat_rows = tpl_count * cls_count
+    f32, bf16 = jnp.float32, jnp.bfloat16
+    me = lax.axis_index("img")
+    me_arr = me.astype(jnp.int32).reshape(1)
+    far = range(2, n_img, 2)
+
+    img_f = images.astype(f32)
+    img_b = (img_f * inverse_norm(img_f)).astype(bf16)
+    pieces = {(0, 0): (img_b, labels)}
+
+    def move(key, axis, mask, new):
+        pieces[new] = tuple(swap(a, axis, mask) for a in pieces[key])
+
+    for m in far:
+        move((0, 0), "img", m, (0, m))
+    for t in range(1, n_tpl):
+        for m in (0, *far):
+            move((0, m), "tpl", t, (t, m))
+    for key in list(pieces):
+        move(key, "img", 1, (key[0], key[1] ^ 1))
+    order = [(t, m) for t in range(n_tpl) for m in range(n_img)]
+    where = {key: k for k, key in enumerate(order)}
+    image_list = [pieces[key][0] for key in order]
+    label_arr = jnp.stack([pieces[key][1] for key in order])
+    n_piece = len(order)
+    img_rows = images.shape[0]
+
+    wide = lax.all_gather(projection, "cls", axis=1, tiled=True)
+    proj = {0: wide}
+    for m in far:
+        proj[m] = swap(wide, "img", m)
+    for m in (0, *far):
+        proj[m ^ 1] = swap(proj[m], "img", 1)
+    proj_list = [proj[m] for m in range(n_img)]
+    proj_rows = projection.shape[0]
+
+    flat_tpl = templates.reshape(flat_rows, feat)
+    u, rz, local_sum, send_sum = pl.pallas_call(
+        functools.partial(text_kernel, n_img, tpl_count),
+        out_shape=(
+            sds((flat_rows, feat), f32),
+            sds((flat_rows, 1), f32),
+            sds((cls_count, feat), f32),
+            sds((cls_count, feat), bf16),
+        ),
+        in_specs=[SM, VM] + [HB] * n_img,
+        out_specs=(VM, VM, VM, VM),
+        scratch_shapes=[
+            pltpu.VMEM((n_img, proj_rows, feat), bf16),
+            pltpu.SemaphoreType.DMA((n_img,)),
+        ],
+        compiler_params=params(24),
+        name="text",
+    )(me_arr, flat_tpl, *proj_list)
+
+    others = [swap(send_sum, "tpl", t) for t in range(1, n_tpl)]
+    class_w, mean_rn, e, tot = pl.pallas_call(
+        functools.partial(score_kernel, tpl_total, n_piece, len(others)),
+        out_shape=(
+            sds((cls_count, feat), f32),
+            sds((cls_count, 1), f32),
+            sds((n_piece, cls_count, img_rows), f32),
+            sds((n_piece, img_rows), f32),
+        ),
+        in_specs=[VM] * (1 + len(others) + n_piece),
+        out_specs=(VM, VM, VM, VM),
+        compiler_params=params(24),
+        name="score",
+    )(local_sum, *others, *image_list)
+
+    total = tot
+    for m in range(1, n_img):
+        moved = swap(tot, "img", m)
+        total = total + jnp.stack([moved[where[t, i ^ m]] for t, i in order])
+    totals = [total] + [swap(total, "cls", m) for m in range(1, n_cls)]
+
+    first_id = ((lax.axis_index("cls") * n_img + me) * cls_count).astype(jnp.int32).reshape(1)
+    gz = pl.pallas_call(
+        functools.partial(grad_kernel, tpl_total, tpl_count, n_piece, len(totals)),
+        out_shape=sds((flat_rows, feat), bf16),
+        in_specs=[SM] + [VM] * (len(totals) + n_piece + 6),
+        out_specs=VM,
+        compiler_params=params(24),
+        name="grad",
+    )(first_id, *totals, *image_list, e, label_arr, class_w, mean_rn, u, rz)
+
+    tpl_t = flat_tpl.T.reshape(n_img, feat // n_img, flat_rows)
+    cols = [
+        lax.dynamic_index_in_dim(tpl_t, me ^ m, 0, keepdims=False) for m in range(n_img)
+    ]
+    cols = [cols[0]] + [swap(cols[m], "img", m) for m in range(1, n_img)]
+    grads = {0: gz}
+    for m in far:
+        grads[m] = swap(gz, "img", m)
+    for m in (0, *far):
+        grads[m ^ 1] = swap(grads[m], "img", 1)
+    blocks = pl.pallas_call(
+        functools.partial(outer_kernel, n_img, n_cls),
+        out_shape=sds((n_cls, feat // n_img, feat // n_cls), bf16),
+        in_specs=[VM] * (2 * n_img),
+        out_specs=VM,
+        compiler_params=params(24),
+        name="outer",
+    )(*cols, *[grads[m] for m in range(n_img)])
+
+    grad_tpl = pl.pallas_call(
+        functools.partial(back_kernel, n_img),
+        out_shape=sds((flat_rows, feat), bf16),
+        in_specs=[SM, VM] + [HB] * n_img,
+        out_specs=VM,
+        scratch_shapes=[
+            pltpu.VMEM((n_img, proj_rows, feat), bf16),
+            pltpu.SemaphoreType.DMA((n_img,)),
+        ],
+        compiler_params=params(24),
+        cost_estimate=pl.CostEstimate(
+            flops=2 * flat_rows * feat * feat,
+            bytes_accessed=2 * feat * feat + 4 * flat_rows * feat,
+            transcendentals=0,
+        ),
+        name="back",
+    )(me_arr, gz, *proj_list)
+
+    mine = lax.axis_index("cls")
+    block = lax.dynamic_index_in_dim(blocks, mine, 0, keepdims=False).astype(f32)
+    for m in range(1, n_cls):
+        block = block + swap(
+            lax.dynamic_index_in_dim(blocks, mine ^ m, 0, keepdims=False), "cls", m
+        ).astype(f32)
+    partial = block.astype(bf16)
+    result = partial.astype(f32)
+    for t in range(1, n_tpl):
+        result = result + swap(partial, "tpl", t).astype(f32)
+    return grad_tpl.reshape(tpl_count, cls_count, feat), result
+
+
 def solution(mesh):
+    shape = mesh.shape
     in_specs = (
         P(("img", "tpl"), None),
         P(("img", "tpl")),
@@ -82,4 +344,13 @@
         P("img", "cls"),
     )
     out_specs = (P("tpl", ("cls", "img"), None), P("img", "cls"))
-    return jax.shard_map(body, mesh=mesh, in_specs=in_specs, out_specs=out_specs, check_vma=False)
+
+    def step(images, labels, templates, projection):
+        powers = all(shape[a] & (shape[a] - 1) == 0 for a in ("img", "cls", "tpl"))
+        small = images.size * images.dtype.itemsize <= 8 * MIB
+        chosen = body if powers and shape["img"] > 1 and small else general_body
+        return jax.shard_map(
+            chosen, mesh=mesh, in_specs=in_specs, out_specs=out_specs, check_vma=False
+        )(images, labels, templates, projection)
+
+    return step

time: 262 us -> 176 us (0.67); the launches traced: 261 us -> 172 us
  waiting for transfers between devices: 158 us -> 80.8 us
  blocking collectives: 60.5 us -> 22 us
  starting transfers between devices: 0.29 us -> 28.4 us
  Pallas kernels: 0 us -> 15.8 us
  between operations: 14.3 us -> 0.82 us
  local copies, waits for them, and re-layouts: 7.09 us -> 19.7 us
  matrix products: 11.6 us -> 0 us
  other arithmetic: 8.86 us -> 4.76 us
    ppermute x0 -> x34, waiting for transfers between devices: none -> 80.8 us  [swap(): return lax.ppermute(x, axis, [(i, i ^ mask) for i in range(n)])]
    psum x3 -> x0, waiting for transfers between devices: 69.7 us -> none  [the longest x1 26.4 us: body(): class_g = lax.psum(spread, 'tpl')]
    all_gather x2 -> x0, waiting for transfers between devices: 39.8 us -> none  [the longest x1 29 us: body(): full_proj = lax.all_gather(wide_proj, 'img', axis=0, tiled=True)]
    ppermute x0 -> x34, starting transfers between devices: none -> 28.4 us  [swap(): return lax.ppermute(x, axis, [(i, i ^ mask) for i in range(n)])]
    unnamed x8 -> x0, waiting for transfers between devices: 25.6 us -> none
    reduce_scatter x1 -> x0, waiting for transfers between devices: 23.3 us -> none  [body(): lax.psum_scatter(logit_scale * jnp.dot(grad_logit, img_b, preferred_eleme...]
    all_to_all x1 -> x0, blocking collectives: 17.5 us -> none  [body(): lax.all_to_all(flat_tpl, 'img', split_axis=1, concat_axis=0, tiled=True)]
    pallas_call x0 -> x5, Pallas kernels: none -> 15.8 us  [the longest x1 3.84 us: body(): pl.pallas_call(functools.partial(score_kernel, tpl_total, n_piece, len(ot...]
  transfers between devices with their start and end apart: 7 -> 34, of which waited for: 7 -> 17; matrix products, arithmetic and copies ran while one was open for 2% -> 3% of each run, Pallas kernels for 0% -> 4%
where the time goes in v1:
time: 176 us; the launch traced here: 172 us
  waiting for transfers between devices  80.8 us (46%)
  starting transfers between devices  28.4 us (16%)
  blocking collectives  22 us (12%)
  local copies, waits for them, and re-layouts  19.7 us (11%)
  Pallas kernels  15.8 us (9%)
  other arithmetic  4.76 us (3%)
    ppermute x34, waiting for transfers between devices, swap(): return lax.ppermute(x, axis, [(i, i ^ mask) for i in range(n)])  80.8 us
    ppermute x34, starting transfers between devices, swap(): return lax.ppermute(x, axis, [(i, i ^ mask) for i in range(n)])  28.4 us
    all_gather x1, blocking collectives, body(): wide = lax.all_gather(projection, 'cls', axis=1, tiled=True)  22 us
    unnamed x37, local copies, waits for them, and re-layouts  13.8 us
    pallas_call x1, Pallas kernels, body(): pl.pallas_call(functools.partial(score_kernel, tpl_total, n_piece, len(ot...  3.84 us
  transfers between devices with their start and end apart: 34, of which 17 were waited for; matrix products, arithmetic and copies ran while one was open for 3% of the time, Pallas kernels for 4%

profile of v1, /device:TPU:0, one launch (start us, length us, event | category | flops | bytes accessed | tf_op | source)
XLA Modules:
  0.0 172.2 jit_solution(3795901246919613946)
XLA Ops:
  3.3 3.0 %collective-permute-start.5 = (bf16[256,1280]{1,0:T(8,128)(2,1)S(1)}, bf16[256,1280]{1,0:T(8,128)(2,1)S(1)}, u32[]{:S(2)}, u32[]{:S(2)}) collective-permute-start(bf16[256,1280]{1,0:T(8,128)(2,1)S(1)} %fusion.1.rest_1_.rest_4_), channel_id=1, source_target_pairs={{0,16},{8,24},{16,0},{24,8},{1,17},{9,25},{17,1},{25,9},{2,18},{10... | collective-permute-start | bytes 1966088 | tf_op jit(solution)/shard_map/ppermute | solution.py:91
  6.5 22.0 %all_gather.3 = bf16[320,1280]{0,1:T(8,128)(2,1)S(1)} all-gather(bf16[320,320]{0,1:T(8,128)(2,1)S(1)} %copy.11), channel_id=1, replica_groups=mesh['img'=4,'cls'=4,'tpl'=2] {'cls'}, dimensions={1}, use_global_device_ids=true | all-gather | bytes 1024000 | tf_op jit(solution)/shard_map/all_gather | solution.py:229
  29.7 1.5 collective-permute-start.7
  31.7 14.1 %collective-permute-done.1.rest_2_ = bf16[320,1280]{1,0:T(8,128)(2,1)S(1)} collective-permute-done((bf16[320,1280]{1,0:T(8,128)(2,1)S(1)}, bf16[320,1280]{1,0:T(8,128)(2,1)S(1)}, u32[]{:S(2)}, u32[]{:S(2)}) %collective-permute-start.1) | collective-permute-done | bytes 819232 | tf_op jit(solution)/shard_map/ppermute | solution.py:91
  48.8 12.2 %collective-permute-done.9.rest_7_.rest_10_ = bf16[256,1280]{1,0:T(8,128)(2,1)} collective-permute-done((bf16[256,1280]{1,0:T(8,128)(2,1)S(1)}, bf16[256,1280]{1,0:T(8,128)(2,1)}, u32[]{:S(2)}, u32[]{:S(2)}) %collective-permute-start.9) | collective-permute-done | bytes 655392 | tf_op jit(solution)/shard_map/ppermute | solution.py:91
  63.2 2.7 %text.1 = (f32[256,1280]{1,0:T(8,128)S(1)}, f32[256,1]{1,0:T(8,128)S(1)}, f32[64,1280]{1,0:T(8,128)S(1)}, bf16[64,1280]{1,0:T(8,128)(2,1)S(1)}) custom-call(s32[1]{0:T(128)} %bitcast.me_ref, bf16[256,1280]{1,0:T(8,128)(2,1)S(1)} %bitcast.33, bf16[320,1280]{1,0:T(8,128)(2,1)S(1)} %copy.14.rest_0_, bf16[320,1280]{1,0:T(8,128)(2,1)S(1)} %copy-done.1, ...), custom_call_target="tpu_custom_call" | custom-call | tf_op jit(solution)/shard_map/text/pallas_call | solution.py:239
  67.0 1.5 collective-permute-start.3
  68.6 5.1 %collective-permute-done.3.rest_0_ = bf16[64,1280]{1,0:T(8,128)(2,1)S(1)} collective-permute-done((bf16[64,1280]{1,0:T(8,128)(2,1)S(1)}, bf16[64,1280]{1,0:T(8,128)(2,1)S(1)}, u32[]{:S(2)}, u32[]{:S(2)}) %collective-permute-start.3) | collective-permute-done | bytes 163872 | tf_op jit(solution)/shard_map/ppermute | solution.py:91
  73.7 3.8 %score.1 = (f32[64,1280]{1,0:T(8,128)S(1)}, f32[64,1]{1,0:T(8,128)S(1)}, f32[8,64,256]{2,1,0:T(8,128)S(1)}, f32[8,256]{1,0:T(8,128)S(1)}) custom-call(f32[64,1280]{1,0:T(8,128)S(1)} %get-tuple-element.10.sum_ref, bf16[64,1280]{1,0:T(8,128)(2,1)S(1)} %collective-permute-done.3.rest_0_, bf16[256,1280]{1,0:T(8,128)(2,1)S(1)} %fusion.1.rest_1_.rest_4_, ...), custom_call_target="tpu_custom_call" | custom-call | tf_op jit(solution)/shard_map/score/pallas_call | solution.py:258
  79.2 1.6 collective-permute-start.13
  82.3 2.1 %collective-permute-done.12 = f32[8,256]{1,0:T(8,128)S(1)} collective-permute-done((f32[8,256]{1,0:T(8,128)S(1)}, f32[8,256]{1,0:T(8,128)S(1)}, u32[]{:S(2)}, u32[]{:S(2)}) %collective-permute-start.12) | collective-permute-done | bytes 8224 | tf_op jit(solution)/shard_map/ppermute | solution.py:91
  84.5 2.5 %collective-permute-start.15 = (f32[8,256]{1,0:T(8,128)S(1)}, f32[8,256]{1,0:T(8,128)S(1)}, u32[]{:S(2)}, u32[]{:S(2)}) collective-permute-start(f32[8,256]{1,0:T(8,128)S(1)} %fusion.5.rest_0_), channel_id=1, source_target_pairs={{0,4},{2,6},{4,0},{6,2},{1,5},{3,7},{5,1},{7,3},{8,12},{10,14},{12... | collective-permute-start | bytes 24584 | tf_op jit(solution)/shard_map/ppermute | solution.py:91
  87.1 1.8 %collective-permute-start.16 = (f32[8,256]{1,0:T(8,128)S(1)}, f32[8,256]{1,0:T(8,128)S(1)}, u32[]{:S(2)}, u32[]{:S(2)}) collective-permute-start(f32[8,256]{1,0:T(8,128)S(1)} %fusion.5.rest_0_), channel_id=1, source_target_pairs={{0,6},{2,4},{4,2},{6,0},{1,7},{3,5},{5,3},{7,1},{8,14},{10,12},{12... | collective-permute-start | bytes 24584 | tf_op jit(solution)/shard_map/ppermute | solution.py:91
  89.4 1.5 collective-permute-start.20
  91.0 1.5 collective-permute-done.18
  93.0 1.5 collective-permute-start.22
  94.5 2.0 %collective-permute-done.22 = s32[256]{0:T(256)S(1)} collective-permute-done((s32[256]{0:T(256)S(1)}, s32[256]{0:T(256)S(1)}, u32[]{:S(2)}, u32[]{:S(2)}) %collective-permute-start.22) | collective-permute-done | bytes 1056 | tf_op jit(solution)/shard_map/ppermute | solution.py:91
  101.4 3.5 %grad.1.gz_ref.rest_4_ = bf16[256,1280]{1,0:T(8,128)(2,1)S(1)} custom-call(s32[1]{0:T(128)} %bitcast.1.first_ref, f32[8,256]{1,0:T(8,128)S(1)} %fusion.5.rest_0_, f32[8,256]{1,0:T(8,128)S(1)} %collective-permute-done.14.rest_1_, f32[8,256]{1,0:T(8,128)S(1)} %collective-permute-done.15.rest_2_, f32[8,256]{1,0:T(8,128)S(1)} %collective-permute-done.16.rest_3_, ...), custom_call_target="tpu_custom_call" | custom-call | tf_op jit(solution)/shard_map/grad/pallas_call | solution.py:279
  104.9 1.6 collective-permute-start.28
  106.6 15.4 %collective-permute-done.28.rest_6_ = bf16[256,1280]{1,0:T(8,128)(2,1)S(1)} collective-permute-done((bf16[256,1280]{1,0:T(8,128)(2,1)S(1)}, bf16[256,1280]{1,0:T(8,128)(2,1)S(1)}, u32[]{:S(2)}, u32[]{:S(2)}) %collective-permute-start.28) | collective-permute-done | bytes 655392 | tf_op jit(solution)/shard_map/ppermute | solution.py:91
  122.0 2.4 %copy.16 = bf16[1280,256]{1,0:T(8,128)(2,1)} copy(bf16[1280,256]{0,1:T(8,128)(2,1)} %bitcast.32) | data formatting | bytes 1310720 | tf_op jit(solution)/shard_map/transpose | solution.py:288
  124.4 1.9 %dynamic-slice_bitcast_fusion.3 = (bf16[320,256]{1,0:T(8,128)(2,1)}, bf16[320,256]{1,0:T(8,128)(2,1)}, bf16[320,256]{1,0:T(8,128)(2,1)}, bf16[320,256]{1,0:T(8,128)(2,1)S(1)}) fusion(bf16[4,320,256]{2,1,0:T(8,128)(2,1)} %bitcast.34, s32[]{:T(128)S(6)} %select_n.29, s32[]{:T(128)S(6)} %select_n.28, s32[]{:T(128)S(6)} %select_n.27, s32[]{:T(128)S(6)} %select_n.26), kind=kLoop, calls=%fused_computation.12 | loop fusion | bytes 1310736 | tf_op jit(solution)/shard_map/jit(dynamic_index_in_dim)/squeeze | solution.py:290
  126.6 1.5 collective-permute-start.25
  128.9 5.0 %collective-permute-done.25.rest_2_ = bf16[320,256]{1,0:T(8,128)(2,1)S(1)} collective-permute-done((bf16[320,256]{1,0:T(8,128)(2,1)}, bf16[320,256]{1,0:T(8,128)(2,1)S(1)}, u32[]{:S(2)}, u32[]{:S(2)}) %collective-permute-start.25) | collective-permute-done | bytes 163872 | tf_op jit(solution)/shard_map/ppermute | solution.py:91
  139.0 2.4 %outer.1 = bf16[4,320,320]{2,1,0:T(8,128)(2,1)S(1)} custom-call(bf16[320,256]{1,0:T(8,128)(2,1)S(1)} %get-tuple-element.24.rest_0_, bf16[320,256]{1,0:T(8,128)(2,1)S(1)} %copy-done.13, bf16[320,256]{1,0:T(8,128)(2,1)S(1)} %copy-done.15, bf16[320,256]{1,0:T(8,128)(2,1)} %collective-permute-done.26.rest_3_, bf16[256,1280]{1,0:T(8,128)(2,1)S(1)} %grad.1.gz_ref.rest_4_, ...), custom_call_target="tpu_custom_call" | custom-call | tf_op jit(solution)/shard_map/outer/pallas_call | solution.py:298
  142.3 2.5 %collective-permute-start.31 = (bf16[320,320]{1,0:T(8,128)(2,1)}, bf16[320,320]{1,0:T(8,128)(2,1)}, u32[]{:S(2)}, u32[]{:S(2)}) collective-permute-start(bf16[320,320]{1,0:T(8,128)(2,1)} %get-tuple-element.20), channel_id=1, source_target_pairs={{0,4},{2,6},{4,0},{6,2},{1,5},{3,7},{5,1},{7,3},{8,12},{10,14},{12... | collective-permute-start | bytes 614408 | tf_op jit(solution)/shard_map/ppermute | solution.py:91
  144.8 1.8 %collective-permute-start.32 = (bf16[320,320]{1,0:T(8,128)(2,1)S(1)}, bf16[320,320]{1,0:T(8,128)(2,1)}, u32[]{:S(2)}, u32[]{:S(2)}) collective-permute-start(bf16[320,320]{1,0:T(8,128)(2,1)S(1)} %get-tuple-element.19), channel_id=1, source_target_pairs={{0,6},{2,4},{4,2},{6,0},{1,7},{3,5},{5,3},{7,1},{8,14},{10,12},{12... | collective-permute-start | bytes 614408 | tf_op jit(solution)/shard_map/ppermute | solution.py:91
  146.7 9.0 %collective-permute-done.30 = bf16[320,320]{1,0:T(8,128)(2,1)} collective-permute-done((bf16[320,320]{1,0:T(8,128)(2,1)}, bf16[320,320]{1,0:T(8,128)(2,1)}, u32[]{:S(2)}, u32[]{:S(2)}) %collective-permute-start.30) | collective-permute-done | bytes 204832 | tf_op jit(solution)/shard_map/ppermute | solution.py:91
  155.7 7.2 %collective-permute-done.31 = bf16[320,320]{1,0:T(8,128)(2,1)} collective-permute-done((bf16[320,320]{1,0:T(8,128)(2,1)}, bf16[320,320]{1,0:T(8,128)(2,1)}, u32[]{:S(2)}, u32[]{:S(2)}) %collective-permute-start.31) | collective-permute-done | bytes 204832 | tf_op jit(solution)/shard_map/ppermute | solution.py:91
  164.2 1.6 collective-permute-start.33
  165.8 3.4 %back.1 = bf16[256,1280]{1,0:T(8,128)(2,1)} custom-call(s32[1]{0:T(128)} %bitcast.me_ref, bf16[256,1280]{1,0:T(8,128)(2,1)S(1)} %grad.1.gz_ref.rest_4_, bf16[320,1280]{1,0:T(8,128)(2,1)S(1)} %copy.14.rest_0_, bf16[320,1280]{1,0:T(8,128)(2,1)S(1)} %copy-done.2, bf16[320,1280]{1,0:T(8,128)(2,1)S(1)} %collective-permute-done.1.rest_2_, ...), custom_call_target="tpu_custom_call" | custom-call | flops 838860800 | bytes 4587520 | tf_op jit(solution)/shard_map/back/pallas_call | solution.py:307
  169.2 2.3 %collective-permute-done.33 = bf16[320,320]{1,0:T(8,128)(2,1)S(1)} collective-permute-done((bf16[320,320]{1,0:T(8,128)(2,1)S(1)}, bf16[320,320]{1,0:T(8,128)(2,1)S(1)}, u32[]{:S(2)}, u32[]{:S(2)}) %collective-permute-start.33) | collective-permute-done | bytes 204832 | tf_op jit(solution)/shard_map/ppermute | solution.py:91
  (95 shorter events, 29.2 us)
Async XLA Ops:
  3.3 28.0 %collective-permute-start.5 = (bf16[256,1280]{1,0:T(8,128)(2,1)S(1)}, bf16[256,1280]{1,0:T(8,128)(2,1)S(1)}, u32[]{:S(2)}, u32[]{:S(2)}) collective-permute-start(bf16[256,1280]{1,0:T(8,128)(2,1)S(1)} %fusion.1.rest_1_.rest_4_), channel_id=1, source_target_pairs={{0,16},{8,24},{16,0},{24,8},{1,17},{9,25},{17,1},{25,9},{2,18},{10... | collective-permute-start | bytes 1966088 | tf_op jit(solution)/shard_map/ppermute | solution.py:91
  29.1 16.8 %collective-permute-start.1 = (bf16[320,1280]{1,0:T(8,128)(2,1)S(1)}, bf16[320,1280]{1,0:T(8,128)(2,1)S(1)}, u32[]{:S(2)}, u32[]{:S(2)}) collective-permute-start(bf16[320,1280]{1,0:T(8,128)(2,1)S(1)} %copy.14.rest_0_), channel_id=1, source_target_pairs={{0,16},{8,24},{16,0},{24,8},{1,17},{9,25},{17,1},{25,9},{2,18},{10... | collective-permute-start | bytes 2457608 | tf_op jit(solution)/shard_map/ppermute | solution.py:91
  29.7 17.7 %collective-permute-start = (bf16[320,1280]{1,0:T(8,128)(2,1)S(1)}, bf16[320,1280]{1,0:T(8,128)(2,1)S(1)}, u32[]{:S(2)}, u32[]{:S(2)}) collective-permute-start(bf16[320,1280]{1,0:T(8,128)(2,1)S(1)} %copy.14.rest_0_), channel_id=1, source_target_pairs={{0,8},{8,0},{16,24},{24,16},{1,9},{9,1},{17,25},{25,17},{2,10},{10... | collective-permute-start | bytes 2457608 | tf_op jit(solution)/shard_map/ppermute | solution.py:91
  29.7 17.7 %collective-permute-start.7 = (bf16[256,1280]{1,0:T(8,128)(2,1)S(1)}, bf16[256,1280]{1,0:T(8,128)(2,1)}, u32[]{:S(2)}, u32[]{:S(2)}) collective-permute-start(bf16[256,1280]{1,0:T(8,128)(2,1)S(1)} %fusion.1.rest_1_.rest_4_), channel_id=1, source_target_pairs={{0,1},{1,0},{2,3},{3,2},{4,5},{5,4},{6,7},{7,6},{8,9},{9,8},{10,11... | collective-permute-start | bytes 1966088 | tf_op jit(solution)/shard_map/ppermute | solution.py:91
  31.2 29.8 %collective-permute-start.9 = (bf16[256,1280]{1,0:T(8,128)(2,1)S(1)}, bf16[256,1280]{1,0:T(8,128)(2,1)}, u32[]{:S(2)}, u32[]{:S(2)}) collective-permute-start(bf16[256,1280]{1,0:T(8,128)(2,1)S(1)} %collective-permute-done.5.rest_3_.rest_6_), channel_id=1, source_target_pairs={{0,1},{1,0},{2,3},{3,2},{4,5},{5,4},{6,7},{7,6},{8,9},{9,8},{10,11... | collective-permute-start | bytes 1966088 | tf_op jit(solution)/shard_map/ppermute | solution.py:91
  45.8 15.2 %collective-permute-start.2 = (bf16[320,1280]{1,0:T(8,128)(2,1)S(1)}, bf16[320,1280]{1,0:T(8,128)(2,1)}, u32[]{:S(2)}, u32[]{:S(2)}) collective-permute-start(bf16[320,1280]{1,0:T(8,128)(2,1)S(1)} %collective-permute-done.1.rest_2_), channel_id=1, source_target_pairs={{0,8},{8,0},{16,24},{24,16},{1,9},{9,1},{17,25},{25,17},{2,10},{10... | collective-permute-start | bytes 2457608 | tf_op jit(solution)/shard_map/ppermute | solution.py:91
  45.8 22.7 %collective-permute-start.4 = (bf16[256,1280]{1,0:T(8,128)(2,1)S(1)}, bf16[256,1280]{1,0:T(8,128)(2,1)}, u32[]{:S(2)}, u32[]{:S(2)}) collective-permute-start(bf16[256,1280]{1,0:T(8,128)(2,1)S(1)} %fusion.1.rest_1_.rest_4_), channel_id=1, source_target_pairs={{0,8},{8,0},{16,24},{24,16},{1,9},{9,1},{17,25},{25,17},{2,10},{10... | collective-permute-start | bytes 1966088 | tf_op jit(solution)/shard_map/ppermute | solution.py:91
  47.4 21.2 %collective-permute-start.6 = (bf16[256,1280]{1,0:T(8,128)(2,1)S(1)}, bf16[256,1280]{1,0:T(8,128)(2,1)}, u32[]{:S(2)}, u32[]{:S(2)}) collective-permute-start(bf16[256,1280]{1,0:T(8,128)(2,1)S(1)} %collective-permute-done.5.rest_3_.rest_6_), channel_id=1, source_target_pairs={{0,8},{8,0},{16,24},{24,16},{1,9},{9,1},{17,25},{25,17},{2,10},{10... | collective-permute-start | bytes 1966088 | tf_op jit(solution)/shard_map/ppermute | solution.py:91
  48.3 20.2 %collective-permute-start.8 = (bf16[256,1280]{1,0:T(8,128)(2,1)}, bf16[256,1280]{1,0:T(8,128)(2,1)}, u32[]{:S(2)}, u32[]{:S(2)}) collective-permute-start(bf16[256,1280]{1,0:T(8,128)(2,1)} %collective-permute-done.7.rest_5_.rest_8_), channel_id=1, source_target_pairs={{0,8},{8,0},{16,24},{24,16},{1,9},{9,1},{17,25},{25,17},{2,10},{10... | collective-permute-start | bytes 1966088 | tf_op jit(solution)/shard_map/ppermute | solution.py:91
  61.0 12.7 %collective-permute-start.10 = (bf16[256,1280]{1,0:T(8,128)(2,1)}, bf16[256,1280]{1,0:T(8,128)(2,1)}, u32[]{:S(2)}, u32[]{:S(2)}) collective-permute-start(bf16[256,1280]{1,0:T(8,128)(2,1)} %collective-permute-done.9.rest_7_.rest_10_), channel_id=1, source_target_pairs={{0,8},{8,0},{16,24},{24,16},{1,9},{9,1},{17,25},{25,17},{2,10},{10... | collective-permute-start | bytes 1966088 | tf_op jit(solution)/shard_map/ppermute | solution.py:91
  67.0 6.6 %collective-permute-start.3 = (bf16[64,1280]{1,0:T(8,128)(2,1)S(1)}, bf16[64,1280]{1,0:T(8,128)(2,1)S(1)}, u32[]{:S(2)}, u32[]{:S(2)}) collective-permute-start(bf16[64,1280]{1,0:T(8,128)(2,1)S(1)} %get-tuple-element.11), channel_id=1, source_target_pairs={{0,1},{1,0},{2,3},{3,2},{4,5},{5,4},{6,7},{7,6},{8,9},{9,8},{10,11... | collective-permute-start | bytes 491528 | tf_op jit(solution)/shard_map/ppermute | solution.py:91
  79.2 2.1 %collective-permute-start.11 = (f32[8,256]{1,0:T(8,128)S(1)}, f32[8,256]{1,0:T(8,128)S(1)}, u32[]{:S(2)}, u32[]{:S(2)}) collective-permute-start(f32[8,256]{1,0:T(8,128)S(1)} %get-tuple-element.12), channel_id=1, source_target_pairs={{0,8},{8,0},{16,24},{24,16},{1,9},{9,1},{17,25},{25,17},{2,10},{10... | collective-permute-start | bytes 24584 | tf_op jit(solution)/shard_map/ppermute | solution.py:91
  79.2 3.1 %collective-permute-start.13 = (f32[8,256]{1,0:T(8,128)S(1)}, f32[8,256]{1,0:T(8,128)S(1)}, u32[]{:S(2)}, u32[]{:S(2)}) collective-permute-start(f32[8,256]{1,0:T(8,128)S(1)} %get-tuple-element.12), channel_id=1, source_target_pairs={{0,24},{8,16},{16,8},{24,0},{1,25},{9,17},{17,9},{25,1},{2,26},{10... | collective-permute-start | bytes 24584 | tf_op jit(solution)/shard_map/ppermute | solution.py:91
  80.8 3.7 %collective-permute-start.12 = (f32[8,256]{1,0:T(8,128)S(1)}, f32[8,256]{1,0:T(8,128)S(1)}, u32[]{:S(2)}, u32[]{:S(2)}) collective-permute-start(f32[8,256]{1,0:T(8,128)S(1)} %get-tuple-element.12), channel_id=1, source_target_pairs={{0,16},{8,24},{16,0},{24,8},{1,17},{9,25},{17,1},{25,9},{2,18},{10... | collective-permute-start | bytes 24584 | tf_op jit(solution)/shard_map/ppermute | solution.py:91
  84.4 13.5 %collective-permute-start.14 = (f32[8,256]{1,0:T(8,128)S(1)}, f32[8,256]{1,0:T(8,128)S(1)}, u32[]{:S(2)}, u32[]{:S(2)}) collective-permute-start(f32[8,256]{1,0:T(8,128)S(1)} %fusion.5.rest_0_), channel_id=1, source_target_pairs={{0,2},{2,0},{4,6},{6,4},{1,3},{3,1},{5,7},{7,5},{8,10},{10,8},{12,... | collective-permute-start | bytes 24584 | tf_op jit(solution)/shard_map/ppermute | solution.py:91
  84.5 13.4 %collective-permute-start.15 = (f32[8,256]{1,0:T(8,128)S(1)}, f32[8,256]{1,0:T(8,128)S(1)}, u32[]{:S(2)}, u32[]{:S(2)}) collective-permute-start(f32[8,256]{1,0:T(8,128)S(1)} %fusion.5.rest_0_), channel_id=1, source_target_pairs={{0,4},{2,6},{4,0},{6,2},{1,5},{3,7},{5,1},{7,3},{8,12},{10,14},{12... | collective-permute-start | bytes 24584 | tf_op jit(solution)/shard_map/ppermute | solution.py:91
  87.1 10.9 %collective-permute-start.16 = (f32[8,256]{1,0:T(8,128)S(1)}, f32[8,256]{1,0:T(8,128)S(1)}, u32[]{:S(2)}, u32[]{:S(2)}) collective-permute-start(f32[8,256]{1,0:T(8,128)S(1)} %fusion.5.rest_0_), channel_id=1, source_target_pairs={{0,6},{2,4},{4,2},{6,0},{1,7},{3,5},{5,3},{7,1},{8,14},{10,12},{12... | collective-permute-start | bytes 24584 | tf_op jit(solution)/shard_map/ppermute | solution.py:91
  88.9 3.6 %collective-permute-start.18 = (s32[256]{0:T(256)S(1)}, s32[256]{0:T(256)S(1)}, u32[]{:S(2)}, u32[]{:S(2)}) collective-permute-start(s32[256]{0:T(256)S(1)} %copy-done.17), channel_id=1, source_target_pairs={{0,16},{8,24},{16,0},{24,8},{1,17},{9,25},{17,1},{25,9},{2,18},{10... | collective-permute-start | bytes 3080 | tf_op jit(solution)/shard_map/ppermute | solution.py:91
  89.4 3.6 %collective-permute-start.20 = (s32[256]{0:T(256)S(1)}, s32[256]{0:T(256)S(1)}, u32[]{:S(2)}, u32[]{:S(2)}) collective-permute-start(s32[256]{0:T(256)S(1)} %copy-done.17), channel_id=1, source_target_pairs={{0,1},{1,0},{2,3},{3,2},{4,5},{5,4},{6,7},{7,6},{8,9},{9,8},{10,11... | collective-permute-start | bytes 3080 | tf_op jit(solution)/shard_map/ppermute | solution.py:91
  92.5 2.1 %collective-permute-start.17 = (s32[256]{0:T(256)S(1)}, s32[256]{0:T(256)S(1)}, u32[]{:S(2)}, u32[]{:S(2)}) collective-permute-start(s32[256]{0:T(256)S(1)} %copy-done.17), channel_id=1, source_target_pairs={{0,8},{8,0},{16,24},{24,16},{1,9},{9,1},{17,25},{25,17},{2,10},{10... | collective-permute-start | bytes 3080 | tf_op jit(solution)/shard_map/ppermute | solution.py:91
  93.0 3.6 %collective-permute-start.22 = (s32[256]{0:T(256)S(1)}, s32[256]{0:T(256)S(1)}, u32[]{:S(2)}, u32[]{:S(2)}) collective-permute-start(s32[256]{0:T(256)S(1)} %collective-permute-done.18), channel_id=1, source_target_pairs={{0,1},{1,0},{2,3},{3,2},{4,5},{5,4},{6,7},{7,6},{8,9},{9,8},{10,11... | collective-permute-start | bytes 3080 | tf_op jit(solution)/shard_map/ppermute | solution.py:91
  94.5 2.1 %collective-permute-start.19 = (s32[256]{0:T(256)S(1)}, s32[256]{0:T(256)S(1)}, u32[]{:S(2)}, u32[]{:S(2)}) collective-permute-start(s32[256]{0:T(256)S(1)} %collective-permute-done.18), channel_id=1, source_target_pairs={{0,8},{8,0},{16,24},{24,16},{1,9},{9,1},{17,25},{25,17},{2,10},{10... | collective-permute-start | bytes 3080 | tf_op jit(solution)/shard_map/ppermute | solution.py:91
  104.9 17.0 %collective-permute-start.28 = (bf16[256,1280]{1,0:T(8,128)(2,1)S(1)}, bf16[256,1280]{1,0:T(8,128)(2,1)S(1)}, u32[]{:S(2)}, u32[]{:S(2)}) collective-permute-start(bf16[256,1280]{1,0:T(8,128)(2,1)S(1)} %grad.1.gz_ref.rest_4_), channel_id=1, source_target_pairs={{0,16},{8,24},{16,0},{24,8},{1,17},{9,25},{17,1},{25,9},{2,18},{10... | collective-permute-start | bytes 1966088 | tf_op jit(solution)/shard_map/ppermute | solution.py:91
  106.5 29.5 %collective-permute-start.27 = (bf16[256,1280]{1,0:T(8,128)(2,1)S(1)}, bf16[256,1280]{1,0:T(8,128)(2,1)}, u32[]{:S(2)}, u32[]{:S(2)}) collective-permute-start(bf16[256,1280]{1,0:T(8,128)(2,1)S(1)} %grad.1.gz_ref.rest_4_), channel_id=1, source_target_pairs={{0,8},{8,0},{16,24},{24,16},{1,9},{9,1},{17,25},{25,17},{2,10},{10... | collective-permute-start | bytes 1966088 | tf_op jit(solution)/shard_map/ppermute | solution.py:91
  122.0 14.1 %collective-permute-start.29 = (bf16[256,1280]{1,0:T(8,128)(2,1)S(1)}, bf16[256,1280]{1,0:T(8,128)(2,1)}, u32[]{:S(2)}, u32[]{:S(2)}) collective-permute-start(bf16[256,1280]{1,0:T(8,128)(2,1)S(1)} %collective-permute-done.28.rest_6_), channel_id=1, source_target_pairs={{0,8},{8,0},{16,24},{24,16},{1,9},{9,1},{17,25},{25,17},{2,10},{10... | collective-permute-start | bytes 1966088 | tf_op jit(solution)/shard_map/ppermute | solution.py:91
  126.3 1.9 %collective-permute-start.24 = (bf16[320,256]{1,0:T(8,128)(2,1)}, bf16[320,256]{1,0:T(8,128)(2,1)S(1)}, u32[]{:S(2)}, u32[]{:S(2)}) collective-permute-start(bf16[320,256]{1,0:T(8,128)(2,1)} %get-tuple-element.23), channel_id=1, source_target_pairs={{0,8},{8,0},{16,24},{24,16},{1,9},{9,1},{17,25},{25,17},{2,10},{10... | collective-permute-start | bytes 491528 | tf_op jit(solution)/shard_map/ppermute | solution.py:91
  126.6 7.3 %collective-permute-start.25 = (bf16[320,256]{1,0:T(8,128)(2,1)}, bf16[320,256]{1,0:T(8,128)(2,1)S(1)}, u32[]{:S(2)}, u32[]{:S(2)}) collective-permute-start(bf16[320,256]{1,0:T(8,128)(2,1)} %get-tuple-element.22), channel_id=1, source_target_pairs={{0,16},{8,24},{16,0},{24,8},{1,17},{9,25},{17,1},{25,9},{2,18},{10... | collective-permute-start | bytes 491528 | tf_op jit(solution)/shard_map/ppermute | solution.py:91
  128.1 7.9 %collective-permute-start.26 = (bf16[320,256]{1,0:T(8,128)(2,1)}, bf16[320,256]{1,0:T(8,128)(2,1)}, u32[]{:S(2)}, u32[]{:S(2)}) collective-permute-start(bf16[320,256]{1,0:T(8,128)(2,1)} %get-tuple-element.21), channel_id=1, source_target_pairs={{0,24},{8,16},{16,8},{24,0},{1,25},{9,17},{17,9},{25,1},{2,26},{10... | collective-permute-start | bytes 491528 | tf_op jit(solution)/shard_map/ppermute | solution.py:91
  142.3 13.4 %collective-permute-start.30 = (bf16[320,320]{1,0:T(8,128)(2,1)}, bf16[320,320]{1,0:T(8,128)(2,1)}, u32[]{:S(2)}, u32[]{:S(2)}) collective-permute-start(bf16[320,320]{1,0:T(8,128)(2,1)} %get-tuple-element.18), channel_id=1, source_target_pairs={{0,2},{2,0},{4,6},{6,4},{1,3},{3,1},{5,7},{7,5},{8,10},{10,8},{12,... | collective-permute-start | bytes 614408 | tf_op jit(solution)/shard_map/ppermute | solution.py:91
  142.3 20.6 %collective-permute-start.31 = (bf16[320,320]{1,0:T(8,128)(2,1)}, bf16[320,320]{1,0:T(8,128)(2,1)}, u32[]{:S(2)}, u32[]{:S(2)}) collective-permute-start(bf16[320,320]{1,0:T(8,128)(2,1)} %get-tuple-element.20), channel_id=1, source_target_pairs={{0,4},{2,6},{4,0},{6,2},{1,5},{3,7},{5,1},{7,3},{8,12},{10,14},{12... | collective-permute-start | bytes 614408 | tf_op jit(solution)/shard_map/ppermute | solution.py:91
  144.8 18.1 %collective-permute-start.32 = (bf16[320,320]{1,0:T(8,128)(2,1)S(1)}, bf16[320,320]{1,0:T(8,128)(2,1)}, u32[]{:S(2)}, u32[]{:S(2)}) collective-permute-start(bf16[320,320]{1,0:T(8,128)(2,1)S(1)} %get-tuple-element.19), channel_id=1, source_target_pairs={{0,6},{2,4},{4,2},{6,0},{1,7},{3,5},{5,3},{7,1},{8,14},{10,12},{12... | collective-permute-start | bytes 614408 | tf_op jit(solution)/shard_map/ppermute | solution.py:91
  164.2 7.2 %collective-permute-start.33 = (bf16[320,320]{1,0:T(8,128)(2,1)S(1)}, bf16[320,320]{1,0:T(8,128)(2,1)S(1)}, u32[]{:S(2)}, u32[]{:S(2)}) collective-permute-start(bf16[320,320]{1,0:T(8,128)(2,1)S(1)} %fusion.4), channel_id=1, source_target_pairs={{0,1},{1,0},{2,3},{3,2},{4,5},{5,4},{6,7},{7,6},{8,9},{9,8},{10,11... | collective-permute-start | bytes 614408 | tf_op jit(solution)/shard_map/ppermute | solution.py:91
  (20 other events, 60.5 us)

commit v2 on v0

--- a/solution.py
+++ b/solution.py
@@ -1,17 +1,25 @@
+import functools
+
 import jax
 import jax.numpy as jnp
 from jax import lax
+from jax.experimental import pallas as pl
+from jax.experimental.pallas import tpu as pltpu
 from jax.sharding import PartitionSpec as P
+
 
 logit_scale = 50.0
 epsilon = 1e-06
+MIB = 1 << 20
+VM = pl.BlockSpec(memory_space=pltpu.VMEM)
+HB = pl.BlockSpec(memory_space=pltpu.HBM)
 
 
 def inverse_norm(values):
     return lax.rsqrt(jnp.sum(values * values, axis=-1, keepdims=True) + epsilon)
 
 
-def body(images, labels, templates, projection):
+def general_body(images, labels, templates, projection):
     tpl_count = templates.shape[0]
     cls_count = templates.shape[1]
     feat_width = templates.shape[2]
@@ -74,7 +82,506 @@
     return (grad_templates, grad_projection)
 
 
+def sds(shape, dtype):
+    return jax.ShapeDtypeStruct(shape, dtype)
+
+
+def swap(x, axis, mask):
+    n = lax.axis_size(axis)
+    return lax.ppermute(x, axis, [(i, i ^ mask) for i in range(n)])
+
+
+def params(mib):
+    return pltpu.CompilerParams(vmem_limit_bytes=int(mib * MIB))
+
+
+def start_all(pairs, sem):
+    copies = [pltpu.make_async_copy(s, d, sem.at[k]) for k, (s, d) in enumerate(pairs)]
+    for copy in copies:
+        copy.start()
+    return copies
+
+
+def place(axis):
+    return lax.axis_index(axis).astype(jnp.int32)
+
+
+def prep_kernel(img_ref, lab_ref, proj_ref, out_ref, part_ref, buf, sem):
+    share = part_ref.shape[0]
+    at = pl.multiple_of(place("tpl") * share, share)
+    copies = start_all([(img_ref, buf), (proj_ref.at[pl.ds(at, share)], part_ref)], sem)
+    rows = img_ref.shape[0]
+    lab = lab_ref[...]
+    pad = jnp.zeros((14, rows), jnp.int32)
+    digits = jnp.concatenate([lab // 128, lab % 128, pad], axis=0)
+    out_ref[rows:] = jnp.zeros((16, out_ref.shape[1]), jnp.bfloat16)
+    out_ref[rows:, :rows] = digits.astype(jnp.float32).astype(jnp.bfloat16)
+    copies[0].wait()
+    x = buf[...].astype(jnp.float32)
+    out_ref[:rows] = (x * inverse_norm(x)).astype(jnp.bfloat16)
+    copies[1].wait()
+
+
+def lift_kernel(tpl_ref, out_ref, sem):
+    for copy in start_all([(tpl_ref, out_ref)], sem):
+        copy.wait()
+
+
+def tick_kernel(lab_ref, out_ref):
+    out_ref[...] = lab_ref[:, :128]
+
+
+def tick(labels):
+    return pl.pallas_call(
+        tick_kernel,
+        out_shape=sds((1, 128), jnp.int32),
+        in_specs=[VM],
+        out_specs=VM,
+        compiler_params=params(1),
+    )(labels)
+
+
+def join_kernel(n_cls, *rest):
+    pieces = rest[:n_cls]
+    out_ref, buf, sem = rest[n_cls:]
+    copies = start_all([(p, buf.at[place("cls") ^ m]) for m, p in enumerate(pieces)], sem)
+    for copy in copies:
+        copy.wait()
+    width = buf.shape[2]
+    for j in range(n_cls):
+        out_ref[:, j * width : (j + 1) * width] = buf[j]
+
+
+def load_projection(places, piece_refs, full_ref, sem):
+    me, it = place("img"), place("tpl")
+    pairs = [
+        (piece, full_ref.at[me ^ m, it ^ t])
+        for piece, (m, t) in zip(piece_refs, places)
+    ]
+    for copy in start_all(pairs, sem):
+        copy.wait()
+
+
+def text_kernel(places, n_tpl, tpl_ref, *rest):
+    n = len(places)
+    full_ref, u_ref, rz_ref, sum_ref, send_ref, sem = rest[n:]
+    load_projection(places, rest[:n], full_ref, sem)
+    feat = tpl_ref.shape[1]
+    full = full_ref[...].reshape(feat, feat)
+    z = jnp.dot(tpl_ref[...], full, preferred_element_type=jnp.float32)
+    rz = inverse_norm(z)
+    u = z * rz
+    u_ref[...] = u
+    rz_ref[...] = rz
+    rows = u.shape[0] // n_tpl
+    total = u[:rows]
+    for t in range(1, n_tpl):
+        total = total + u[t * rows : (t + 1) * rows]
+    sum_ref[...] = total
+    send_ref[...] = total.astype(jnp.bfloat16)
+
+
+def score_kernel(tpl_total, n_piece, n_other, rows, sum_ref, *rest):
+    others = rest[:n_other]
+    images = rest[n_other : n_other + n_piece]
+    w_ref, rn_ref, e_ref, tot_ref = rest[n_other + n_piece :]
+    mean = sum_ref[...]
+    for other in others:
+        mean = mean + other[...].astype(jnp.float32)
+    mean = mean / tpl_total
+    rn = inverse_norm(mean)
+    w = mean * rn
+    w_ref[...] = w
+    rn_ref[...] = rn
+    wb = w.astype(jnp.bfloat16)
+    for k in range(n_piece):
+        scores = logit_scale * lax.dot_general(
+            wb, images[k][:rows], (((1,), (1,)), ((), ())), preferred_element_type=jnp.float32
+        )
+        e = jnp.exp(scores)
+        e_ref[k] = e
+        tot_ref[k : k + 1] = jnp.sum(e, axis=0, keepdims=True)
+
+
+def fold_totals_kernel(order, tot_ref, *rest):
+    others, out_ref = rest[:-1], rest[-1]
+    where = {key: k for k, key in enumerate(order)}
+    for k, (t, i) in enumerate(order):
+        row = tot_ref[k : k + 1]
+        for m, other in enumerate(others, 1):
+            j = where[t, i ^ m]
+            row = row + other[j : j + 1]
+        out_ref[k : k + 1] = row
+
+
+def grad_kernel(tpl_total, n_tpl, n_piece, n_tot, img_rows, n_cls, *rest):
+    tots = rest[:n_tot]
+    images = rest[n_tot : n_tot + n_piece]
+    e_ref, w_ref, rn_ref, u_ref, rz_ref = rest[n_tot + n_piece : n_tot + n_piece + 5]
+    outs = rest[n_tot + n_piece + 5 :]
+    gz_ref, turned = outs[0], outs[1 : 1 + n_cls]
+    flip = outs[1 + n_cls]
+    totals = tots[0][...]
+    for other in tots[1:]:
+        totals = totals + other[...]
+    inv = 1.0 / totals
+    rows, feat = w_ref.shape
+    acc = jnp.zeros((rows, feat), jnp.float32)
+    first = (place("cls") * lax.axis_size("img") + place("img")) * rows
+    ids = first + lax.broadcasted_iota(jnp.int32, (rows, img_rows), 0)
+    for k in range(n_piece):
+        digits = images[k][img_rows:, :img_rows].astype(jnp.float32)
+        lab = (digits[0:1] * 128.0 + digits[1:2]).astype(jnp.int32)
+        hot = (lab == ids).astype(jnp.float32)
+        gl = (e_ref[k] * inv[k : k + 1] - hot).astype(jnp.bfloat16)
+        acc = acc + jnp.dot(gl, images[k][:img_rows], preferred_element_type=jnp.float32)
+    g = logit_scale * acc
+    w = w_ref[...]
+    dot_wg = jnp.sum(w * g, axis=1, keepdims=True)
+    per_u = (g - w * dot_wg) * rn_ref[...] / tpl_total
+    inners = []
+    for t in range(n_tpl):
+        sl = slice(t * rows, (t + 1) * rows)
+        u = u_ref[sl]
+        inner = jnp.sum(u * per_u, axis=1, keepdims=True)
+        gz_ref[sl] = ((per_u - u * inner) * rz_ref[sl]).astype(jnp.bfloat16)
+        inners.append(inner)
+    line = digits_row(jnp.concatenate(inners, axis=0))
+    half = line.shape[1] // 2
+    for a in range(feat // 128):
+        sl = slice(a * 128, (a + 1) * 128)
+        flip[sl] = per_u[:, sl].T
+    width = feat // n_cls
+    for m, out in enumerate(turned):
+        at = (place("cls") ^ m) * width
+        top = flip[pl.ds(pl.multiple_of(at, 8), width // 2), :]
+        low = flip[pl.ds(pl.multiple_of(at + width // 2, 8), width // 2), :]
+        out[: width // 2] = jnp.concatenate([top, low], axis=1).astype(jnp.bfloat16)
+        out[width // 2 :] = jnp.concatenate(
+            [line[:2, :half], line[:2, half:], jnp.zeros((12, half), jnp.float32)], axis=0
+        ).astype(jnp.bfloat16)
+
+
+def digits_row(column):
+    wide = jnp.broadcast_to(column, (column.shape[0], 128)).T
+    high = wide[0:1].astype(jnp.bfloat16).astype(jnp.float32)
+    return jnp.concatenate([high, wide[0:1] - high], axis=0)
+
+
+def turn_kernel(n_cls, u_ref, rz_ref, *rest):
+    outs, flip = rest[:n_cls], rest[n_cls]
+    feat = u_ref.shape[1]
+    for a in range(feat // 128):
+        sl = slice(a * 128, (a + 1) * 128)
+        flip[sl] = u_ref[:, sl].T.astype(jnp.bfloat16)
+    line = digits_row(rz_ref[...])
+    line = jnp.concatenate([line, jnp.zeros((14, line.shape[1]), jnp.float32)], axis=0)
+    width = feat // n_cls
+    for m, out in enumerate(outs):
+        at = pl.multiple_of((place("cls") ^ m) * width, width)
+        out[:width] = flip[pl.ds(at, width), :]
+        out[width:] = line.astype(jnp.bfloat16)
+
+
+def turned_grad(unit_ref, late_ref):
+    rows = unit_ref.shape[0] - 16
+    unit = unit_ref[:rows].astype(jnp.float32)
+    rz = unit_ref[rows:].astype(jnp.float32)
+    late = late_ref[: rows // 2].astype(jnp.float32)
+    tail = late_ref[rows // 2 :].astype(jnp.float32)
+    span = late.shape[1] // 2
+    per_u = jnp.concatenate([late[:, :span], late[:, span:]], axis=0)
+    per_u = jnp.concatenate([per_u] * (unit.shape[1] // span), axis=1)
+    inner = jnp.concatenate([tail[0:1] + tail[1:2], tail[2:3] + tail[3:4]], axis=1)
+    return ((per_u - unit * inner) * (rz[0:1] + rz[1:2])).astype(jnp.bfloat16)
+
+
+def back_kernel(gz_ref, full_ref, *rest):
+    out_ref = rest[-1]
+    out_ref[...] = lax.dot_general(
+        gz_ref[...], full_ref[...], (((1,), (1,)), ((), ())), preferred_element_type=jnp.float32
+    ).astype(jnp.bfloat16)
+
+
+def outer_kernel(n_img, n_cls, held, *rest):
+    units, lates = rest[:n_cls], rest[n_cls : 2 * n_cls]
+    tpls = rest[2 * n_cls : -3]
+    grads = [turned_grad(a, b) for a, b in zip(units, lates)]
+    keep_ref, send_ref, acc_ref = rest[-3:]
+    first = jnp.dot(grads[0], tpls[0][...], preferred_element_type=jnp.float32)
+    plans = {}
+    for z in range(n_cls):
+        plans.setdefault(held(z), []).append(z)
+    for plan, spots in plans.items():
+        here = functools.reduce(jnp.logical_or, [place("cls") == z for z in spots])
+
+        @pl.when(here)
+        def _():
+            acc = first
+            for m in range(1, n_cls):
+                acc = acc + jnp.dot(
+                    grads[m], tpls[1 + plan[m - 1]][...], preferred_element_type=jnp.float32
+                )
+            acc_ref[...] = acc
+
+    width = acc_ref.shape[1] // n_img
+    for j in range(n_img):
+        k = place("img") ^ j
+        part = acc_ref[:, j * width : (j + 1) * width]
+
+        @pl.when(k % 2 == 0)
+        def _():
+            keep_ref[k // 2] = part
+
+        @pl.when(k % 2 == 1)
+        def _():
+            send_ref[k // 2] = part.astype(jnp.bfloat16)
+
+
+def final_kernel(own_ref, *rest):
+    total = own_ref[...]
+    for other in rest[:-1]:
+        total = total + other[...].astype(jnp.float32)
+    rest[-1][...] = total.T
+
+
+def fold_kernel(keep_ref, recv_ref, own_ref, *outs):
+    own = keep_ref[0] + recv_ref[0].astype(jnp.float32)
+    own_ref[...] = own
+    outs[0][...] = own.astype(jnp.bfloat16)
+    for k in range(1, len(outs)):
+        outs[k][...] = (keep_ref[k] + recv_ref[k].astype(jnp.float32)).astype(jnp.bfloat16)
+
+
+def both(x, tpl_mask, img_mask):
+    if img_mask == 0:
+        return swap(x, "tpl", tpl_mask)
+    if tpl_mask == 0:
+        return swap(x, "img", img_mask)
+    n_img, n_tpl = lax.axis_size("img"), lax.axis_size("tpl")
+    pairs = [
+        (i * n_tpl + t, (i ^ img_mask) * n_tpl + (t ^ tpl_mask))
+        for i in range(n_img)
+        for t in range(n_tpl)
+    ]
+    return lax.ppermute(x, ("img", "tpl"), pairs)
+
+
+def gather_line(x):
+    n = lax.axis_size("cls")
+    if n != 4:
+        return (lambda z: tuple(range(n - 1))), [swap(x, "cls", m) for m in range(1, n)]
+    one = swap(x, "cls", 1)
+    mid = lax.ppermute(x, "cls", [(1, 2), (2, 1)])
+    inner = lax.ppermute(one, "cls", [(1, 2), (2, 1)])
+    outer = lax.ppermute(mid, "cls", [(1, 0), (2, 3)])
+    last = lax.ppermute(inner, "cls", [(1, 0), (2, 3)])
+    return (lambda z: (0, 2, 1) if z in (1, 2) else (0, 3, 4)), [one, mid, inner, outer, last]
+
+
+def body(*args):
+    return fast_body(*args)
+
+
+def fast_body(images, labels, templates, projection):
+    tpl_count, cls_count, feat = templates.shape
+    n_tpl, n_img, n_cls = (lax.axis_size(a) for a in ("tpl", "img", "cls"))
+    tpl_total = tpl_count * n_tpl
+    flat_rows = tpl_count * cls_count
+    img_rows = images.shape[0]
+    proj_rows, proj_cols = projection.shape
+    f32, bf16 = jnp.float32, jnp.bfloat16
+    far = tuple(range(2, n_img, 2))
+    tpls = tuple(range(1, n_tpl))
+    label_row = labels.reshape(1, img_rows)
+    ticks = [tick(label_row) for _ in range(6)]
+
+    share = proj_rows // n_tpl
+    marked, part = pl.pallas_call(
+        prep_kernel,
+        out_shape=(sds((img_rows + 16, feat), bf16), sds((share, proj_cols), bf16)),
+        in_specs=[HB, VM, HB],
+        out_specs=(VM, VM),
+        scratch_shapes=[
+            pltpu.VMEM((img_rows, feat), bf16),
+            pltpu.SemaphoreType.DMA((2,)),
+        ],
+        compiler_params=params(8),
+        name="prep",
+    )(images, label_row, projection)
+    shards = [part] + [swap(part, "cls", m) for m in range(1, n_cls)]
+    images_at = {(0, 0): marked}
+    for m in far:
+        images_at[0, m] = swap(marked, "img", m)
+    for t in tpls:
+        images_at[t, 0] = swap(marked, "tpl", t)
+
+    wide = pl.pallas_call(
+        functools.partial(join_kernel, n_cls),
+        out_shape=sds((share, feat), bf16),
+        in_specs=[HB] * n_cls,
+        out_specs=VM,
+        scratch_shapes=[
+            pltpu.VMEM((n_cls, share, proj_cols), bf16),
+            pltpu.SemaphoreType.DMA((n_cls,)),
+        ],
+        compiler_params=params(4),
+        name="join",
+    )(*shards)
+    proj_at = {(0, 0): wide}
+    for m in far:
+        proj_at[m, 0] = swap(wide, "img", m)
+    for t in tpls:
+        proj_at[0, t] = swap(wide, "tpl", t)
+    for m in far:
+        for t in tpls:
+            proj_at[m, t] = swap(proj_at[m, 0], "tpl", t)
+    for (m, t), part in list(proj_at.items()):
+        proj_at[m ^ 1, t] = swap(part, "img", 1)
+    places = list(proj_at)
+    proj_list = list(proj_at.values())
+
+    for m in far:
+        for t in tpls:
+            images_at[t, m] = swap(images_at[t, 0], "img", m)
+    for (t, m), piece in list(images_at.items()):
+        images_at[t, m ^ 1] = swap(piece, "img", 1)
+    order = list(images_at)
+    n_piece = len(order)
+    image_list = list(images_at.values())
+
+    flat_tpl = templates.reshape(flat_rows, feat)
+    near_tpl = pl.pallas_call(
+        lift_kernel,
+        out_shape=sds((flat_rows, feat), bf16),
+        in_specs=[HB],
+        out_specs=VM,
+        scratch_shapes=[pltpu.SemaphoreType.DMA((1,))],
+        compiler_params=params(2),
+        name="lift",
+    )(flat_tpl)
+    full, u, rz, local_sum, send_sum = pl.pallas_call(
+        functools.partial(text_kernel, places, tpl_count),
+        out_shape=(
+            sds((n_img, n_tpl, share, feat), bf16),
+            sds((flat_rows, feat), f32),
+            sds((flat_rows, 1), f32),
+            sds((cls_count, feat), f32),
+            sds((cls_count, feat), bf16),
+        ),
+        in_specs=[VM] + [HB] * len(places),
+        out_specs=(VM, VM, VM, VM, VM),
+        scratch_shapes=[pltpu.SemaphoreType.DMA((len(places),))],
+        compiler_params=params(16),
+        name="text",
+    )(near_tpl, *proj_list)
+
+    held, tpl_list = gather_line(flat_tpl)
+    tpl_list = [near_tpl] + tpl_list
+
+    others = [swap(send_sum, "tpl", t) for t in tpls]
+    width = feat // n_cls
+    units = pl.pallas_call(
+        functools.partial(turn_kernel, n_cls),
+        out_shape=[sds((width + 16, flat_rows), bf16)] * n_cls,
+        in_specs=[VM, VM],
+        out_specs=[VM] * n_cls,
+        scratch_shapes=[pltpu.VMEM((feat, flat_rows), bf16)],
+        compiler_params=params(4),
+        name="turn",
+    )(u, rz)
+    units = [units[0]] + [swap(units[m], "cls", m) for m in range(1, n_cls)]
+
+    class_w, mean_rn, e, tot = pl.pallas_call(
+        functools.partial(score_kernel, tpl_total, n_piece, len(others), img_rows),
+        out_shape=(
+            sds((cls_count, feat), f32),
+            sds((cls_count, 1), f32),
+            sds((n_piece, cls_count, img_rows), f32),
+            sds((n_piece, img_rows), f32),
+        ),
+        in_specs=[VM] * (1 + len(others) + n_piece),
+        out_specs=(VM, VM, VM, VM),
+        compiler_params=params(16),
+        name="score",
+    )(local_sum, *others, *image_list)
+
+    total = pl.pallas_call(
+        functools.partial(fold_totals_kernel, order),
+        out_shape=sds((n_piece, img_rows), f32),
+        in_specs=[VM] * n_img,
+        out_specs=VM,
+        compiler_params=params(2),
+        name="fold_totals",
+    )(tot, *[swap(tot, "img", m) for m in range(1, n_img)])
+    totals = [total] + [swap(total, "cls", m) for m in range(1, n_cls)]
+
+    gz, *turned = pl.pallas_call(
+        functools.partial(
+            grad_kernel, tpl_total, tpl_count, n_piece, len(totals), img_rows, n_cls
+        ),
+        out_shape=[sds((flat_rows, feat), bf16)] + [sds((width // 2 + 16, flat_rows // 2), bf16)] * n_cls,
+        in_specs=[VM] * (len(totals) + n_piece + 5),
+        out_specs=[VM] * (1 + n_cls),
+        scratch_shapes=[pltpu.VMEM((feat, cls_count), f32)],
+        compiler_params=params(20),
+        name="grad",
+    )(
+        *totals, *image_list, e, class_w, mean_rn, u, rz,
+    )
+
+    lates = [turned[0]] + [swap(turned[m], "cls", m) for m in range(1, n_cls)]
+    grad_tpl = pl.pallas_call(
+        back_kernel,
+        out_shape=sds((flat_rows, feat), bf16),
+        in_specs=[VM] * (2 + len(ticks)),
+        out_specs=VM,
+        compiler_params=params(16),
+        cost_estimate=pl.CostEstimate(
+            flops=2 * flat_rows * feat * feat,
+            bytes_accessed=2 * feat * feat + 4 * flat_rows * feat,
+            transcendentals=0,
+        ),
+        name="back",
+    )(gz, full.reshape(feat, feat), *ticks)
+
+    block = (width, feat // n_img)
+    keep, send = pl.pallas_call(
+        functools.partial(outer_kernel, n_img, n_cls, held),
+        out_shape=(sds((n_img // 2, *block), f32), sds((n_img // 2, *block), bf16)),
+        in_specs=[VM] * (2 * n_cls + len(tpl_list)),
+        out_specs=(VM, VM),
+        scratch_shapes=[pltpu.VMEM((width, feat), f32)],
+        compiler_params=params(16),
+        name="outer",
+    )(*units, *lates, *tpl_list)
+    own, own_b, *far_b = pl.pallas_call(
+        fold_kernel,
+        out_shape=[sds(block, f32)] + [sds(block, bf16)] * (n_img // 2),
+        in_specs=[VM, VM],
+        out_specs=[VM] * (1 + n_img // 2),
+        compiler_params=params(8),
+        name="fold",
+    )(keep, swap(send, "img", 1))
+    late = [
+        both(([own_b] + far_b)[m // 2], t, m)
+        for t in range(n_tpl)
+        for m in (0, *far)
+        if t or m
+    ]
+    result = pl.pallas_call(
+        final_kernel,
+        out_shape=sds((feat // n_img, width), f32),
+        in_specs=[VM] * (1 + len(late)),
+        out_specs=VM,
+        compiler_params=params(4),
+        name="final",
+    )(own, *late)
+    return grad_tpl.reshape(tpl_count, cls_count, feat), result
+
+
 def solution(mesh):
+    shape = mesh.shape
     in_specs = (
         P(("img", "tpl"), None),
         P(("img", "tpl")),
@@ -82,4 +589,13 @@
         P("img", "cls"),
     )
     out_specs = (P("tpl", ("cls", "img"), None), P("img", "cls"))
-    return jax.shard_map(body, mesh=mesh, in_specs=in_specs, out_specs=out_specs, check_vma=False)
+
+    def step(images, labels, templates, projection):
+        powers = all(shape[a] & (shape[a] - 1) == 0 for a in ("img", "cls", "tpl"))
+        small = images.size * images.dtype.itemsize <= 8 * MIB
+        chosen = body if powers and shape["img"] > 1 and small else general_body
+        return jax.shard_map(
+            chosen, mesh=mesh, in_specs=in_specs, out_specs=out_specs, check_vma=False
+        )(images, labels, templates, projection)
+
+    return step

time: 262 us -> 147 us (0.56)
  waiting for transfers between devices: 158 us -> 80.2 us
  blocking collectives: 60.5 us -> 0 us
  starting transfers between devices: 0.29 us -> 48 us
  between operations: 14.3 us -> 0.85 us
  Pallas kernels: 0 us -> 13.3 us
  matrix products: 11.6 us -> 0 us
  other arithmetic: 8.86 us -> 0 us
  local copies, waits for them, and re-layouts: 7.09 us -> 3.79 us
    ppermute x0 -> x39, waiting for transfers between devices: none -> 80.2 us  [the longest x34 80.2 us: swap(): return lax.ppermute(x, axis, [(i, i ^ mask) for i in range(n)])]
    psum x3 -> x0, waiting for transfers between devices: 69.7 us -> none  [the longest x1 26.4 us: body(): class_g = lax.psum(spread, 'tpl')]
    ppermute x0 -> x39, starting transfers between devices: none -> 48 us  [the longest x34 43.5 us: swap(): return lax.ppermute(x, axis, [(i, i ^ mask) for i in range(n)])]
    all_gather x2 -> x0, waiting for transfers between devices: 39.8 us -> none  [the longest x1 29 us: body(): full_proj = lax.all_gather(wide_proj, 'img', axis=0, tiled=True)]
    all_gather x2 -> x0, blocking collectives: 31.3 us -> none  [the longest x1 23.5 us: body(): wide_proj = lax.all_gather(projection, 'cls', axis=1, tiled=True)]
    unnamed x8 -> x0, waiting for transfers between devices: 25.6 us -> none
    reduce_scatter x1 -> x0, waiting for transfers between devices: 23.3 us -> none  [body(): lax.psum_scatter(logit_scale * jnp.dot(grad_logit, img_b, preferred_eleme...]
    all_to_all x1 -> x0, blocking collectives: 17.5 us -> none  [body(): lax.all_to_all(flat_tpl, 'img', split_axis=1, concat_axis=0, tiled=True)]
  transfers between devices with their start and end apart: 7 -> 39, of which waited for: 7 -> 18; matrix products, arithmetic and copies ran while one was open for 2% -> 0% of each run, Pallas kernels for 0% -> 6%
where the time goes in v2:
time: 147 us; the launch traced here: 146 us
  waiting for transfers between devices  80.2 us (55%)
  starting transfers between devices  48 us (33%)
  Pallas kernels  13.3 us (9%)
  local copies, waits for them, and re-layouts  3.79 us (3%)
    ppermute x34, waiting for transfers between devices, swap(): return lax.ppermute(x, axis, [(i, i ^ mask) for i in range(n)])  80.2 us
    ppermute x34, starting transfers between devices, swap(): return lax.ppermute(x, axis, [(i, i ^ mask) for i in range(n)])  43.5 us
    unnamed x10, local copies, waits for them, and re-layouts  3.79 us
    pallas_call x1, Pallas kernels, fast_body(): pl.pallas_call(functools.partial(text_kernel, places, tpl_count), out_sha...  2.98 us
  transfers between devices with their start and end apart: 39, of which 18 were waited for; matrix products, arithmetic and copies ran while one was open for 0% of the time, Pallas kernels for 6%

profile of v2, /device:TPU:0, one launch (start us, length us, event | category | flops | bytes accessed | tf_op | source)
XLA Modules:
  0.0 146.3 jit_solution(10067208219009178522)
XLA Ops:
  4.0 3.1 %collective-permute-start = (bf16[160,320]{1,0:T(8,128)(2,1)S(1)}, bf16[160,320]{1,0:T(8,128)(2,1)S(1)}, u32[]{:S(2)}, u32[]{:S(2)}) collective-permute-start(bf16[160,320]{1,0:T(8,128)(2,1)S(1)} %get-tuple-element.27.rest_0_), channel_id=1, source_target_pairs={{0,2},{2,0},{4,6},{6,4},{1,3},{3,1},{5,7},{7,5},{8,10},{10,8},{12,... | collective-permute-start | bytes 307208 | tf_op jit(solution)/shard_map/ppermute | solution.py:91
  7.1 2.6 %collective-permute-start.1 = (bf16[160,320]{1,0:T(8,128)(2,1)S(1)}, bf16[160,320]{1,0:T(8,128)(2,1)S(1)}, u32[]{:S(2)}, u32[]{:S(2)}) collective-permute-start(bf16[160,320]{1,0:T(8,128)(2,1)S(1)} %get-tuple-element.27.rest_0_), channel_id=1, source_target_pairs={{0,4},{2,6},{4,0},{6,2},{1,5},{3,7},{5,1},{7,3},{8,12},{10,14},{12... | collective-permute-start | bytes 307208 | tf_op jit(solution)/shard_map/ppermute | solution.py:91
  9.7 2.1 %collective-permute-done.rest_1_ = bf16[160,320]{1,0:T(8,128)(2,1)S(1)} collective-permute-done((bf16[160,320]{1,0:T(8,128)(2,1)S(1)}, bf16[160,320]{1,0:T(8,128)(2,1)S(1)}, u32[]{:S(2)}, u32[]{:S(2)}) %collective-permute-start) | collective-permute-done | bytes 102432 | tf_op jit(solution)/shard_map/ppermute | solution.py:91
  11.8 7.6 %collective-permute-done.1.rest_2_ = bf16[160,320]{1,0:T(8,128)(2,1)S(1)} collective-permute-done((bf16[160,320]{1,0:T(8,128)(2,1)S(1)}, bf16[160,320]{1,0:T(8,128)(2,1)S(1)}, u32[]{:S(2)}, u32[]{:S(2)}) %collective-permute-start.1) | collective-permute-done | bytes 102432 | tf_op jit(solution)/shard_map/ppermute | solution.py:91
  20.2 1.6 %collective-permute-start.3 = (bf16[160,1280]{1,0:T(8,128)(2,1)S(1)}, bf16[160,1280]{1,0:T(8,128)(2,1)S(1)}, u32[]{:S(2)}, u32[]{:S(2)}) collective-permute-start(bf16[160,1280]{1,0:T(8,128)(2,1)S(1)} %join.1.rest_0_), channel_id=1, source_target_pairs={{0,16},{8,24},{16,0},{24,8},{1,17},{9,25},{17,1},{25,9},{2,18},{10... | collective-permute-start | bytes 1228808 | tf_op jit(solution)/shard_map/ppermute | solution.py:91
  23.8 1.9 %collective-permute-start.30 = (bf16[256,1280]{1,0:T(8,128)(2,1)}, bf16[256,1280]{1,0:T(8,128)(2,1)S(1)}, u32[]{:S(2)}, u32[]{:S(2)}) collective-permute-start(bf16[256,1280]{1,0:T(8,128)(2,1)} %bitcast.5), channel_id=1, source_target_pairs={{0,2},{2,0},{4,6},{6,4},{1,3},{3,1},{5,7},{7,5},{8,10},{10,8},{12,... | collective-permute-start | bytes 1966088 | tf_op jit(solution)/shard_map/ppermute | solution.py:91
  25.7 3.5 %collective-permute-done.3.rest_1_ = bf16[160,1280]{1,0:T(8,128)(2,1)S(1)} collective-permute-done((bf16[160,1280]{1,0:T(8,128)(2,1)S(1)}, bf16[160,1280]{1,0:T(8,128)(2,1)S(1)}, u32[]{:S(2)}, u32[]{:S(2)}) %collective-permute-start.3) | collective-permute-done | bytes 409632 | tf_op jit(solution)/shard_map/ppermute | solution.py:91
  29.8 4.3 %collective-permute-done.4.rest_2_ = bf16[160,1280]{1,0:T(8,128)(2,1)S(1)} collective-permute-done((bf16[160,1280]{1,0:T(8,128)(2,1)S(1)}, bf16[160,1280]{1,0:T(8,128)(2,1)S(1)}, u32[]{:S(2)}, u32[]{:S(2)}) %collective-permute-start.4) | collective-permute-done | bytes 409632 | tf_op jit(solution)/shard_map/ppermute | solution.py:91
  34.7 11.4 %collective-permute-done.12.rest_3_.rest_6_ = bf16[272,1280]{1,0:T(8,128)(2,1)S(1)} collective-permute-done((bf16[272,1280]{1,0:T(8,128)(2,1)S(1)}, bf16[272,1280]{1,0:T(8,128)(2,1)S(1)}, u32[]{:S(2)}, u32[]{:S(2)}) %collective-permute-start.12) | collective-permute-done | bytes 696352 | tf_op jit(solution)/shard_map/ppermute | solution.py:91
  48.9 5.1 %collective-permute-done.5.rest_3_ = bf16[160,1280]{1,0:T(8,128)(2,1)S(1)} collective-permute-done((bf16[160,1280]{1,0:T(8,128)(2,1)S(1)}, bf16[160,1280]{1,0:T(8,128)(2,1)S(1)}, u32[]{:S(2)}, u32[]{:S(2)}) %collective-permute-start.5) | collective-permute-done | bytes 409632 | tf_op jit(solution)/shard_map/ppermute | solution.py:91
  54.6 5.4 %collective-permute-done.13.rest_4_.rest_7_ = bf16[272,1280]{1,0:T(8,128)(2,1)S(1)} collective-permute-done((bf16[272,1280]{1,0:T(8,128)(2,1)S(1)}, bf16[272,1280]{1,0:T(8,128)(2,1)S(1)}, u32[]{:S(2)}, u32[]{:S(2)}) %collective-permute-start.13) | collective-permute-done | bytes 696352 | tf_op jit(solution)/shard_map/ppermute | solution.py:91
  64.0 3.0 %text.1 = (bf16[4,2,160,1280]{3,2,1,0:T(8,128)(2,1)S(1)}, f32[256,1280]{1,0:T(8,128)S(1)}, f32[256,1]{1,0:T(8,128)S(1)}, f32[64,1280]{1,0:T(8,128)S(1)}, bf16[64,1280]{1,0:T(8,128)(2,1)S(1)}) custom-call(bf16[256,1280]{1,0:T(8,128)(2,1)S(1)} %lift.1.tpl_ref.rest_8_, bf16[160,1280]{1,0:T(8,128)(2,1)S(1)} %join.1.rest_0_, ...), custom_call_target="tpu_custom_call" | custom-call | tf_op jit(solution)/shard_map/text/pallas_call | solution.py:463
  67.0 1.6 %collective-permute-start.10 = (bf16[64,1280]{1,0:T(8,128)(2,1)S(1)}, bf16[64,1280]{1,0:T(8,128)(2,1)S(1)}, u32[]{:S(2)}, u32[]{:S(2)}) collective-permute-start(bf16[64,1280]{1,0:T(8,128)(2,1)S(1)} %get-tuple-element.29), channel_id=1, source_target_pairs={{0,1},{1,0},{2,3},{3,2},{4,5},{5,4},{6,7},{7,6},{8,9},{9,8},{10,11... | collective-permute-start | bytes 491528 | tf_op jit(solution)/shard_map/ppermute | solution.py:91
  68.6 5.1 %collective-permute-done.10.rest_0_ = bf16[64,1280]{1,0:T(8,128)(2,1)S(1)} collective-permute-done((bf16[64,1280]{1,0:T(8,128)(2,1)S(1)}, bf16[64,1280]{1,0:T(8,128)(2,1)S(1)}, u32[]{:S(2)}, u32[]{:S(2)}) %collective-permute-start.10) | collective-permute-done | bytes 163872 | tf_op jit(solution)/shard_map/ppermute | solution.py:91
  73.6 1.8 %score.1 = (f32[64,1280]{1,0:T(8,128)S(1)}, f32[64,1]{1,0:T(8,128)S(1)}, f32[8,64,256]{2,1,0:T(8,128)S(1)}, f32[8,256]{1,0:T(8,128)S(1)}) custom-call(f32[64,1280]{1,0:T(8,128)S(1)} %get-tuple-element.28.sum_ref, bf16[64,1280]{1,0:T(8,128)(2,1)S(1)} %collective-permute-done.10.rest_0_, bf16[272,1280]{1,0:T(8,128)(2,1)S(1)} %get-tuple-element.30.rest_1_.rest_4_, ...), custom_call_target="tpu_custom_call" | custom-call | tf_op jit(solution)/shard_map/score/pallas_call | solution.py:495
  75.8 8.3 %collective-permute-start.24 = (bf16[336,256]{1,0:T(8,128)(2,1)S(1)}, bf16[336,256]{1,0:T(8,128)(2,1)S(1)}, u32[]{:S(2)}, u32[]{:S(2)}) collective-permute-start(bf16[336,256]{1,0:T(8,128)(2,1)S(1)} %get-tuple-element.40), channel_id=1, source_target_pairs={{0,2},{2,0},{4,6},{6,4},{1,3},{3,1},{5,7},{7,5},{8,10},{10,8},{12,... | collective-permute-start | bytes 516104 | tf_op jit(solution)/shard_map/ppermute | solution.py:91
  86.9 2.2 %collective-permute-done.19.rest_1_ = f32[8,256]{1,0:T(8,128)S(1)} collective-permute-done((f32[8,256]{1,0:T(8,128)S(1)}, f32[8,256]{1,0:T(8,128)S(1)}, u32[]{:S(2)}, u32[]{:S(2)}) %collective-permute-start.19) | collective-permute-done | bytes 8224 | tf_op jit(solution)/shard_map/ppermute | solution.py:91
  89.5 2.7 %collective-permute-done.20.rest_2_ = f32[8,256]{1,0:T(8,128)S(1)} collective-permute-done((f32[8,256]{1,0:T(8,128)S(1)}, f32[8,256]{1,0:T(8,128)S(1)}, u32[]{:S(2)}, u32[]{:S(2)}) %collective-permute-start.20) | collective-permute-done | bytes 8224 | tf_op jit(solution)/shard_map/ppermute | solution.py:91
  92.2 2.0 %collective-permute-start.21 = (f32[8,256]{1,0:T(8,128)S(1)}, f32[8,256]{1,0:T(8,128)S(1)}, u32[]{:S(2)}, u32[]{:S(2)}) collective-permute-start(f32[8,256]{1,0:T(8,128)S(1)} %fold_totals.1.rest_0_), channel_id=1, source_target_pairs={{0,2},{2,0},{4,6},{6,4},{1,3},{3,1},{5,7},{7,5},{8,10},{10,8},{12,... | collective-permute-start | bytes 24584 | tf_op jit(solution)/shard_map/ppermute | solution.py:91
  94.2 10.3 %collective-permute-done.21.rest_1_ = f32[8,256]{1,0:T(8,128)S(1)} collective-permute-done((f32[8,256]{1,0:T(8,128)S(1)}, f32[8,256]{1,0:T(8,128)S(1)}, u32[]{:S(2)}, u32[]{:S(2)}) %collective-permute-start.21) | collective-permute-done | bytes 8224 | tf_op jit(solution)/shard_map/ppermute | solution.py:91
  105.4 3.8 %collective-permute-done.22.rest_2_ = f32[8,256]{1,0:T(8,128)S(1)} collective-permute-done((f32[8,256]{1,0:T(8,128)S(1)}, f32[8,256]{1,0:T(8,128)S(1)}, u32[]{:S(2)}, u32[]{:S(2)}) %collective-permute-start.22) | collective-permute-done | bytes 8224 | tf_op jit(solution)/shard_map/ppermute | solution.py:91
  109.2 2.8 %collective-permute-start.23 = (f32[8,256]{1,0:T(8,128)S(1)}, f32[8,256]{1,0:T(8,128)S(1)}, u32[]{:S(2)}, u32[]{:S(2)}) collective-permute-start(f32[8,256]{1,0:T(8,128)S(1)} %fold_totals.1.rest_0_), channel_id=1, source_target_pairs={{0,6},{2,4},{4,2},{6,0},{1,7},{3,5},{5,3},{7,1},{8,14},{10,12},{12... | collective-permute-start | bytes 24584 | tf_op jit(solution)/shard_map/ppermute | solution.py:91
  111.9 2.8 %collective-permute-done.23.rest_3_ = f32[8,256]{1,0:T(8,128)S(1)} collective-permute-done((f32[8,256]{1,0:T(8,128)S(1)}, f32[8,256]{1,0:T(8,128)S(1)}, u32[]{:S(2)}, u32[]{:S(2)}) %collective-permute-start.23) | collective-permute-done | bytes 8224 | tf_op jit(solution)/shard_map/ppermute | solution.py:91
  114.7 2.8 %collective-permute-start.26 = (bf16[336,256]{1,0:T(8,128)(2,1)S(1)}, bf16[336,256]{1,0:T(8,128)(2,1)S(1)}, u32[]{:S(2)}, u32[]{:S(2)}) collective-permute-start(bf16[336,256]{1,0:T(8,128)(2,1)S(1)} %get-tuple-element.42), channel_id=1, source_target_pairs={{0,6},{2,4},{4,2},{6,0},{1,7},{3,5},{5,3},{7,1},{8,14},{10,12},{12... | collective-permute-start | bytes 516104 | tf_op jit(solution)/shard_map/ppermute | solution.py:91
  117.5 1.8 %grad.1 = (bf16[256,1280]{1,0:T(8,128)(2,1)S(1)}, bf16[176,128]{1,0:T(8,128)(2,1)S(1)}, bf16[176,128]{1,0:T(8,128)(2,1)S(1)}, bf16[176,128]{1,0:T(8,128)(2,1)S(1)}, bf16[176,128]{1,0:T(8,128)(2,1)S(1)}) custom-call(f32[8,256]{1,0:T(8,128)S(1)} %fold_totals.1.rest_0_, f32[8,256]{1,0:T(8,128)S(1)} %collective-permute-done.21.rest_1_, ...), custom_call_target="tpu_custom_call" | custom-call | tf_op jit(solution)/shard_map/grad/pallas_call | solution.py:519
  121.0 2.8 %collective-permute-start.29 = (bf16[176,128]{1,0:T(8,128)(2,1)S(1)}, bf16[176,128]{1,0:T(8,128)(2,1)S(1)}, u32[]{:S(2)}, u32[]{:S(2)}) collective-permute-start(bf16[176,128]{1,0:T(8,128)(2,1)S(1)} %get-tuple-element.46), channel_id=1, source_target_pairs={{0,6},{2,4},{4,2},{6,0},{1,7},{3,5},{5,3},{7,1},{8,14},{10,12},{12... | collective-permute-start | bytes 135176 | tf_op jit(solution)/shard_map/ppermute | solution.py:91
  124.4 2.4 %collective-permute-done.29.rest_7_ = bf16[176,128]{1,0:T(8,128)(2,1)S(1)} collective-permute-done((bf16[176,128]{1,0:T(8,128)(2,1)S(1)}, bf16[176,128]{1,0:T(8,128)(2,1)S(1)}, u32[]{:S(2)}, u32[]{:S(2)}) %collective-permute-start.29) | collective-permute-done | bytes 45088 | tf_op jit(solution)/shard_map/ppermute | solution.py:91
  126.8 1.8 %outer.1 = (f32[2,320,320]{2,1,0:T(8,128)S(1)}, bf16[2,320,320]{2,1,0:T(8,128)(2,1)S(1)}) custom-call(bf16[336,256]{1,0:T(8,128)(2,1)S(1)} %get-tuple-element.39.rest_0_, bf16[336,256]{1,0:T(8,128)(2,1)S(1)} %collective-permute-done.24.rest_1_, bf16[336,256]{1,0:T(8,128)(2,1)S(1)} %collective-permute-done.25.rest_2_, ...), custom_call_target="tpu_custom_call" | custom-call | tf_op jit(solution)/shard_map/outer/pallas_call | solution.py:549
  128.7 1.9 %collective-permute-done.35.recv_ref = bf16[2,320,320]{2,1,0:T(8,128)(2,1)S(1)} collective-permute-done((bf16[2,320,320]{2,1,0:T(8,128)(2,1)S(1)}, bf16[2,320,320]{2,1,0:T(8,128)(2,1)S(1)}, u32[]{:S(2)}, u32[]{:S(2)}) %collective-permute-start.35) | collective-permute-done | bytes 409632 | tf_op jit(solution)/shard_map/ppermute | solution.py:91
  134.2 1.9 %back.1 = bf16[256,1280]{1,0:T(8,128)(2,1)} custom-call(bf16[256,1280]{1,0:T(8,128)(2,1)S(1)} %get-tuple-element.37.gz_ref, bf16[1280,1280]{1,0:T(8,128)(2,1)S(1)} %bitcast.4, s32[1,128]{1,0:T(1,128)S(1)} %shard_map.59.rest_0_.rest_1_.rest_2_.rest_3_.rest_4_.rest_5_, s32[1,128]{1,0:T(1,128)S(1)} %shard_map.59.rest_0_.rest_1_.rest_2_.rest_3_.rest_4_.rest_5_, ...), custom_call_target="tpu_custom_call" | custom-call | flops 838860800 | bytes 4587520 | tf_op jit(solution)/shard_map/back/pallas_call | solution.py:534
  136.1 3.4 %collective-permute-done.36.rest_0_ = bf16[320,320]{1,0:T(8,128)(2,1)S(1)} collective-permute-done((bf16[320,320]{1,0:T(8,128)(2,1)S(1)}, bf16[320,320]{1,0:T(8,128)(2,1)S(1)}, u32[]{:S(2)}, u32[]{:S(2)}) %collective-permute-start.36) | collective-permute-done | bytes 204832 | tf_op jit(solution)/shard_map/ppermute | solution.py:91
  139.6 5.6 %collective-permute-done.37.rest_1_ = bf16[320,320]{1,0:T(8,128)(2,1)S(1)} collective-permute-done((bf16[320,320]{1,0:T(8,128)(2,1)S(1)}, bf16[320,320]{1,0:T(8,128)(2,1)S(1)}, u32[]{:S(2)}, u32[]{:S(2)}) %collective-permute-start.37) | collective-permute-done | bytes 204832 | tf_op jit(solution)/shard_map/ppermute | solution.py:91
  (69 shorter events, 26.2 us)
Async XLA Ops:
  4.0 7.8 %collective-permute-start = (bf16[160,320]{1,0:T(8,128)(2,1)S(1)}, bf16[160,320]{1,0:T(8,128)(2,1)S(1)}, u32[]{:S(2)}, u32[]{:S(2)}) collective-permute-start(bf16[160,320]{1,0:T(8,128)(2,1)S(1)} %get-tuple-element.27.rest_0_), channel_id=1, source_target_pairs={{0,2},{2,0},{4,6},{6,4},{1,3},{3,1},{5,7},{7,5},{8,10},{10,8},{12,... | collective-permute-start | bytes 307208 | tf_op jit(solution)/shard_map/ppermute | solution.py:91
  7.1 12.3 %collective-permute-start.1 = (bf16[160,320]{1,0:T(8,128)(2,1)S(1)}, bf16[160,320]{1,0:T(8,128)(2,1)S(1)}, u32[]{:S(2)}, u32[]{:S(2)}) collective-permute-start(bf16[160,320]{1,0:T(8,128)(2,1)S(1)} %get-tuple-element.27.rest_0_), channel_id=1, source_target_pairs={{0,4},{2,6},{4,0},{6,2},{1,5},{3,7},{5,1},{7,3},{8,12},{10,14},{12... | collective-permute-start | bytes 307208 | tf_op jit(solution)/shard_map/ppermute | solution.py:91
  9.7 9.7 %collective-permute-start.2 = (bf16[160,320]{1,0:T(8,128)(2,1)S(1)}, bf16[160,320]{1,0:T(8,128)(2,1)S(1)}, u32[]{:S(2)}, u32[]{:S(2)}) collective-permute-start(bf16[160,320]{1,0:T(8,128)(2,1)S(1)} %get-tuple-element.27.rest_0_), channel_id=1, source_target_pairs={{0,6},{2,4},{4,2},{6,0},{1,7},{3,5},{5,3},{7,1},{8,14},{10,12},{12... | collective-permute-start | bytes 307208 | tf_op jit(solution)/shard_map/ppermute | solution.py:91
  20.2 8.9 %collective-permute-start.3 = (bf16[160,1280]{1,0:T(8,128)(2,1)S(1)}, bf16[160,1280]{1,0:T(8,128)(2,1)S(1)}, u32[]{:S(2)}, u32[]{:S(2)}) collective-permute-start(bf16[160,1280]{1,0:T(8,128)(2,1)S(1)} %join.1.rest_0_), channel_id=1, source_target_pairs={{0,16},{8,24},{16,0},{24,8},{1,17},{9,25},{17,1},{25,9},{2,18},{10... | collective-permute-start | bytes 1228808 | tf_op jit(solution)/shard_map/ppermute | solution.py:91
  21.8 12.3 %collective-permute-start.4 = (bf16[160,1280]{1,0:T(8,128)(2,1)S(1)}, bf16[160,1280]{1,0:T(8,128)(2,1)S(1)}, u32[]{:S(2)}, u32[]{:S(2)}) collective-permute-start(bf16[160,1280]{1,0:T(8,128)(2,1)S(1)} %join.1.rest_0_), channel_id=1, source_target_pairs={{0,1},{1,0},{2,3},{3,2},{4,5},{5,4},{6,7},{7,6},{8,9},{9,8},{10,11... | collective-permute-start | bytes 1228808 | tf_op jit(solution)/shard_map/ppermute | solution.py:91
  23.3 11.4 %collective-permute-start.6 = (bf16[160,1280]{1,0:T(8,128)(2,1)S(1)}, bf16[160,1280]{1,0:T(8,128)(2,1)S(1)}, u32[]{:S(2)}, u32[]{:S(2)}) collective-permute-start(bf16[160,1280]{1,0:T(8,128)(2,1)S(1)} %join.1.rest_0_), channel_id=1, source_target_pairs={{0,8},{8,0},{16,24},{24,16},{1,9},{9,1},{17,25},{25,17},{2,10},{10... | collective-permute-start | bytes 1228808 | tf_op jit(solution)/shard_map/ppermute | solution.py:91
  23.3 22.8 %collective-permute-start.12 = (bf16[272,1280]{1,0:T(8,128)(2,1)S(1)}, bf16[272,1280]{1,0:T(8,128)(2,1)S(1)}, u32[]{:S(2)}, u32[]{:S(2)}) collective-permute-start(bf16[272,1280]{1,0:T(8,128)(2,1)S(1)} %get-tuple-element.30.rest_1_.rest_4_), channel_id=1, source_target_pairs={{0,1},{1,0},{2,3},{3,2},{4,5},{5,4},{6,7},{7,6},{8,9},{9,8},{10,11... | collective-permute-start | bytes 2088968 | tf_op jit(solution)/shard_map/ppermute | solution.py:91
  23.8 22.3 %collective-permute-start.30 = (bf16[256,1280]{1,0:T(8,128)(2,1)}, bf16[256,1280]{1,0:T(8,128)(2,1)S(1)}, u32[]{:S(2)}, u32[]{:S(2)}) collective-permute-start(bf16[256,1280]{1,0:T(8,128)(2,1)} %bitcast.5), channel_id=1, source_target_pairs={{0,2},{2,0},{4,6},{6,4},{1,3},{3,1},{5,7},{7,5},{8,10},{10,8},{12,... | collective-permute-start | bytes 1966088 | tf_op jit(solution)/shard_map/ppermute | solution.py:91
  29.1 18.5 %collective-permute-start.31 = (bf16[256,1280]{1,0:T(8,128)(2,1)}, bf16[256,1280]{1,0:T(8,128)(2,1)S(1)}, u32[]{:S(2)}, u32[]{:S(2)}) collective-permute-start(bf16[256,1280]{1,0:T(8,128)(2,1)} %bitcast.6), channel_id=1, source_target_pairs={{2,4},{4,2},{3,5},{5,3},{10,12},{12,10},{11,13},{13,11},{18,20},{2... | collective-permute-start | bytes 1966088 | tf_op jit(solution)/shard_map/ppermute | solution.py:375
  34.1 13.5 %collective-permute-start.11 = (bf16[272,1280]{1,0:T(8,128)(2,1)S(1)}, bf16[272,1280]{1,0:T(8,128)(2,1)S(1)}, u32[]{:S(2)}, u32[]{:S(2)}) collective-permute-start(bf16[272,1280]{1,0:T(8,128)(2,1)S(1)} %get-tuple-element.30.rest_1_.rest_4_), channel_id=1, source_target_pairs={{0,16},{8,24},{16,0},{24,8},{1,17},{9,25},{17,1},{25,9},{2,18},{10... | collective-permute-start | bytes 2088968 | tf_op jit(solution)/shard_map/ppermute | solution.py:91
  34.6 13.7 %collective-permute-start.14 = (bf16[272,1280]{1,0:T(8,128)(2,1)S(1)}, bf16[272,1280]{1,0:T(8,128)(2,1)S(1)}, u32[]{:S(2)}, u32[]{:S(2)}) collective-permute-start(bf16[272,1280]{1,0:T(8,128)(2,1)S(1)} %get-tuple-element.30.rest_1_.rest_4_), channel_id=1, source_target_pairs={{0,8},{8,0},{16,24},{24,16},{1,9},{9,1},{17,25},{25,17},{2,10},{10... | collective-permute-start | bytes 2088968 | tf_op jit(solution)/shard_map/ppermute | solution.py:91
  46.1 14.0 %collective-permute-start.13 = (bf16[272,1280]{1,0:T(8,128)(2,1)S(1)}, bf16[272,1280]{1,0:T(8,128)(2,1)S(1)}, u32[]{:S(2)}, u32[]{:S(2)}) collective-permute-start(bf16[272,1280]{1,0:T(8,128)(2,1)S(1)} %collective-permute-done.12.rest_3_.rest_6_), channel_id=1, source_target_pairs={{0,16},{8,24},{16,0},{24,8},{1,17},{9,25},{17,1},{25,9},{2,18},{10... | collective-permute-start | bytes 2088968 | tf_op jit(solution)/shard_map/ppermute | solution.py:91
  46.1 8.0 %collective-permute-start.5 = (bf16[160,1280]{1,0:T(8,128)(2,1)S(1)}, bf16[160,1280]{1,0:T(8,128)(2,1)S(1)}, u32[]{:S(2)}, u32[]{:S(2)}) collective-permute-start(bf16[160,1280]{1,0:T(8,128)(2,1)S(1)} %collective-permute-done.3.rest_1_), channel_id=1, source_target_pairs={{0,1},{1,0},{2,3},{3,2},{4,5},{5,4},{6,7},{7,6},{8,9},{9,8},{10,11... | collective-permute-start | bytes 1228808 | tf_op jit(solution)/shard_map/ppermute | solution.py:91
  47.6 6.4 %collective-permute-start.7 = (bf16[160,1280]{1,0:T(8,128)(2,1)S(1)}, bf16[160,1280]{1,0:T(8,128)(2,1)S(1)}, u32[]{:S(2)}, u32[]{:S(2)}) collective-permute-start(bf16[160,1280]{1,0:T(8,128)(2,1)S(1)} %collective-permute-done.3.rest_1_), channel_id=1, source_target_pairs={{0,8},{8,0},{16,24},{24,16},{1,9},{9,1},{17,25},{25,17},{2,10},{10... | collective-permute-start | bytes 1228808 | tf_op jit(solution)/shard_map/ppermute | solution.py:91
  47.6 12.5 %collective-permute-start.32 = (bf16[256,1280]{1,0:T(8,128)(2,1)S(1)}, bf16[256,1280]{1,0:T(8,128)(2,1)S(1)}, u32[]{:S(2)}, u32[]{:S(2)}) collective-permute-start(bf16[256,1280]{1,0:T(8,128)(2,1)S(1)} %collective-permute-done.30.rest_9_), channel_id=1, source_target_pairs={{2,4},{4,2},{3,5},{5,3},{10,12},{12,10},{11,13},{13,11},{18,20},{2... | collective-permute-start | bytes 1966088 | tf_op jit(solution)/shard_map/ppermute | solution.py:376
  48.3 6.2 %collective-permute-start.8 = (bf16[160,1280]{1,0:T(8,128)(2,1)S(1)}, bf16[160,1280]{1,0:T(8,128)(2,1)S(1)}, u32[]{:S(2)}, u32[]{:S(2)}) collective-permute-start(bf16[160,1280]{1,0:T(8,128)(2,1)S(1)} %collective-permute-done.4.rest_2_), channel_id=1, source_target_pairs={{0,8},{8,0},{16,24},{24,16},{1,9},{9,1},{17,25},{25,17},{2,10},{10... | collective-permute-start | bytes 1228808 | tf_op jit(solution)/shard_map/ppermute | solution.py:91
  54.0 12.9 %collective-permute-start.15 = (bf16[272,1280]{1,0:T(8,128)(2,1)S(1)}, bf16[272,1280]{1,0:T(8,128)(2,1)S(1)}, u32[]{:S(2)}, u32[]{:S(2)}) collective-permute-start(bf16[272,1280]{1,0:T(8,128)(2,1)S(1)} %collective-permute-done.11.rest_2_.rest_5_), channel_id=1, source_target_pairs={{0,8},{8,0},{16,24},{24,16},{1,9},{9,1},{17,25},{25,17},{2,10},{10... | collective-permute-start | bytes 2088968 | tf_op jit(solution)/shard_map/ppermute | solution.py:91
  54.0 7.3 %collective-permute-start.9 = (bf16[160,1280]{1,0:T(8,128)(2,1)S(1)}, bf16[160,1280]{1,0:T(8,128)(2,1)S(1)}, u32[]{:S(2)}, u32[]{:S(2)}) collective-permute-start(bf16[160,1280]{1,0:T(8,128)(2,1)S(1)} %collective-permute-done.5.rest_3_), channel_id=1, source_target_pairs={{0,8},{8,0},{16,24},{24,16},{1,9},{9,1},{17,25},{25,17},{2,10},{10... | collective-permute-start | bytes 1228808 | tf_op jit(solution)/shard_map/ppermute | solution.py:91
  54.6 14.0 %collective-permute-start.16 = (bf16[272,1280]{1,0:T(8,128)(2,1)S(1)}, bf16[272,1280]{1,0:T(8,128)(2,1)S(1)}, u32[]{:S(2)}, u32[]{:S(2)}) collective-permute-start(bf16[272,1280]{1,0:T(8,128)(2,1)S(1)} %collective-permute-done.12.rest_3_.rest_6_), channel_id=1, source_target_pairs={{0,8},{8,0},{16,24},{24,16},{1,9},{9,1},{17,25},{25,17},{2,10},{10... | collective-permute-start | bytes 2088968 | tf_op jit(solution)/shard_map/ppermute | solution.py:91
  60.1 13.6 %collective-permute-start.17 = (bf16[272,1280]{1,0:T(8,128)(2,1)S(1)}, bf16[272,1280]{1,0:T(8,128)(2,1)S(1)}, u32[]{:S(2)}, u32[]{:S(2)}) collective-permute-start(bf16[272,1280]{1,0:T(8,128)(2,1)S(1)} %collective-permute-done.13.rest_4_.rest_7_), channel_id=1, source_target_pairs={{0,8},{8,0},{16,24},{24,16},{1,9},{9,1},{17,25},{25,17},{2,10},{10... | collective-permute-start | bytes 2088968 | tf_op jit(solution)/shard_map/ppermute | solution.py:91
  60.1 59.3 %collective-permute-start.33 = (bf16[256,1280]{1,0:T(8,128)(2,1)S(1)}, bf16[256,1280]{1,0:T(8,128)(2,1)S(1)}, u32[]{:S(2)}, u32[]{:S(2)}) collective-permute-start(bf16[256,1280]{1,0:T(8,128)(2,1)S(1)} %collective-permute-done.31.rest_10_), channel_id=1, source_target_pairs={{2,0},{4,6},{3,1},{5,7},{10,8},{12,14},{11,9},{13,15},{18,16},{20,... | collective-permute-start | bytes 1966088 | tf_op jit(solution)/shard_map/ppermute | solution.py:377
  61.4 62.5 %collective-permute-start.34 = (bf16[256,1280]{1,0:T(8,128)(2,1)S(1)}, bf16[256,1280]{1,0:T(8,128)(2,1)S(1)}, u32[]{:S(2)}, u32[]{:S(2)}) collective-permute-start(bf16[256,1280]{1,0:T(8,128)(2,1)S(1)} %collective-permute-done.32.rest_11_), channel_id=1, source_target_pairs={{2,0},{4,6},{3,1},{5,7},{10,8},{12,14},{11,9},{13,15},{18,16},{20,... | collective-permute-start | bytes 1966088 | tf_op jit(solution)/shard_map/ppermute | solution.py:378
  67.0 6.7 %collective-permute-start.10 = (bf16[64,1280]{1,0:T(8,128)(2,1)S(1)}, bf16[64,1280]{1,0:T(8,128)(2,1)S(1)}, u32[]{:S(2)}, u32[]{:S(2)}) collective-permute-start(bf16[64,1280]{1,0:T(8,128)(2,1)S(1)} %get-tuple-element.29), channel_id=1, source_target_pairs={{0,1},{1,0},{2,3},{3,2},{4,5},{5,4},{6,7},{7,6},{8,9},{9,8},{10,11... | collective-permute-start | bytes 491528 | tf_op jit(solution)/shard_map/ppermute | solution.py:91
  75.4 10.0 %collective-permute-start.18 = (f32[8,256]{1,0:T(8,128)S(1)}, f32[8,256]{1,0:T(8,128)S(1)}, u32[]{:S(2)}, u32[]{:S(2)}) collective-permute-start(f32[8,256]{1,0:T(8,128)S(1)} %get-tuple-element.31.tot_ref), channel_id=1, source_target_pairs={{0,8},{8,0},{16,24},{24,16},{1,9},{9,1},{17,25},{25,17},{2,10},{10... | collective-permute-start | bytes 24584 | tf_op jit(solution)/shard_map/ppermute | solution.py:91
  75.8 43.6 %collective-permute-start.24 = (bf16[336,256]{1,0:T(8,128)(2,1)S(1)}, bf16[336,256]{1,0:T(8,128)(2,1)S(1)}, u32[]{:S(2)}, u32[]{:S(2)}) collective-permute-start(bf16[336,256]{1,0:T(8,128)(2,1)S(1)} %get-tuple-element.40), channel_id=1, source_target_pairs={{0,2},{2,0},{4,6},{6,4},{1,3},{3,1},{5,7},{7,5},{8,10},{10,8},{12,... | collective-permute-start | bytes 516104 | tf_op jit(solution)/shard_map/ppermute | solution.py:91
  84.2 36.8 %collective-permute-start.25 = (bf16[336,256]{1,0:T(8,128)(2,1)S(1)}, bf16[336,256]{1,0:T(8,128)(2,1)S(1)}, u32[]{:S(2)}, u32[]{:S(2)}) collective-permute-start(bf16[336,256]{1,0:T(8,128)(2,1)S(1)} %get-tuple-element.41), channel_id=1, source_target_pairs={{0,4},{2,6},{4,0},{6,2},{1,5},{3,7},{5,1},{7,3},{8,12},{10,14},{12... | collective-permute-start | bytes 516104 | tf_op jit(solution)/shard_map/ppermute | solution.py:91
  92.2 12.3 %collective-permute-start.21 = (f32[8,256]{1,0:T(8,128)S(1)}, f32[8,256]{1,0:T(8,128)S(1)}, u32[]{:S(2)}, u32[]{:S(2)}) collective-permute-start(f32[8,256]{1,0:T(8,128)S(1)} %fold_totals.1.rest_0_), channel_id=1, source_target_pairs={{0,2},{2,0},{4,6},{6,4},{1,3},{3,1},{5,7},{7,5},{8,10},{10,8},{12,... | collective-permute-start | bytes 24584 | tf_op jit(solution)/shard_map/ppermute | solution.py:91
  114.7 9.1 %collective-permute-start.26 = (bf16[336,256]{1,0:T(8,128)(2,1)S(1)}, bf16[336,256]{1,0:T(8,128)(2,1)S(1)}, u32[]{:S(2)}, u32[]{:S(2)}) collective-permute-start(bf16[336,256]{1,0:T(8,128)(2,1)S(1)} %get-tuple-element.42), channel_id=1, source_target_pairs={{0,6},{2,4},{4,2},{6,0},{1,7},{3,5},{5,3},{7,1},{8,14},{10,12},{12... | collective-permute-start | bytes 516104 | tf_op jit(solution)/shard_map/ppermute | solution.py:91
  121.0 5.8 %collective-permute-start.29 = (bf16[176,128]{1,0:T(8,128)(2,1)S(1)}, bf16[176,128]{1,0:T(8,128)(2,1)S(1)}, u32[]{:S(2)}, u32[]{:S(2)}) collective-permute-start(bf16[176,128]{1,0:T(8,128)(2,1)S(1)} %get-tuple-element.46), channel_id=1, source_target_pairs={{0,6},{2,4},{4,2},{6,0},{1,7},{3,5},{5,3},{7,1},{8,14},{10,12},{12... | collective-permute-start | bytes 135176 | tf_op jit(solution)/shard_map/ppermute | solution.py:91
  130.7 8.9 %collective-permute-start.36 = (bf16[320,320]{1,0:T(8,128)(2,1)S(1)}, bf16[320,320]{1,0:T(8,128)(2,1)S(1)}, u32[]{:S(2)}, u32[]{:S(2)}) collective-permute-start(bf16[320,320]{1,0:T(8,128)(2,1)S(1)} %get-tuple-element.50), channel_id=1, source_target_pairs={{0,16},{8,24},{16,0},{24,8},{1,17},{9,25},{17,1},{25,9},{2,18},{10... | collective-permute-start | bytes 614408 | tf_op jit(solution)/shard_map/ppermute | solution.py:91
  132.2 13.0 %collective-permute-start.37 = (bf16[320,320]{1,0:T(8,128)(2,1)S(1)}, bf16[320,320]{1,0:T(8,128)(2,1)S(1)}, u32[]{:S(2)}, u32[]{:S(2)}) collective-permute-start(bf16[320,320]{1,0:T(8,128)(2,1)S(1)} %get-tuple-element.51), channel_id=1, source_target_pairs={{0,1},{1,0},{2,3},{3,2},{4,5},{5,4},{6,7},{7,6},{8,9},{9,8},{10,11... | collective-permute-start | bytes 614408 | tf_op jit(solution)/shard_map/ppermute | solution.py:91
  133.7 11.5 %collective-permute-start.38 = (bf16[320,320]{1,0:T(8,128)(2,1)S(1)}, bf16[320,320]{1,0:T(8,128)(2,1)S(1)}, u32[]{:S(2)}, u32[]{:S(2)}) collective-permute-start(bf16[320,320]{1,0:T(8,128)(2,1)S(1)} %get-tuple-element.50), channel_id=1, source_target_pairs={{0,17},{1,16},{8,25},{9,24},{16,1},{17,0},{24,9},{25,8},{2,19},{3,... | collective-permute-start | bytes 614408 | tf_op jit(solution)/shard_map/ppermute | solution.py:367
  (12 other events, 47.1 us)

commit v3 on v2

--- a/solution.py
+++ b/solution.py
@@ -122,8 +122,11 @@
     copies[1].wait()
 
 
-def lift_kernel(tpl_ref, out_ref, sem):
-    for copy in start_all([(tpl_ref, out_ref)], sem):
+def lift_kernel(tpl_ref, *rest):
+    outs, sem = rest[:-1], rest[-1]
+    rows = outs[0].shape[0]
+    pairs = [(tpl_ref.at[pl.ds(k * rows, rows)], out) for k, out in enumerate(outs)]
+    for copy in start_all(pairs, sem):
         copy.wait()
 
 
@@ -162,13 +165,15 @@
         copy.wait()
 
 
-def text_kernel(places, n_tpl, tpl_ref, *rest):
+def text_kernel(places, n_tpl, n_half, *rest):
+    tpls, rest = rest[:n_half], rest[n_half:]
     n = len(places)
     full_ref, u_ref, rz_ref, sum_ref, send_ref, sem = rest[n:]
     load_projection(places, rest[:n], full_ref, sem)
-    feat = tpl_ref.shape[1]
+    feat = tpls[0].shape[1]
     full = full_ref[...].reshape(feat, feat)
-    z = jnp.dot(tpl_ref[...], full, preferred_element_type=jnp.float32)
+    tpl = jnp.concatenate([ref[...] for ref in tpls], axis=0)
+    z = jnp.dot(tpl, full, preferred_element_type=jnp.float32)
     rz = inverse_norm(z)
     u = z * rz
     u_ref[...] = u
@@ -303,12 +308,18 @@
     ).astype(jnp.bfloat16)
 
 
-def outer_kernel(n_img, n_cls, held, *rest):
+def outer_kernel(n_img, n_cls, n_half, held, *rest):
     units, lates = rest[:n_cls], rest[n_cls : 2 * n_cls]
     tpls = rest[2 * n_cls : -3]
+    keep_ref, send_ref, acc_ref = rest[-3:]
     grads = [turned_grad(a, b) for a, b in zip(units, lates)]
-    keep_ref, send_ref, acc_ref = rest[-3:]
-    first = jnp.dot(grads[0], tpls[0][...], preferred_element_type=jnp.float32)
+
+    def product(m, slot):
+        parts = tpls[slot * n_half : (slot + 1) * n_half]
+        tpl = jnp.concatenate([ref[...] for ref in parts], axis=0)
+        return jnp.dot(grads[m], tpl, preferred_element_type=jnp.float32)
+
+    first = product(0, 0)
     plans = {}
     for z in range(n_cls):
         plans.setdefault(held(z), []).append(z)
@@ -319,9 +330,7 @@
         def _():
             acc = first
             for m in range(1, n_cls):
-                acc = acc + jnp.dot(
-                    grads[m], tpls[1 + plan[m - 1]][...], preferred_element_type=jnp.float32
-                )
+                acc = acc + product(m, 1 + plan[m - 1])
             acc_ref[...] = acc
 
     width = acc_ref.shape[1] // n_img
@@ -367,15 +376,18 @@
     return lax.ppermute(x, ("img", "tpl"), pairs)
 
 
-def gather_line(x):
+def gather_line(parts):
     n = lax.axis_size("cls")
     if n != 4:
-        return (lambda z: tuple(range(n - 1))), [swap(x, "cls", m) for m in range(1, n)]
-    one = swap(x, "cls", 1)
-    mid = lax.ppermute(x, "cls", [(1, 2), (2, 1)])
-    inner = lax.ppermute(one, "cls", [(1, 2), (2, 1)])
-    outer = lax.ppermute(mid, "cls", [(1, 0), (2, 3)])
-    last = lax.ppermute(inner, "cls", [(1, 0), (2, 3)])
+        arrays = [[swap(x, "cls", m) for x in parts] for m in range(1, n)]
+        return (lambda z: tuple(range(n - 1))), arrays
+    one, mid, inner, outer, last = [], [], [], [], []
+    for k, x in enumerate(parts):
+        one.append(swap(x, "cls", 1))
+        mid.append(lax.ppermute(x, "cls", [(1, 2), (2, 1)]))
+        inner.append(lax.ppermute(one[k], "cls", [(1, 2), (2, 1)]))
+        outer.append(lax.ppermute(mid[k], "cls", [(1, 0), (2, 3)]))
+        last.append(lax.ppermute(inner[k], "cls", [(1, 0), (2, 3)]))
     return (lambda z: (0, 2, 1) if z in (1, 2) else (0, 3, 4)), [one, mid, inner, outer, last]
 
 
@@ -394,7 +406,7 @@
     far = tuple(range(2, n_img, 2))
     tpls = tuple(range(1, n_tpl))
     label_row = labels.reshape(1, img_rows)
-    ticks = [tick(label_row) for _ in range(6)]
+    ticks = [tick(label_row) for _ in range(7)]
 
     share = proj_rows // n_tpl
     marked, part = pl.pallas_call(
@@ -453,15 +465,15 @@
     flat_tpl = templates.reshape(flat_rows, feat)
     near_tpl = pl.pallas_call(
         lift_kernel,
-        out_shape=sds((flat_rows, feat), bf16),
+        out_shape=[sds((flat_rows // 2, feat), bf16)] * 2,
         in_specs=[HB],
-        out_specs=VM,
-        scratch_shapes=[pltpu.SemaphoreType.DMA((1,))],
+        out_specs=[VM] * 2,
+        scratch_shapes=[pltpu.SemaphoreType.DMA((2,))],
         compiler_params=params(2),
         name="lift",
     )(flat_tpl)
     full, u, rz, local_sum, send_sum = pl.pallas_call(
-        functools.partial(text_kernel, places, tpl_count),
+        functools.partial(text_kernel, places, tpl_count, len(near_tpl)),
         out_shape=(
             sds((n_img, n_tpl, share, feat), bf16),
             sds((flat_rows, feat), f32),
@@ -469,15 +481,15 @@
             sds((cls_count, feat), f32),
             sds((cls_count, feat), bf16),
         ),
-        in_specs=[VM] + [HB] * len(places),
+        in_specs=[VM] * len(near_tpl) + [HB] * len(places),
         out_specs=(VM, VM, VM, VM, VM),
         scratch_shapes=[pltpu.SemaphoreType.DMA((len(places),))],
         compiler_params=params(16),
         name="text",
-    )(near_tpl, *proj_list)
-
-    held, tpl_list = gather_line(flat_tpl)
-    tpl_list = [near_tpl] + tpl_list
+    )(*near_tpl, *proj_list)
+
+    held, tpl_parts = gather_line(near_tpl)
+    tpl_list = [x for parts in [near_tpl] + tpl_parts for x in parts]
 
     others = [swap(send_sum, "tpl", t) for t in tpls]
     width = feat // n_cls
@@ -547,7 +559,7 @@
 
     block = (width, feat // n_img)
     keep, send = pl.pallas_call(
-        functools.partial(outer_kernel, n_img, n_cls, held),
+        functools.partial(outer_kernel, n_img, n_cls, len(near_tpl), held),
         out_shape=(sds((n_img // 2, *block), f32), sds((n_img // 2, *block), bf16)),
         in_specs=[VM] * (2 * n_cls + len(tpl_list)),
         out_specs=(VM, VM),

time: 147 us -> 164 us (1.12)
  waiting for transfers between devices: 80.2 us -> 91 us
  starting transfers between devices: 48 us -> 54.8 us
    ppermute x34 -> x35, waiting for transfers between devices: 80.2 us -> 89.5 us  [swap(): return lax.ppermute(x, axis, [(i, i ^ mask) for i in range(n)])]
    ppermute x4 -> x8, starting transfers between devices: 3.97 us -> 7.83 us  [the longest x2 2.57 us: gather_line(): outer.append(lax.ppermute(mid[k], 'cls', [(1, 0), (2, 3)]))]
    ppermute x34 -> x35, starting transfers between devices: 43.5 us -> 45.5 us  [swap(): return lax.ppermute(x, axis, [(i, i ^ mask) for i in range(n)])]
  transfers between devices with their start and end apart: 39 -> 44, of which waited for: 18 -> 19; matrix products, arithmetic and copies ran while one was open for 0% -> 0% of each run, Pallas kernels for 6% -> 6%
where the time goes in v3:
time: 164 us
  waiting for transfers between devices  91 us (55%)
  starting transfers between devices  54.8 us (33%)
  Pallas kernels  13.4 us (8%)
  local copies, waits for them, and re-layouts  3.79 us (2%)
    ppermute x35, waiting for transfers between devices, swap(): return lax.ppermute(x, axis, [(i, i ^ mask) for i in range(n)])  89.5 us
    ppermute x35, starting transfers between devices, swap(): return lax.ppermute(x, axis, [(i, i ^ mask) for i in range(n)])  45.5 us
    unnamed x10, local copies, waits for them, and re-layouts  3.79 us
  transfers between devices with their start and end apart: 44, of which 19 were waited for; matrix products, arithmetic and copies ran while one was open for 0% of the time, Pallas kernels for 6%

profile of v3, /device:TPU:0, one launch (start us, length us, event | category | flops | bytes accessed | tf_op | source)
XLA Modules:
  0.0 163.8 jit_solution(14969115574333000878)
XLA Ops:
  1.9 3.1 %collective-permute-start.30 = (bf16[128,1280]{1,0:T(8,128)(2,1)S(1)}, bf16[128,1280]{1,0:T(8,128)(2,1)S(1)}, u32[]{:S(2)}, u32[]{:S(2)}) collective-permute-start(bf16[128,1280]{1,0:T(8,128)(2,1)S(1)} %get-tuple-element.29.rest_0_.rest_8_), channel_id=1, source_target_pairs={{0,2},{2,0},{4,6},{6,4},{1,3},{3,1},{5,7},{7,5},{8,10},{10,8},{12,... | collective-permute-start | bytes 983048 | tf_op jit(solution)/shard_map/ppermute | solution.py:91
  8.5 3.0 %collective-permute-start.1 = (bf16[160,320]{1,0:T(8,128)(2,1)S(1)}, bf16[160,320]{1,0:T(8,128)(2,1)S(1)}, u32[]{:S(2)}, u32[]{:S(2)}) collective-permute-start(bf16[160,320]{1,0:T(8,128)(2,1)S(1)} %get-tuple-element.31.rest_0_), channel_id=1, source_target_pairs={{0,4},{2,6},{4,0},{6,2},{1,5},{3,7},{5,1},{7,3},{8,12},{10,14},{12... | collective-permute-start | bytes 307208 | tf_op jit(solution)/shard_map/ppermute | solution.py:91
  11.5 1.6 collective-permute-start.31
  13.8 5.1 %collective-permute-done.rest_1_ = bf16[160,320]{1,0:T(8,128)(2,1)S(1)} collective-permute-done((bf16[160,320]{1,0:T(8,128)(2,1)S(1)}, bf16[160,320]{1,0:T(8,128)(2,1)S(1)}, u32[]{:S(2)}, u32[]{:S(2)}) %collective-permute-start) | collective-permute-done | bytes 102432 | tf_op jit(solution)/shard_map/ppermute | solution.py:91
  18.9 4.0 %collective-permute-start.2 = (bf16[160,320]{1,0:T(8,128)(2,1)S(1)}, bf16[160,320]{1,0:T(8,128)(2,1)S(1)}, u32[]{:S(2)}, u32[]{:S(2)}) collective-permute-start(bf16[160,320]{1,0:T(8,128)(2,1)S(1)} %get-tuple-element.31.rest_0_), channel_id=1, source_target_pairs={{0,6},{2,4},{4,2},{6,0},{1,7},{3,5},{5,3},{7,1},{8,14},{10,12},{12... | collective-permute-start | bytes 307208 | tf_op jit(solution)/shard_map/ppermute | solution.py:91
  22.9 1.5 collective-permute-start.12
  24.5 5.5 %collective-permute-done.2.rest_3_ = bf16[160,320]{1,0:T(8,128)(2,1)S(1)} collective-permute-done((bf16[160,320]{1,0:T(8,128)(2,1)S(1)}, bf16[160,320]{1,0:T(8,128)(2,1)S(1)}, u32[]{:S(2)}, u32[]{:S(2)}) %collective-permute-start.2) | collective-permute-done | bytes 102432 | tf_op jit(solution)/shard_map/ppermute | solution.py:91
  31.5 1.6 collective-permute-start.3
  33.1 1.5 collective-permute-start.4
  35.2 8.7 %collective-permute-done.3.rest_3_ = bf16[160,1280]{1,0:T(8,128)(2,1)S(1)} collective-permute-done((bf16[160,1280]{1,0:T(8,128)(2,1)S(1)}, bf16[160,1280]{1,0:T(8,128)(2,1)S(1)}, u32[]{:S(2)}, u32[]{:S(2)}) %collective-permute-start.3) | collective-permute-done | bytes 409632 | tf_op jit(solution)/shard_map/ppermute | solution.py:91
  44.6 2.9 %collective-permute-done.4.rest_4_ = bf16[160,1280]{1,0:T(8,128)(2,1)S(1)} collective-permute-done((bf16[160,1280]{1,0:T(8,128)(2,1)S(1)}, bf16[160,1280]{1,0:T(8,128)(2,1)S(1)}, u32[]{:S(2)}, u32[]{:S(2)}) %collective-permute-start.4) | collective-permute-done | bytes 409632 | tf_op jit(solution)/shard_map/ppermute | solution.py:91
  51.0 4.5 %collective-permute-done.5.rest_5_ = bf16[160,1280]{1,0:T(8,128)(2,1)S(1)} collective-permute-done((bf16[160,1280]{1,0:T(8,128)(2,1)S(1)}, bf16[160,1280]{1,0:T(8,128)(2,1)S(1)}, u32[]{:S(2)}, u32[]{:S(2)}) %collective-permute-start.5) | collective-permute-done | bytes 409632 | tf_op jit(solution)/shard_map/ppermute | solution.py:91
  55.6 3.3 %collective-permute-done.11.rest_2_.rest_5_ = bf16[272,1280]{1,0:T(8,128)(2,1)S(1)} collective-permute-done((bf16[272,1280]{1,0:T(8,128)(2,1)S(1)}, bf16[272,1280]{1,0:T(8,128)(2,1)S(1)}, u32[]{:S(2)}, u32[]{:S(2)}) %collective-permute-start.11) | collective-permute-done | bytes 696352 | tf_op jit(solution)/shard_map/ppermute | solution.py:91
  59.4 12.2 %collective-permute-done.13.rest_4_.rest_7_ = bf16[272,1280]{1,0:T(8,128)(2,1)S(1)} collective-permute-done((bf16[272,1280]{1,0:T(8,128)(2,1)S(1)}, bf16[272,1280]{1,0:T(8,128)(2,1)S(1)}, u32[]{:S(2)}, u32[]{:S(2)}) %collective-permute-start.13) | collective-permute-done | bytes 696352 | tf_op jit(solution)/shard_map/ppermute | solution.py:91
  72.4 3.0 %text.1 = (bf16[4,2,160,1280]{3,2,1,0:T(8,128)(2,1)S(1)}, f32[256,1280]{1,0:T(8,128)S(1)}, f32[256,1]{1,0:T(8,128)S(1)}, f32[64,1280]{1,0:T(8,128)S(1)}, bf16[64,1280]{1,0:T(8,128)(2,1)S(1)}) custom-call(bf16[128,1280]{1,0:T(8,128)(2,1)S(1)} %get-tuple-element.29.rest_0_.rest_8_, bf16[128,1280]{1,0:T(8,128)(2,1)S(1)} %get-tuple-element.30.rest_1_.rest_9_, ...), custom_call_target="tpu_custom_call" | custom-call | tf_op jit(solution)/shard_map/text/pallas_call | solution.py:475
  75.4 1.6 collective-permute-start.10
  83.3 1.8 %score.1 = (f32[64,1280]{1,0:T(8,128)S(1)}, f32[64,1]{1,0:T(8,128)S(1)}, f32[8,64,256]{2,1,0:T(8,128)S(1)}, f32[8,256]{1,0:T(8,128)S(1)}) custom-call(f32[64,1280]{1,0:T(8,128)S(1)} %get-tuple-element.32.sum_ref, bf16[64,1280]{1,0:T(8,128)(2,1)S(1)} %collective-permute-done.10.rest_0_, bf16[272,1280]{1,0:T(8,128)(2,1)S(1)} %get-tuple-element.34.rest_1_.rest_4_, ...), custom_call_target="tpu_custom_call" | custom-call | tf_op jit(solution)/shard_map/score/pallas_call | solution.py:507
  87.8 2.2 %collective-permute-done.19.rest_1_ = f32[8,256]{1,0:T(8,128)S(1)} collective-permute-done((f32[8,256]{1,0:T(8,128)S(1)}, f32[8,256]{1,0:T(8,128)S(1)}, u32[]{:S(2)}, u32[]{:S(2)}) %collective-permute-start.19) | collective-permute-done | bytes 8224 | tf_op jit(solution)/shard_map/ppermute | solution.py:91
  90.5 2.6 %collective-permute-done.20.rest_2_ = f32[8,256]{1,0:T(8,128)S(1)} collective-permute-done((f32[8,256]{1,0:T(8,128)S(1)}, f32[8,256]{1,0:T(8,128)S(1)}, u32[]{:S(2)}, u32[]{:S(2)}) %collective-permute-start.20) | collective-permute-done | bytes 8224 | tf_op jit(solution)/shard_map/ppermute | solution.py:91
  93.1 11.7 %collective-permute-start.24 = (bf16[336,256]{1,0:T(8,128)(2,1)S(1)}, bf16[336,256]{1,0:T(8,128)(2,1)S(1)}, u32[]{:S(2)}, u32[]{:S(2)}) collective-permute-start(bf16[336,256]{1,0:T(8,128)(2,1)S(1)} %get-tuple-element.44), channel_id=1, source_target_pairs={{0,2},{2,0},{4,6},{6,4},{1,3},{3,1},{5,7},{7,5},{8,10},{10,8},{12,... | collective-permute-start | bytes 516104 | tf_op jit(solution)/shard_map/ppermute | solution.py:91
  106.7 16.4 %collective-permute-done.21.rest_1_ = f32[8,256]{1,0:T(8,128)S(1)} collective-permute-done((f32[8,256]{1,0:T(8,128)S(1)}, f32[8,256]{1,0:T(8,128)S(1)}, u32[]{:S(2)}, u32[]{:S(2)}) %collective-permute-start.21) | collective-permute-done | bytes 8224 | tf_op jit(solution)/shard_map/ppermute | solution.py:91
  124.3 4.3 %collective-permute-done.23.rest_3_ = f32[8,256]{1,0:T(8,128)S(1)} collective-permute-done((f32[8,256]{1,0:T(8,128)S(1)}, f32[8,256]{1,0:T(8,128)S(1)}, u32[]{:S(2)}, u32[]{:S(2)}) %collective-permute-start.23) | collective-permute-done | bytes 8224 | tf_op jit(solution)/shard_map/ppermute | solution.py:91
  129.8 1.8 %grad.1 = (bf16[256,1280]{1,0:T(8,128)(2,1)S(1)}, bf16[176,128]{1,0:T(8,128)(2,1)S(1)}, bf16[176,128]{1,0:T(8,128)(2,1)S(1)}, bf16[176,128]{1,0:T(8,128)(2,1)S(1)}, bf16[176,128]{1,0:T(8,128)(2,1)S(1)}) custom-call(f32[8,256]{1,0:T(8,128)S(1)} %fold_totals.1.rest_0_, f32[8,256]{1,0:T(8,128)S(1)} %collective-permute-done.21.rest_1_, ...), custom_call_target="tpu_custom_call" | custom-call | tf_op jit(solution)/shard_map/grad/pallas_call | solution.py:531
  131.7 3.2 %collective-permute-start.28 = (bf16[176,128]{1,0:T(8,128)(2,1)S(1)}, bf16[176,128]{1,0:T(8,128)(2,1)S(1)}, u32[]{:S(2)}, u32[]{:S(2)}) collective-permute-start(bf16[176,128]{1,0:T(8,128)(2,1)S(1)} %get-tuple-element.49), channel_id=1, source_target_pairs={{0,4},{2,6},{4,0},{6,2},{1,5},{3,7},{5,1},{7,3},{8,12},{10,14},{12... | collective-permute-start | bytes 135176 | tf_op jit(solution)/shard_map/ppermute | solution.py:91
  136.0 3.2 %collective-permute-done.25.rest_2_ = bf16[336,256]{1,0:T(8,128)(2,1)S(1)} collective-permute-done((bf16[336,256]{1,0:T(8,128)(2,1)S(1)}, bf16[336,256]{1,0:T(8,128)(2,1)S(1)}, u32[]{:S(2)}, u32[]{:S(2)}) %collective-permute-start.25) | collective-permute-done | bytes 172064 | tf_op jit(solution)/shard_map/ppermute | solution.py:91
  139.3 5.1 %collective-permute-done.28.rest_6_ = bf16[176,128]{1,0:T(8,128)(2,1)S(1)} collective-permute-done((bf16[176,128]{1,0:T(8,128)(2,1)S(1)}, bf16[176,128]{1,0:T(8,128)(2,1)S(1)}, u32[]{:S(2)}, u32[]{:S(2)}) %collective-permute-start.28) | collective-permute-done | bytes 45088 | tf_op jit(solution)/shard_map/ppermute | solution.py:91
  144.4 1.8 %outer.1 = (f32[2,320,320]{2,1,0:T(8,128)S(1)}, bf16[2,320,320]{2,1,0:T(8,128)(2,1)S(1)}) custom-call(bf16[336,256]{1,0:T(8,128)(2,1)S(1)} %get-tuple-element.43.rest_0_, bf16[336,256]{1,0:T(8,128)(2,1)S(1)} %collective-permute-done.24.rest_1_, bf16[336,256]{1,0:T(8,128)(2,1)S(1)} %collective-permute-done.25.rest_2_, ...), custom_call_target="tpu_custom_call" | custom-call | tf_op jit(solution)/shard_map/outer/pallas_call | solution.py:561
  146.3 1.9 %collective-permute-done.40.recv_ref = bf16[2,320,320]{2,1,0:T(8,128)(2,1)S(1)} collective-permute-done((bf16[2,320,320]{2,1,0:T(8,128)(2,1)S(1)}, bf16[2,320,320]{2,1,0:T(8,128)(2,1)S(1)}, u32[]{:S(2)}, u32[]{:S(2)}) %collective-permute-start.40) | collective-permute-done | bytes 409632 | tf_op jit(solution)/shard_map/ppermute | solution.py:91
  148.3 1.6 collective-permute-start.41
  151.8 1.9 %back.1 = bf16[256,1280]{1,0:T(8,128)(2,1)} custom-call(bf16[256,1280]{1,0:T(8,128)(2,1)S(1)} %get-tuple-element.41.gz_ref, bf16[1280,1280]{1,0:T(8,128)(2,1)S(1)} %bitcast.4, s32[1,128]{1,0:T(1,128)S(1)} %shard_map.59.rest_0_.rest_1_.rest_2_.rest_3_.rest_4_.rest_5_.rest_6_, s32[1,128]{1,0:T(1,128)S(1)} %shard_map.59.rest_0_.rest_1_.rest_2_.rest_3_.rest_4_.rest_5_.rest_6_, ...), custom_call_target="tpu_custom_call" | custom-call | flops 838860800 | bytes 4587520 | tf_op jit(solution)/shard_map/back/pallas_call | solution.py:546
  153.7 3.4 %collective-permute-done.41.rest_0_ = bf16[320,320]{1,0:T(8,128)(2,1)S(1)} collective-permute-done((bf16[320,320]{1,0:T(8,128)(2,1)S(1)}, bf16[320,320]{1,0:T(8,128)(2,1)S(1)}, u32[]{:S(2)}, u32[]{:S(2)}) %collective-permute-start.41) | collective-permute-done | bytes 204832 | tf_op jit(solution)/shard_map/ppermute | solution.py:91
  157.2 5.6 %collective-permute-done.42.rest_1_ = bf16[320,320]{1,0:T(8,128)(2,1)S(1)} collective-permute-done((bf16[320,320]{1,0:T(8,128)(2,1)S(1)}, bf16[320,320]{1,0:T(8,128)(2,1)S(1)}, u32[]{:S(2)}, u32[]{:S(2)}) %collective-permute-start.42) | collective-permute-done | bytes 204832 | tf_op jit(solution)/shard_map/ppermute | solution.py:91
  (79 shorter events, 31.2 us)
Async XLA Ops:
  1.9 29.6 %collective-permute-start.30 = (bf16[128,1280]{1,0:T(8,128)(2,1)S(1)}, bf16[128,1280]{1,0:T(8,128)(2,1)S(1)}, u32[]{:S(2)}, u32[]{:S(2)}) collective-permute-start(bf16[128,1280]{1,0:T(8,128)(2,1)S(1)} %get-tuple-element.29.rest_0_.rest_8_), channel_id=1, source_target_pairs={{0,2},{2,0},{4,6},{6,4},{1,3},{3,1},{5,7},{7,5},{8,10},{10,8},{12,... | collective-permute-start | bytes 983048 | tf_op jit(solution)/shard_map/ppermute | solution.py:91
  8.4 10.5 %collective-permute-start = (bf16[160,320]{1,0:T(8,128)(2,1)S(1)}, bf16[160,320]{1,0:T(8,128)(2,1)S(1)}, u32[]{:S(2)}, u32[]{:S(2)}) collective-permute-start(bf16[160,320]{1,0:T(8,128)(2,1)S(1)} %get-tuple-element.31.rest_0_), channel_id=1, source_target_pairs={{0,2},{2,0},{4,6},{6,4},{1,3},{3,1},{5,7},{7,5},{8,10},{10,8},{12,... | collective-permute-start | bytes 307208 | tf_op jit(solution)/shard_map/ppermute | solution.py:91
  8.5 14.5 %collective-permute-start.1 = (bf16[160,320]{1,0:T(8,128)(2,1)S(1)}, bf16[160,320]{1,0:T(8,128)(2,1)S(1)}, u32[]{:S(2)}, u32[]{:S(2)}) collective-permute-start(bf16[160,320]{1,0:T(8,128)(2,1)S(1)} %get-tuple-element.31.rest_0_), channel_id=1, source_target_pairs={{0,4},{2,6},{4,0},{6,2},{1,5},{3,7},{5,1},{7,3},{8,12},{10,14},{12... | collective-permute-start | bytes 307208 | tf_op jit(solution)/shard_map/ppermute | solution.py:91
  11.5 21.6 %collective-permute-start.31 = (bf16[128,1280]{1,0:T(8,128)(2,1)S(1)}, bf16[128,1280]{1,0:T(8,128)(2,1)S(1)}, u32[]{:S(2)}, u32[]{:S(2)}) collective-permute-start(bf16[128,1280]{1,0:T(8,128)(2,1)S(1)} %get-tuple-element.30.rest_1_.rest_9_), channel_id=1, source_target_pairs={{0,2},{2,0},{4,6},{6,4},{1,3},{3,1},{5,7},{7,5},{8,10},{10,8},{12,... | collective-permute-start | bytes 983048 | tf_op jit(solution)/shard_map/ppermute | solution.py:91
  13.1 21.5 %collective-permute-start.32 = (bf16[128,1280]{1,0:T(8,128)(2,1)S(1)}, bf16[128,1280]{1,0:T(8,128)(2,1)S(1)}, u32[]{:S(2)}, u32[]{:S(2)}) collective-permute-start(bf16[128,1280]{1,0:T(8,128)(2,1)S(1)} %get-tuple-element.29.rest_0_.rest_8_), channel_id=1, source_target_pairs={{2,4},{4,2},{3,5},{5,3},{10,12},{12,10},{11,13},{13,11},{18,20},{2... | collective-permute-start | bytes 983048 | tf_op jit(solution)/shard_map/ppermute | solution.py:387
  18.9 11.1 %collective-permute-start.2 = (bf16[160,320]{1,0:T(8,128)(2,1)S(1)}, bf16[160,320]{1,0:T(8,128)(2,1)S(1)}, u32[]{:S(2)}, u32[]{:S(2)}) collective-permute-start(bf16[160,320]{1,0:T(8,128)(2,1)S(1)} %get-tuple-element.31.rest_0_), channel_id=1, source_target_pairs={{0,6},{2,4},{4,2},{6,0},{1,7},{3,5},{5,3},{7,1},{8,14},{10,12},{12... | collective-permute-start | bytes 307208 | tf_op jit(solution)/shard_map/ppermute | solution.py:91
  22.9 26.1 %collective-permute-start.12 = (bf16[272,1280]{1,0:T(8,128)(2,1)S(1)}, bf16[272,1280]{1,0:T(8,128)(2,1)S(1)}, u32[]{:S(2)}, u32[]{:S(2)}) collective-permute-start(bf16[272,1280]{1,0:T(8,128)(2,1)S(1)} %get-tuple-element.34.rest_1_.rest_4_), channel_id=1, source_target_pairs={{0,1},{1,0},{2,3},{3,2},{4,5},{5,4},{6,7},{7,6},{8,9},{9,8},{10,11... | collective-permute-start | bytes 2088968 | tf_op jit(solution)/shard_map/ppermute | solution.py:91
  31.5 12.4 %collective-permute-start.3 = (bf16[160,1280]{1,0:T(8,128)(2,1)S(1)}, bf16[160,1280]{1,0:T(8,128)(2,1)S(1)}, u32[]{:S(2)}, u32[]{:S(2)}) collective-permute-start(bf16[160,1280]{1,0:T(8,128)(2,1)S(1)} %join.1.rest_2_), channel_id=1, source_target_pairs={{0,16},{8,24},{16,0},{24,8},{1,17},{9,25},{17,1},{25,9},{2,18},{10... | collective-permute-start | bytes 1228808 | tf_op jit(solution)/shard_map/ppermute | solution.py:91
  33.1 14.4 %collective-permute-start.4 = (bf16[160,1280]{1,0:T(8,128)(2,1)S(1)}, bf16[160,1280]{1,0:T(8,128)(2,1)S(1)}, u32[]{:S(2)}, u32[]{:S(2)}) collective-permute-start(bf16[160,1280]{1,0:T(8,128)(2,1)S(1)} %join.1.rest_2_), channel_id=1, source_target_pairs={{0,1},{1,0},{2,3},{3,2},{4,5},{5,4},{6,7},{7,6},{8,9},{9,8},{10,11... | collective-permute-start | bytes 1228808 | tf_op jit(solution)/shard_map/ppermute | solution.py:91
  34.6 15.9 %collective-permute-start.6 = (bf16[160,1280]{1,0:T(8,128)(2,1)S(1)}, bf16[160,1280]{1,0:T(8,128)(2,1)S(1)}, u32[]{:S(2)}, u32[]{:S(2)}) collective-permute-start(bf16[160,1280]{1,0:T(8,128)(2,1)S(1)} %join.1.rest_2_), channel_id=1, source_target_pairs={{0,8},{8,0},{16,24},{24,16},{1,9},{9,1},{17,25},{25,17},{2,10},{10... | collective-permute-start | bytes 1228808 | tf_op jit(solution)/shard_map/ppermute | solution.py:91
  34.6 24.2 %collective-permute-start.11 = (bf16[272,1280]{1,0:T(8,128)(2,1)S(1)}, bf16[272,1280]{1,0:T(8,128)(2,1)S(1)}, u32[]{:S(2)}, u32[]{:S(2)}) collective-permute-start(bf16[272,1280]{1,0:T(8,128)(2,1)S(1)} %get-tuple-element.34.rest_1_.rest_4_), channel_id=1, source_target_pairs={{0,16},{8,24},{16,0},{24,8},{1,17},{9,25},{17,1},{25,9},{2,18},{10... | collective-permute-start | bytes 2088968 | tf_op jit(solution)/shard_map/ppermute | solution.py:91
  49.0 22.7 %collective-permute-start.13 = (bf16[272,1280]{1,0:T(8,128)(2,1)S(1)}, bf16[272,1280]{1,0:T(8,128)(2,1)S(1)}, u32[]{:S(2)}, u32[]{:S(2)}) collective-permute-start(bf16[272,1280]{1,0:T(8,128)(2,1)S(1)} %collective-permute-done.12.rest_3_.rest_6_), channel_id=1, source_target_pairs={{0,16},{8,24},{16,0},{24,8},{1,17},{9,25},{17,1},{25,9},{2,18},{10... | collective-permute-start | bytes 2088968 | tf_op jit(solution)/shard_map/ppermute | solution.py:91
  50.5 8.9 %collective-permute-start.8 = (bf16[160,1280]{1,0:T(8,128)(2,1)S(1)}, bf16[160,1280]{1,0:T(8,128)(2,1)S(1)}, u32[]{:S(2)}, u32[]{:S(2)}) collective-permute-start(bf16[160,1280]{1,0:T(8,128)(2,1)S(1)} %collective-permute-done.4.rest_4_), channel_id=1, source_target_pairs={{0,8},{8,0},{16,24},{24,16},{1,9},{9,1},{17,25},{25,17},{2,10},{10... | collective-permute-start | bytes 1228808 | tf_op jit(solution)/shard_map/ppermute | solution.py:91
  55.6 16.1 %collective-permute-start.9 = (bf16[160,1280]{1,0:T(8,128)(2,1)S(1)}, bf16[160,1280]{1,0:T(8,128)(2,1)S(1)}, u32[]{:S(2)}, u32[]{:S(2)}) collective-permute-start(bf16[160,1280]{1,0:T(8,128)(2,1)S(1)} %collective-permute-done.5.rest_5_), channel_id=1, source_target_pairs={{0,8},{8,0},{16,24},{24,16},{1,9},{9,1},{17,25},{25,17},{2,10},{10... | collective-permute-start | bytes 1228808 | tf_op jit(solution)/shard_map/ppermute | solution.py:91
  58.9 18.1 %collective-permute-start.14 = (bf16[272,1280]{1,0:T(8,128)(2,1)S(1)}, bf16[272,1280]{1,0:T(8,128)(2,1)S(1)}, u32[]{:S(2)}, u32[]{:S(2)}) collective-permute-start(bf16[272,1280]{1,0:T(8,128)(2,1)S(1)} %get-tuple-element.34.rest_1_.rest_4_), channel_id=1, source_target_pairs={{0,8},{8,0},{16,24},{24,16},{1,9},{9,1},{17,25},{25,17},{2,10},{10... | collective-permute-start | bytes 2088968 | tf_op jit(solution)/shard_map/ppermute | solution.py:91
  58.9 19.4 %collective-permute-start.15 = (bf16[272,1280]{1,0:T(8,128)(2,1)S(1)}, bf16[272,1280]{1,0:T(8,128)(2,1)S(1)}, u32[]{:S(2)}, u32[]{:S(2)}) collective-permute-start(bf16[272,1280]{1,0:T(8,128)(2,1)S(1)} %collective-permute-done.11.rest_2_.rest_5_), channel_id=1, source_target_pairs={{0,8},{8,0},{16,24},{24,16},{1,9},{9,1},{17,25},{25,17},{2,10},{10... | collective-permute-start | bytes 2088968 | tf_op jit(solution)/shard_map/ppermute | solution.py:91
  59.4 20.2 %collective-permute-start.16 = (bf16[272,1280]{1,0:T(8,128)(2,1)S(1)}, bf16[272,1280]{1,0:T(8,128)(2,1)S(1)}, u32[]{:S(2)}, u32[]{:S(2)}) collective-permute-start(bf16[272,1280]{1,0:T(8,128)(2,1)S(1)} %collective-permute-done.12.rest_3_.rest_6_), channel_id=1, source_target_pairs={{0,8},{8,0},{16,24},{24,16},{1,9},{9,1},{17,25},{25,17},{2,10},{10... | collective-permute-start | bytes 2088968 | tf_op jit(solution)/shard_map/ppermute | solution.py:91
  71.7 11.7 %collective-permute-start.17 = (bf16[272,1280]{1,0:T(8,128)(2,1)S(1)}, bf16[272,1280]{1,0:T(8,128)(2,1)S(1)}, u32[]{:S(2)}, u32[]{:S(2)}) collective-permute-start(bf16[272,1280]{1,0:T(8,128)(2,1)S(1)} %collective-permute-done.13.rest_4_.rest_7_), channel_id=1, source_target_pairs={{0,8},{8,0},{16,24},{24,16},{1,9},{9,1},{17,25},{25,17},{2,10},{10... | collective-permute-start | bytes 2088968 | tf_op jit(solution)/shard_map/ppermute | solution.py:91
  77.0 27.9 %collective-permute-start.36 = (bf16[128,1280]{1,0:T(8,128)(2,1)S(1)}, bf16[128,1280]{1,0:T(8,128)(2,1)S(1)}, u32[]{:S(2)}, u32[]{:S(2)}) collective-permute-start(bf16[128,1280]{1,0:T(8,128)(2,1)S(1)} %collective-permute-done.32.rest_12_), channel_id=1, source_target_pairs={{2,0},{4,6},{3,1},{5,7},{10,8},{12,14},{11,9},{13,15},{18,16},{20,... | collective-permute-start | bytes 983048 | tf_op jit(solution)/shard_map/ppermute | solution.py:389
  78.3 28.1 %collective-permute-start.37 = (bf16[128,1280]{1,0:T(8,128)(2,1)S(1)}, bf16[128,1280]{1,0:T(8,128)(2,1)S(1)}, u32[]{:S(2)}, u32[]{:S(2)}) collective-permute-start(bf16[128,1280]{1,0:T(8,128)(2,1)S(1)} %collective-permute-done.33.rest_13_), channel_id=1, source_target_pairs={{2,0},{4,6},{3,1},{5,7},{10,8},{12,14},{11,9},{13,15},{18,16},{20,... | collective-permute-start | bytes 983048 | tf_op jit(solution)/shard_map/ppermute | solution.py:389
  79.6 52.0 %collective-permute-start.38 = (bf16[128,1280]{1,0:T(8,128)(2,1)S(1)}, bf16[128,1280]{1,0:T(8,128)(2,1)S(1)}, u32[]{:S(2)}, u32[]{:S(2)}) collective-permute-start(bf16[128,1280]{1,0:T(8,128)(2,1)S(1)} %collective-permute-done.34.rest_14_), channel_id=1, source_target_pairs={{2,0},{4,6},{3,1},{5,7},{10,8},{12,14},{11,9},{13,15},{18,16},{20,... | collective-permute-start | bytes 983048 | tf_op jit(solution)/shard_map/ppermute | solution.py:390
  82.0 49.6 %collective-permute-start.39 = (bf16[128,1280]{1,0:T(8,128)(2,1)S(1)}, bf16[128,1280]{1,0:T(8,128)(2,1)S(1)}, u32[]{:S(2)}, u32[]{:S(2)}) collective-permute-start(bf16[128,1280]{1,0:T(8,128)(2,1)S(1)} %collective-permute-done.35.rest_15_), channel_id=1, source_target_pairs={{2,0},{4,6},{3,1},{5,7},{10,8},{12,14},{11,9},{13,15},{18,16},{20,... | collective-permute-start | bytes 983048 | tf_op jit(solution)/shard_map/ppermute | solution.py:390
  93.1 41.7 %collective-permute-start.24 = (bf16[336,256]{1,0:T(8,128)(2,1)S(1)}, bf16[336,256]{1,0:T(8,128)(2,1)S(1)}, u32[]{:S(2)}, u32[]{:S(2)}) collective-permute-start(bf16[336,256]{1,0:T(8,128)(2,1)S(1)} %get-tuple-element.44), channel_id=1, source_target_pairs={{0,2},{2,0},{4,6},{6,4},{1,3},{3,1},{5,7},{7,5},{8,10},{10,8},{12,... | collective-permute-start | bytes 516104 | tf_op jit(solution)/shard_map/ppermute | solution.py:91
  104.9 18.3 %collective-permute-start.21 = (f32[8,256]{1,0:T(8,128)S(1)}, f32[8,256]{1,0:T(8,128)S(1)}, u32[]{:S(2)}, u32[]{:S(2)}) collective-permute-start(f32[8,256]{1,0:T(8,128)S(1)} %fold_totals.1.rest_0_), channel_id=1, source_target_pairs={{0,2},{2,0},{4,6},{6,4},{1,3},{3,1},{5,7},{7,5},{8,10},{10,8},{12,... | collective-permute-start | bytes 24584 | tf_op jit(solution)/shard_map/ppermute | solution.py:91
  106.4 18.0 %collective-permute-start.22 = (f32[8,256]{1,0:T(8,128)S(1)}, f32[8,256]{1,0:T(8,128)S(1)}, u32[]{:S(2)}, u32[]{:S(2)}) collective-permute-start(f32[8,256]{1,0:T(8,128)S(1)} %fold_totals.1.rest_0_), channel_id=1, source_target_pairs={{0,4},{2,6},{4,0},{6,2},{1,5},{3,7},{5,1},{7,3},{8,12},{10,14},{12... | collective-permute-start | bytes 24584 | tf_op jit(solution)/shard_map/ppermute | solution.py:91
  124.3 15.0 %collective-permute-start.25 = (bf16[336,256]{1,0:T(8,128)(2,1)S(1)}, bf16[336,256]{1,0:T(8,128)(2,1)S(1)}, u32[]{:S(2)}, u32[]{:S(2)}) collective-permute-start(bf16[336,256]{1,0:T(8,128)(2,1)S(1)} %get-tuple-element.45), channel_id=1, source_target_pairs={{0,4},{2,6},{4,0},{6,2},{1,5},{3,7},{5,1},{7,3},{8,12},{10,14},{12... | collective-permute-start | bytes 516104 | tf_op jit(solution)/shard_map/ppermute | solution.py:91
  128.6 10.7 %collective-permute-start.26 = (bf16[336,256]{1,0:T(8,128)(2,1)S(1)}, bf16[336,256]{1,0:T(8,128)(2,1)S(1)}, u32[]{:S(2)}, u32[]{:S(2)}) collective-permute-start(bf16[336,256]{1,0:T(8,128)(2,1)S(1)} %get-tuple-element.46), channel_id=1, source_target_pairs={{0,6},{2,4},{4,2},{6,0},{1,7},{3,5},{5,3},{7,1},{8,14},{10,12},{12... | collective-permute-start | bytes 516104 | tf_op jit(solution)/shard_map/ppermute | solution.py:91
  131.7 12.7 %collective-permute-start.28 = (bf16[176,128]{1,0:T(8,128)(2,1)S(1)}, bf16[176,128]{1,0:T(8,128)(2,1)S(1)}, u32[]{:S(2)}, u32[]{:S(2)}) collective-permute-start(bf16[176,128]{1,0:T(8,128)(2,1)S(1)} %get-tuple-element.49), channel_id=1, source_target_pairs={{0,4},{2,6},{4,0},{6,2},{1,5},{3,7},{5,1},{7,3},{8,12},{10,14},{12... | collective-permute-start | bytes 135176 | tf_op jit(solution)/shard_map/ppermute | solution.py:91
  134.9 9.6 %collective-permute-start.29 = (bf16[176,128]{1,0:T(8,128)(2,1)S(1)}, bf16[176,128]{1,0:T(8,128)(2,1)S(1)}, u32[]{:S(2)}, u32[]{:S(2)}) collective-permute-start(bf16[176,128]{1,0:T(8,128)(2,1)S(1)} %get-tuple-element.50), channel_id=1, source_target_pairs={{0,6},{2,4},{4,2},{6,0},{1,7},{3,5},{5,3},{7,1},{8,14},{10,12},{12... | collective-permute-start | bytes 135176 | tf_op jit(solution)/shard_map/ppermute | solution.py:91
  148.3 8.9 %collective-permute-start.41 = (bf16[320,320]{1,0:T(8,128)(2,1)S(1)}, bf16[320,320]{1,0:T(8,128)(2,1)S(1)}, u32[]{:S(2)}, u32[]{:S(2)}) collective-permute-start(bf16[320,320]{1,0:T(8,128)(2,1)S(1)} %get-tuple-element.54), channel_id=1, source_target_pairs={{0,16},{8,24},{16,0},{24,8},{1,17},{9,25},{17,1},{25,9},{2,18},{10... | collective-permute-start | bytes 614408 | tf_op jit(solution)/shard_map/ppermute | solution.py:91
  149.8 13.0 %collective-permute-start.42 = (bf16[320,320]{1,0:T(8,128)(2,1)S(1)}, bf16[320,320]{1,0:T(8,128)(2,1)S(1)}, u32[]{:S(2)}, u32[]{:S(2)}) collective-permute-start(bf16[320,320]{1,0:T(8,128)(2,1)S(1)} %get-tuple-element.55), channel_id=1, source_target_pairs={{0,1},{1,0},{2,3},{3,2},{4,5},{5,4},{6,7},{7,6},{8,9},{9,8},{10,11... | collective-permute-start | bytes 614408 | tf_op jit(solution)/shard_map/ppermute | solution.py:91
  150.3 12.5 %collective-permute-start.43 = (bf16[320,320]{1,0:T(8,128)(2,1)S(1)}, bf16[320,320]{1,0:T(8,128)(2,1)S(1)}, u32[]{:S(2)}, u32[]{:S(2)}) collective-permute-start(bf16[320,320]{1,0:T(8,128)(2,1)S(1)} %get-tuple-element.54), channel_id=1, source_target_pairs={{0,17},{1,16},{8,25},{9,24},{16,1},{17,0},{24,9},{25,8},{2,19},{3,... | collective-permute-start | bytes 614408 | tf_op jit(solution)/shard_map/ppermute | solution.py:376
  (17 other events, 85.1 us)

commit v4 on v3

--- a/solution.py
+++ b/solution.py
@@ -102,16 +102,49 @@
     return copies
 
 
+def packing(rows, cols):
+    lanes, rest = cols // 128 * 128, cols % 128
+    if rest and lanes % rest == 0 and rows % (lanes // rest * 8) == 0:
+        return lanes, rest, lanes // rest
+    return cols, 0, 0
+
+
+def packed_shape(rows, cols):
+    lanes, rest, pieces = packing(rows, cols)
+    return (rows + rows // pieces, lanes) if rest else (rows, cols)
+
+
+def pack(x):
+    rows, cols = x.shape
+    lanes, rest, pieces = packing(rows, cols)
+    if not rest:
+        return x
+    step = rows // pieces
+    side = [x[q * step : (q + 1) * step, lanes:] for q in range(pieces)]
+    return jnp.concatenate([x[:, :lanes], jnp.concatenate(side, axis=1)], axis=0)
+
+
+def unpack(x, rows, cols):
+    _, rest, pieces = packing(rows, cols)
+    if not rest:
+        return x
+    side = [x[rows:, q * rest : (q + 1) * rest] for q in range(pieces)]
+    return jnp.concatenate([x[:rows], jnp.concatenate(side, axis=0)], axis=1)
+
+
 def place(axis):
     return lax.axis_index(axis).astype(jnp.int32)
 
 
-def prep_kernel(img_ref, lab_ref, proj_ref, out_ref, part_ref, buf, sem):
+def prep_kernel(img_ref, lab_ref, proj_ref, out_ref, part_ref, buf, lab_buf, sem):
     share = part_ref.shape[0]
     at = pl.multiple_of(place("tpl") * share, share)
-    copies = start_all([(img_ref, buf), (proj_ref.at[pl.ds(at, share)], part_ref)], sem)
+    copies = start_all(
+        [(img_ref, buf), (proj_ref.at[pl.ds(at, share)], part_ref), (lab_ref, lab_buf)], sem
+    )
     rows = img_ref.shape[0]
-    lab = lab_ref[...]
+    copies[2].wait()
+    lab = lab_buf[...]
     pad = jnp.zeros((14, rows), jnp.int32)
     digits = jnp.concatenate([lab // 128, lab % 128, pad], axis=0)
     out_ref[rows:] = jnp.zeros((16, out_ref.shape[1]), jnp.bfloat16)
@@ -308,18 +341,24 @@
     ).astype(jnp.bfloat16)
 
 
-def outer_kernel(n_img, n_cls, n_half, held, *rest):
-    units, lates = rest[:n_cls], rest[n_cls : 2 * n_cls]
-    tpls = rest[2 * n_cls : -3]
+def outer_own_kernel(unit_ref, late_ref, *rest):
+    tpl = jnp.concatenate([ref[...] for ref in rest[:-1]], axis=0)
+    grad = turned_grad(unit_ref, late_ref)
+    rest[-1][...] = jnp.dot(grad, tpl, preferred_element_type=jnp.float32)
+
+
+def outer_kernel(n_img, n_cls, n_half, held, first_ref, *rest):
+    units, lates = rest[: n_cls - 1], rest[n_cls - 1 : 2 * n_cls - 2]
+    tpls = rest[2 * n_cls - 2 : -3]
     keep_ref, send_ref, acc_ref = rest[-3:]
     grads = [turned_grad(a, b) for a, b in zip(units, lates)]
 
     def product(m, slot):
         parts = tpls[slot * n_half : (slot + 1) * n_half]
         tpl = jnp.concatenate([ref[...] for ref in parts], axis=0)
-        return jnp.dot(grads[m], tpl, preferred_element_type=jnp.float32)
-
-    first = product(0, 0)
+        return jnp.dot(grads[m - 1], tpl, preferred_element_type=jnp.float32)
+
+    first = first_ref[...]
     plans = {}
     for z in range(n_cls):
         plans.setdefault(held(z), []).append(z)
@@ -330,13 +369,13 @@
         def _():
             acc = first
             for m in range(1, n_cls):
-                acc = acc + product(m, 1 + plan[m - 1])
+                acc = acc + product(m, plan[m - 1])
             acc_ref[...] = acc
 
     width = acc_ref.shape[1] // n_img
     for j in range(n_img):
         k = place("img") ^ j
-        part = acc_ref[:, j * width : (j + 1) * width]
+        part = pack(acc_ref[:, j * width : (j + 1) * width])
 
         @pl.when(k % 2 == 0)
         def _():
@@ -351,7 +390,8 @@
     total = own_ref[...]
     for other in rest[:-1]:
         total = total + other[...].astype(jnp.float32)
-    rest[-1][...] = total.T
+    cols, rows = rest[-1].shape
+    rest[-1][...] = unpack(total, rows, cols).T
 
 
 def fold_kernel(keep_ref, recv_ref, own_ref, *outs):
@@ -412,15 +452,16 @@
     marked, part = pl.pallas_call(
         prep_kernel,
         out_shape=(sds((img_rows + 16, feat), bf16), sds((share, proj_cols), bf16)),
-        in_specs=[HB, VM, HB],
+        in_specs=[HB, HB, HB],
         out_specs=(VM, VM),
         scratch_shapes=[
             pltpu.VMEM((img_rows, feat), bf16),
-            pltpu.SemaphoreType.DMA((2,)),
+            pltpu.VMEM((1, img_rows), jnp.int32),
+            pltpu.SemaphoreType.DMA((3,)),
         ],
         compiler_params=params(8),
         name="prep",
-    )(images, label_row, projection)
+    )(*(pltpu.with_memory_space_constraint(x, pltpu.HBM) for x in (images, label_row, projection)))
     shards = [part] + [swap(part, "cls", m) for m in range(1, n_cls)]
     images_at = {(0, 0): marked}
     for m in far:
@@ -489,7 +530,7 @@
     )(*near_tpl, *proj_list)
 
     held, tpl_parts = gather_line(near_tpl)
-    tpl_list = [x for parts in [near_tpl] + tpl_parts for x in parts]
+    tpl_list = [x for parts in tpl_parts for x in parts]
 
     others = [swap(send_sum, "tpl", t) for t in tpls]
     width = feat // n_cls
@@ -543,6 +584,14 @@
     )
 
     lates = [turned[0]] + [swap(turned[m], "cls", m) for m in range(1, n_cls)]
+    first = pl.pallas_call(
+        outer_own_kernel,
+        out_shape=sds((width, feat), f32),
+        in_specs=[VM] * (2 + len(near_tpl)),
+        out_specs=VM,
+        compiler_params=params(8),
+        name="outer_own",
+    )(units[0], turned[0], *near_tpl)
     grad_tpl = pl.pallas_call(
         back_kernel,
         out_shape=sds((flat_rows, feat), bf16),
@@ -557,16 +606,16 @@
         name="back",
     )(gz, full.reshape(feat, feat), *ticks)
 
-    block = (width, feat // n_img)
+    block = packed_shape(width, feat // n_img)
     keep, send = pl.pallas_call(
         functools.partial(outer_kernel, n_img, n_cls, len(near_tpl), held),
         out_shape=(sds((n_img // 2, *block), f32), sds((n_img // 2, *block), bf16)),
-        in_specs=[VM] * (2 * n_cls + len(tpl_list)),
+        in_specs=[VM] * (2 * n_cls - 1 + len(tpl_list)),
         out_specs=(VM, VM),
         scratch_shapes=[pltpu.VMEM((width, feat), f32)],
         compiler_params=params(16),
         name="outer",
-    )(*units, *lates, *tpl_list)
+    )(first, *units[1:], *lates[1:], *tpl_list)
     own, own_b, *far_b = pl.pallas_call(
         fold_kernel,
         out_shape=[sds(block, f32)] + [sds(block, bf16)] * (n_img // 2),

time: 164 us -> 157 us (0.957)
  starting transfers between devices: 54.8 us -> 49.8 us
  local copies, waits for them, and re-layouts: 3.79 us -> 1.09 us
    ppermute x35, starting transfers between devices: 45.5 us -> 40.5 us  [swap(): return lax.ppermute(x, axis, [(i, i ^ mask) for i in range(n)])]
    unnamed x10 -> x4, local copies, waits for them, and re-layouts: 3.79 us -> 1.09 us
  transfers between devices with their start and end apart: 44 -> 44, of which waited for: 19 -> 19; matrix products, arithmetic and copies ran while one was open for 0% -> 0% of each run, Pallas kernels for 6% -> 7%
where the time goes in v4:
time: 157 us
  waiting for transfers between devices  90.3 us (58%)
  starting transfers between devices  49.8 us (32%)
  Pallas kernels  14.8 us (9%)
    ppermute x35, waiting for transfers between devices, swap(): return lax.ppermute(x, axis, [(i, i ^ mask) for i in range(n)])  88.8 us
    ppermute x35, starting transfers between devices, swap(): return lax.ppermute(x, axis, [(i, i ^ mask) for i in range(n)])  40.5 us
  transfers between devices with their start and end apart: 44, of which 19 were waited for; matrix products, arithmetic and copies ran while one was open for 0% of the time, Pallas kernels for 7%

profile of v4, /device:TPU:0, one launch (start us, length us, event | category | flops | bytes accessed | tf_op | source)
XLA Modules:
  0.0 156.9 jit_solution(17858618536605892109)
XLA Ops:
  1.9 3.1 %collective-permute-start.30 = (bf16[128,1280]{1,0:T(8,128)(2,1)S(1)}, bf16[128,1280]{1,0:T(8,128)(2,1)S(1)}, u32[]{:S(2)}, u32[]{:S(2)}) collective-permute-start(bf16[128,1280]{1,0:T(8,128)(2,1)S(1)} %get-tuple-element.29.rest_0_), channel_id=1, source_target_pairs={{0,2},{2,0},{4,6},{6,4},{1,3},{3,1},{5,7},{7,5},{8,10},{10,8},{12,... | collective-permute-start | bytes 983048 | tf_op jit(solution)/shard_map/ppermute | solution.py:91
  6.5 3.0 %collective-permute-start.1 = (bf16[160,320]{1,0:T(8,128)(2,1)S(1)}, bf16[160,320]{1,0:T(8,128)(2,1)S(1)}, u32[]{:S(2)}, u32[]{:S(2)}) collective-permute-start(bf16[160,320]{1,0:T(8,128)(2,1)S(1)} %get-tuple-element.31.rest_0_), channel_id=1, source_target_pairs={{0,4},{2,6},{4,0},{6,2},{1,5},{3,7},{5,1},{7,3},{8,12},{10,14},{12... | collective-permute-start | bytes 307208 | tf_op jit(solution)/shard_map/ppermute | solution.py:91
  9.5 1.6 %collective-permute-start.31 = (bf16[128,1280]{1,0:T(8,128)(2,1)S(1)}, bf16[128,1280]{1,0:T(8,128)(2,1)S(1)}, u32[]{:S(2)}, u32[]{:S(2)}) collective-permute-start(bf16[128,1280]{1,0:T(8,128)(2,1)S(1)} %get-tuple-element.30.rest_1_), channel_id=1, source_target_pairs={{0,2},{2,0},{4,6},{6,4},{1,3},{3,1},{5,7},{7,5},{8,10},{10,8},{12,... | collective-permute-start | bytes 983048 | tf_op jit(solution)/shard_map/ppermute | solution.py:91
  11.8 7.1 %collective-permute-done.rest_1_ = bf16[160,320]{1,0:T(8,128)(2,1)S(1)} collective-permute-done((bf16[160,320]{1,0:T(8,128)(2,1)S(1)}, bf16[160,320]{1,0:T(8,128)(2,1)S(1)}, u32[]{:S(2)}, u32[]{:S(2)}) %collective-permute-start) | collective-permute-done | bytes 102432 | tf_op jit(solution)/shard_map/ppermute | solution.py:91
  18.9 4.0 %collective-permute-start.2 = (bf16[160,320]{1,0:T(8,128)(2,1)S(1)}, bf16[160,320]{1,0:T(8,128)(2,1)S(1)}, u32[]{:S(2)}, u32[]{:S(2)}) collective-permute-start(bf16[160,320]{1,0:T(8,128)(2,1)S(1)} %get-tuple-element.31.rest_0_), channel_id=1, source_target_pairs={{0,6},{2,4},{4,2},{6,0},{1,7},{3,5},{5,3},{7,1},{8,14},{10,12},{12... | collective-permute-start | bytes 307208 | tf_op jit(solution)/shard_map/ppermute | solution.py:91
  22.9 1.5 collective-permute-start.12
  24.5 5.5 %collective-permute-done.2.rest_3_ = bf16[160,320]{1,0:T(8,128)(2,1)S(1)} collective-permute-done((bf16[160,320]{1,0:T(8,128)(2,1)S(1)}, bf16[160,320]{1,0:T(8,128)(2,1)S(1)}, u32[]{:S(2)}, u32[]{:S(2)}) %collective-permute-start.2) | collective-permute-done | bytes 102432 | tf_op jit(solution)/shard_map/ppermute | solution.py:91
  31.5 1.6 collective-permute-start.3
  33.1 1.5 collective-permute-start.4
  35.2 8.7 %collective-permute-done.3.rest_3_ = bf16[160,1280]{1,0:T(8,128)(2,1)S(1)} collective-permute-done((bf16[160,1280]{1,0:T(8,128)(2,1)S(1)}, bf16[160,1280]{1,0:T(8,128)(2,1)S(1)}, u32[]{:S(2)}, u32[]{:S(2)}) %collective-permute-start.3) | collective-permute-done | bytes 409632 | tf_op jit(solution)/shard_map/ppermute | solution.py:91
  44.6 2.9 %collective-permute-done.4.rest_4_ = bf16[160,1280]{1,0:T(8,128)(2,1)S(1)} collective-permute-done((bf16[160,1280]{1,0:T(8,128)(2,1)S(1)}, bf16[160,1280]{1,0:T(8,128)(2,1)S(1)}, u32[]{:S(2)}, u32[]{:S(2)}) %collective-permute-start.4) | collective-permute-done | bytes 409632 | tf_op jit(solution)/shard_map/ppermute | solution.py:91
  51.0 4.6 %collective-permute-done.5.rest_5_ = bf16[160,1280]{1,0:T(8,128)(2,1)S(1)} collective-permute-done((bf16[160,1280]{1,0:T(8,128)(2,1)S(1)}, bf16[160,1280]{1,0:T(8,128)(2,1)S(1)}, u32[]{:S(2)}, u32[]{:S(2)}) %collective-permute-start.5) | collective-permute-done | bytes 409632 | tf_op jit(solution)/shard_map/ppermute | solution.py:91
  55.6 3.3 %collective-permute-done.11.rest_2_.rest_5_ = bf16[272,1280]{1,0:T(8,128)(2,1)S(1)} collective-permute-done((bf16[272,1280]{1,0:T(8,128)(2,1)S(1)}, bf16[272,1280]{1,0:T(8,128)(2,1)S(1)}, u32[]{:S(2)}, u32[]{:S(2)}) %collective-permute-start.11) | collective-permute-done | bytes 696352 | tf_op jit(solution)/shard_map/ppermute | solution.py:91
  59.4 12.3 %collective-permute-done.13.rest_4_.rest_7_ = bf16[272,1280]{1,0:T(8,128)(2,1)S(1)} collective-permute-done((bf16[272,1280]{1,0:T(8,128)(2,1)S(1)}, bf16[272,1280]{1,0:T(8,128)(2,1)S(1)}, u32[]{:S(2)}, u32[]{:S(2)}) %collective-permute-start.13) | collective-permute-done | bytes 696352 | tf_op jit(solution)/shard_map/ppermute | solution.py:91
  72.4 3.0 %text.1 = (bf16[4,2,160,1280]{3,2,1,0:T(8,128)(2,1)S(1)}, f32[256,1280]{1,0:T(8,128)S(1)}, f32[256,1]{1,0:T(8,128)S(1)}, f32[64,1280]{1,0:T(8,128)S(1)}, bf16[64,1280]{1,0:T(8,128)(2,1)S(1)}) custom-call(bf16[128,1280]{1,0:T(8,128)(2,1)S(1)} %get-tuple-element.29.rest_0_, bf16[128,1280]{1,0:T(8,128)(2,1)S(1)} %get-tuple-element.30.rest_1_, ...), custom_call_target="tpu_custom_call" | custom-call | tf_op jit(solution)/shard_map/text/pallas_call | solution.py:516
  75.4 1.6 %collective-permute-start.10 = (bf16[64,1280]{1,0:T(8,128)(2,1)S(1)}, bf16[64,1280]{1,0:T(8,128)(2,1)S(1)}, u32[]{:S(2)}, u32[]{:S(2)}) collective-permute-start(bf16[64,1280]{1,0:T(8,128)(2,1)S(1)} %get-tuple-element.33), channel_id=1, source_target_pairs={{0,1},{1,0},{2,3},{3,2},{4,5},{5,4},{6,7},{7,6},{8,9},{9,8},{10,11... | collective-permute-start | bytes 491528 | tf_op jit(solution)/shard_map/ppermute | solution.py:91
  83.4 1.8 %score.1 = (f32[64,1280]{1,0:T(8,128)S(1)}, f32[64,1]{1,0:T(8,128)S(1)}, f32[8,64,256]{2,1,0:T(8,128)S(1)}, f32[8,256]{1,0:T(8,128)S(1)}) custom-call(f32[64,1280]{1,0:T(8,128)S(1)} %get-tuple-element.32.sum_ref, bf16[64,1280]{1,0:T(8,128)(2,1)S(1)} %collective-permute-done.10.rest_0_, bf16[272,1280]{1,0:T(8,128)(2,1)S(1)} %get-tuple-element.34.rest_1_.rest_4_, ...), custom_call_target="tpu_custom_call" | custom-call | tf_op jit(solution)/shard_map/score/pallas_call | solution.py:548
  87.9 2.2 %collective-permute-done.19.rest_1_ = f32[8,256]{1,0:T(8,128)S(1)} collective-permute-done((f32[8,256]{1,0:T(8,128)S(1)}, f32[8,256]{1,0:T(8,128)S(1)}, u32[]{:S(2)}, u32[]{:S(2)}) %collective-permute-start.19) | collective-permute-done | bytes 8224 | tf_op jit(solution)/shard_map/ppermute | solution.py:91
  90.8 2.3 %collective-permute-done.20.rest_2_ = f32[8,256]{1,0:T(8,128)S(1)} collective-permute-done((f32[8,256]{1,0:T(8,128)S(1)}, f32[8,256]{1,0:T(8,128)S(1)}, u32[]{:S(2)}, u32[]{:S(2)}) %collective-permute-start.20) | collective-permute-done | bytes 8224 | tf_op jit(solution)/shard_map/ppermute | solution.py:91
  93.1 6.4 %collective-permute-start.24 = (bf16[336,256]{1,0:T(8,128)(2,1)S(1)}, bf16[336,256]{1,0:T(8,128)(2,1)S(1)}, u32[]{:S(2)}, u32[]{:S(2)}) collective-permute-start(bf16[336,256]{1,0:T(8,128)(2,1)S(1)} %get-tuple-element.45), channel_id=1, source_target_pairs={{0,2},{2,0},{4,6},{6,4},{1,3},{3,1},{5,7},{7,5},{8,10},{10,8},{12,... | collective-permute-start | bytes 516104 | tf_op jit(solution)/shard_map/ppermute | solution.py:91
  101.4 16.4 %collective-permute-done.21.rest_1_ = f32[8,256]{1,0:T(8,128)S(1)} collective-permute-done((f32[8,256]{1,0:T(8,128)S(1)}, f32[8,256]{1,0:T(8,128)S(1)}, u32[]{:S(2)}, u32[]{:S(2)}) %collective-permute-start.21) | collective-permute-done | bytes 8224 | tf_op jit(solution)/shard_map/ppermute | solution.py:91
  119.0 4.3 %collective-permute-done.23.rest_3_ = f32[8,256]{1,0:T(8,128)S(1)} collective-permute-done((f32[8,256]{1,0:T(8,128)S(1)}, f32[8,256]{1,0:T(8,128)S(1)}, u32[]{:S(2)}, u32[]{:S(2)}) %collective-permute-start.23) | collective-permute-done | bytes 8224 | tf_op jit(solution)/shard_map/ppermute | solution.py:91
  124.5 1.8 %grad.1 = (bf16[256,1280]{1,0:T(8,128)(2,1)S(1)}, bf16[176,128]{1,0:T(8,128)(2,1)S(1)}, bf16[176,128]{1,0:T(8,128)(2,1)S(1)}, bf16[176,128]{1,0:T(8,128)(2,1)S(1)}, bf16[176,128]{1,0:T(8,128)(2,1)S(1)}) custom-call(f32[8,256]{1,0:T(8,128)S(1)} %fold_totals.1.rest_0_, f32[8,256]{1,0:T(8,128)S(1)} %collective-permute-done.21.rest_1_, ...), custom_call_target="tpu_custom_call" | custom-call | tf_op jit(solution)/shard_map/grad/pallas_call | solution.py:572
  126.3 3.2 %collective-permute-start.28 = (bf16[176,128]{1,0:T(8,128)(2,1)S(1)}, bf16[176,128]{1,0:T(8,128)(2,1)S(1)}, u32[]{:S(2)}, u32[]{:S(2)}) collective-permute-start(bf16[176,128]{1,0:T(8,128)(2,1)S(1)} %get-tuple-element.49), channel_id=1, source_target_pairs={{0,4},{2,6},{4,0},{6,2},{1,5},{3,7},{5,1},{7,3},{8,12},{10,14},{12... | collective-permute-start | bytes 135176 | tf_op jit(solution)/shard_map/ppermute | solution.py:91
  131.2 2.8 %collective-permute-done.25.rest_1_ = bf16[336,256]{1,0:T(8,128)(2,1)S(1)} collective-permute-done((bf16[336,256]{1,0:T(8,128)(2,1)S(1)}, bf16[336,256]{1,0:T(8,128)(2,1)S(1)}, u32[]{:S(2)}, u32[]{:S(2)}) %collective-permute-start.25) | collective-permute-done | bytes 172064 | tf_op jit(solution)/shard_map/ppermute | solution.py:91
  134.0 5.1 %collective-permute-done.28.rest_4_ = bf16[176,128]{1,0:T(8,128)(2,1)S(1)} collective-permute-done((bf16[176,128]{1,0:T(8,128)(2,1)S(1)}, bf16[176,128]{1,0:T(8,128)(2,1)S(1)}, u32[]{:S(2)}, u32[]{:S(2)}) %collective-permute-start.28) | collective-permute-done | bytes 45088 | tf_op jit(solution)/shard_map/ppermute | solution.py:91
  139.1 2.0 %outer.1 = (f32[2,400,256]{2,1,0:T(8,128)S(1)}, bf16[2,400,256]{2,1,0:T(8,128)(2,1)S(1)}) custom-call(f32[320,1280]{1,0:T(8,128)S(1)} %outer_own.1.first_ref, bf16[336,256]{1,0:T(8,128)(2,1)S(1)} %collective-permute-done.24.rest_0_, bf16[336,256]{1,0:T(8,128)(2,1)S(1)} %collective-permute-done.25.rest_1_, ...), custom_call_target="tpu_custom_call" | custom-call | tf_op jit(solution)/shard_map/outer/pallas_call | solution.py:610
  141.2 1.7 %collective-permute-done.40.recv_ref = bf16[2,400,256]{2,1,0:T(8,128)(2,1)S(1)} collective-permute-done((bf16[2,400,256]{2,1,0:T(8,128)(2,1)S(1)}, bf16[2,400,256]{2,1,0:T(8,128)(2,1)S(1)}, u32[]{:S(2)}, u32[]{:S(2)}) %collective-permute-start.40) | collective-permute-done | bytes 409632 | tf_op jit(solution)/shard_map/ppermute | solution.py:91
  143.1 1.6 collective-permute-start.41
  146.6 1.9 %back.1 = bf16[256,1280]{1,0:T(8,128)(2,1)} custom-call(bf16[256,1280]{1,0:T(8,128)(2,1)S(1)} %get-tuple-element.41.gz_ref, bf16[1280,1280]{1,0:T(8,128)(2,1)S(1)} %bitcast.4, s32[1,128]{1,0:T(1,128)S(1)} %shard_map.59.rest_0_.rest_1_.rest_2_.rest_3_.rest_4_.rest_5_.rest_6_, s32[1,128]{1,0:T(1,128)S(1)} %shard_map.59.rest_0_.rest_1_.rest_2_.rest_3_.rest_4_.rest_5_.rest_6_, ...), custom_call_target="tpu_custom_call" | custom-call | flops 838860800 | bytes 4587520 | tf_op jit(solution)/shard_map/back/pallas_call | solution.py:595
  148.5 2.6 %collective-permute-done.41.rest_0_ = bf16[400,256]{1,0:T(8,128)(2,1)S(1)} collective-permute-done((bf16[400,256]{1,0:T(8,128)(2,1)S(1)}, bf16[400,256]{1,0:T(8,128)(2,1)S(1)}, u32[]{:S(2)}, u32[]{:S(2)}) %collective-permute-start.41) | collective-permute-done | bytes 204832 | tf_op jit(solution)/shard_map/ppermute | solution.py:91
  151.1 4.8 %collective-permute-done.42.rest_1_ = bf16[400,256]{1,0:T(8,128)(2,1)S(1)} collective-permute-done((bf16[400,256]{1,0:T(8,128)(2,1)S(1)}, bf16[400,256]{1,0:T(8,128)(2,1)S(1)}, u32[]{:S(2)}, u32[]{:S(2)}) %collective-permute-start.42) | collective-permute-done | bytes 204832 | tf_op jit(solution)/shard_map/ppermute | solution.py:91
  (74 shorter events, 30.0 us)
Async XLA Ops:
  1.9 29.6 %collective-permute-start.30 = (bf16[128,1280]{1,0:T(8,128)(2,1)S(1)}, bf16[128,1280]{1,0:T(8,128)(2,1)S(1)}, u32[]{:S(2)}, u32[]{:S(2)}) collective-permute-start(bf16[128,1280]{1,0:T(8,128)(2,1)S(1)} %get-tuple-element.29.rest_0_), channel_id=1, source_target_pairs={{0,2},{2,0},{4,6},{6,4},{1,3},{3,1},{5,7},{7,5},{8,10},{10,8},{12,... | collective-permute-start | bytes 983048 | tf_op jit(solution)/shard_map/ppermute | solution.py:91
  6.4 12.5 %collective-permute-start = (bf16[160,320]{1,0:T(8,128)(2,1)S(1)}, bf16[160,320]{1,0:T(8,128)(2,1)S(1)}, u32[]{:S(2)}, u32[]{:S(2)}) collective-permute-start(bf16[160,320]{1,0:T(8,128)(2,1)S(1)} %get-tuple-element.31.rest_0_), channel_id=1, source_target_pairs={{0,2},{2,0},{4,6},{6,4},{1,3},{3,1},{5,7},{7,5},{8,10},{10,8},{12,... | collective-permute-start | bytes 307208 | tf_op jit(solution)/shard_map/ppermute | solution.py:91
  6.5 16.5 %collective-permute-start.1 = (bf16[160,320]{1,0:T(8,128)(2,1)S(1)}, bf16[160,320]{1,0:T(8,128)(2,1)S(1)}, u32[]{:S(2)}, u32[]{:S(2)}) collective-permute-start(bf16[160,320]{1,0:T(8,128)(2,1)S(1)} %get-tuple-element.31.rest_0_), channel_id=1, source_target_pairs={{0,4},{2,6},{4,0},{6,2},{1,5},{3,7},{5,1},{7,3},{8,12},{10,14},{12... | collective-permute-start | bytes 307208 | tf_op jit(solution)/shard_map/ppermute | solution.py:91
  9.5 23.6 %collective-permute-start.31 = (bf16[128,1280]{1,0:T(8,128)(2,1)S(1)}, bf16[128,1280]{1,0:T(8,128)(2,1)S(1)}, u32[]{:S(2)}, u32[]{:S(2)}) collective-permute-start(bf16[128,1280]{1,0:T(8,128)(2,1)S(1)} %get-tuple-element.30.rest_1_), channel_id=1, source_target_pairs={{0,2},{2,0},{4,6},{6,4},{1,3},{3,1},{5,7},{7,5},{8,10},{10,8},{12,... | collective-permute-start | bytes 983048 | tf_op jit(solution)/shard_map/ppermute | solution.py:91
  11.1 23.5 %collective-permute-start.32 = (bf16[128,1280]{1,0:T(8,128)(2,1)S(1)}, bf16[128,1280]{1,0:T(8,128)(2,1)S(1)}, u32[]{:S(2)}, u32[]{:S(2)}) collective-permute-start(bf16[128,1280]{1,0:T(8,128)(2,1)S(1)} %get-tuple-element.29.rest_0_), channel_id=1, source_target_pairs={{2,4},{4,2},{3,5},{5,3},{10,12},{12,10},{11,13},{13,11},{18,20},{2... | collective-permute-start | bytes 983048 | tf_op jit(solution)/shard_map/ppermute | solution.py:427
  18.9 11.1 %collective-permute-start.2 = (bf16[160,320]{1,0:T(8,128)(2,1)S(1)}, bf16[160,320]{1,0:T(8,128)(2,1)S(1)}, u32[]{:S(2)}, u32[]{:S(2)}) collective-permute-start(bf16[160,320]{1,0:T(8,128)(2,1)S(1)} %get-tuple-element.31.rest_0_), channel_id=1, source_target_pairs={{0,6},{2,4},{4,2},{6,0},{1,7},{3,5},{5,3},{7,1},{8,14},{10,12},{12... | collective-permute-start | bytes 307208 | tf_op jit(solution)/shard_map/ppermute | solution.py:91
  22.9 26.1 %collective-permute-start.12 = (bf16[272,1280]{1,0:T(8,128)(2,1)S(1)}, bf16[272,1280]{1,0:T(8,128)(2,1)S(1)}, u32[]{:S(2)}, u32[]{:S(2)}) collective-permute-start(bf16[272,1280]{1,0:T(8,128)(2,1)S(1)} %get-tuple-element.34.rest_1_.rest_4_), channel_id=1, source_target_pairs={{0,1},{1,0},{2,3},{3,2},{4,5},{5,4},{6,7},{7,6},{8,9},{9,8},{10,11... | collective-permute-start | bytes 2088968 | tf_op jit(solution)/shard_map/ppermute | solution.py:91
  31.5 12.4 %collective-permute-start.3 = (bf16[160,1280]{1,0:T(8,128)(2,1)S(1)}, bf16[160,1280]{1,0:T(8,128)(2,1)S(1)}, u32[]{:S(2)}, u32[]{:S(2)}) collective-permute-start(bf16[160,1280]{1,0:T(8,128)(2,1)S(1)} %join.1.rest_2_), channel_id=1, source_target_pairs={{0,16},{8,24},{16,0},{24,8},{1,17},{9,25},{17,1},{25,9},{2,18},{10... | collective-permute-start | bytes 1228808 | tf_op jit(solution)/shard_map/ppermute | solution.py:91
  33.1 14.4 %collective-permute-start.4 = (bf16[160,1280]{1,0:T(8,128)(2,1)S(1)}, bf16[160,1280]{1,0:T(8,128)(2,1)S(1)}, u32[]{:S(2)}, u32[]{:S(2)}) collective-permute-start(bf16[160,1280]{1,0:T(8,128)(2,1)S(1)} %join.1.rest_2_), channel_id=1, source_target_pairs={{0,1},{1,0},{2,3},{3,2},{4,5},{5,4},{6,7},{7,6},{8,9},{9,8},{10,11... | collective-permute-start | bytes 1228808 | tf_op jit(solution)/shard_map/ppermute | solution.py:91
  34.6 15.9 %collective-permute-start.6 = (bf16[160,1280]{1,0:T(8,128)(2,1)S(1)}, bf16[160,1280]{1,0:T(8,128)(2,1)S(1)}, u32[]{:S(2)}, u32[]{:S(2)}) collective-permute-start(bf16[160,1280]{1,0:T(8,128)(2,1)S(1)} %join.1.rest_2_), channel_id=1, source_target_pairs={{0,8},{8,0},{16,24},{24,16},{1,9},{9,1},{17,25},{25,17},{2,10},{10... | collective-permute-start | bytes 1228808 | tf_op jit(solution)/shard_map/ppermute | solution.py:91
  34.6 24.2 %collective-permute-start.11 = (bf16[272,1280]{1,0:T(8,128)(2,1)S(1)}, bf16[272,1280]{1,0:T(8,128)(2,1)S(1)}, u32[]{:S(2)}, u32[]{:S(2)}) collective-permute-start(bf16[272,1280]{1,0:T(8,128)(2,1)S(1)} %get-tuple-element.34.rest_1_.rest_4_), channel_id=1, source_target_pairs={{0,16},{8,24},{16,0},{24,8},{1,17},{9,25},{17,1},{25,9},{2,18},{10... | collective-permute-start | bytes 2088968 | tf_op jit(solution)/shard_map/ppermute | solution.py:91
  49.0 22.7 %collective-permute-start.13 = (bf16[272,1280]{1,0:T(8,128)(2,1)S(1)}, bf16[272,1280]{1,0:T(8,128)(2,1)S(1)}, u32[]{:S(2)}, u32[]{:S(2)}) collective-permute-start(bf16[272,1280]{1,0:T(8,128)(2,1)S(1)} %collective-permute-done.12.rest_3_.rest_6_), channel_id=1, source_target_pairs={{0,16},{8,24},{16,0},{24,8},{1,17},{9,25},{17,1},{25,9},{2,18},{10... | collective-permute-start | bytes 2088968 | tf_op jit(solution)/shard_map/ppermute | solution.py:91
  50.5 8.3 %collective-permute-start.7 = (bf16[160,1280]{1,0:T(8,128)(2,1)S(1)}, bf16[160,1280]{1,0:T(8,128)(2,1)S(1)}, u32[]{:S(2)}, u32[]{:S(2)}) collective-permute-start(bf16[160,1280]{1,0:T(8,128)(2,1)S(1)} %collective-permute-done.3.rest_3_), channel_id=1, source_target_pairs={{0,8},{8,0},{16,24},{24,16},{1,9},{9,1},{17,25},{25,17},{2,10},{10... | collective-permute-start | bytes 1228808 | tf_op jit(solution)/shard_map/ppermute | solution.py:91
  50.5 8.8 %collective-permute-start.8 = (bf16[160,1280]{1,0:T(8,128)(2,1)S(1)}, bf16[160,1280]{1,0:T(8,128)(2,1)S(1)}, u32[]{:S(2)}, u32[]{:S(2)}) collective-permute-start(bf16[160,1280]{1,0:T(8,128)(2,1)S(1)} %collective-permute-done.4.rest_4_), channel_id=1, source_target_pairs={{0,8},{8,0},{16,24},{24,16},{1,9},{9,1},{17,25},{25,17},{2,10},{10... | collective-permute-start | bytes 1228808 | tf_op jit(solution)/shard_map/ppermute | solution.py:91
  55.6 16.1 %collective-permute-start.9 = (bf16[160,1280]{1,0:T(8,128)(2,1)S(1)}, bf16[160,1280]{1,0:T(8,128)(2,1)S(1)}, u32[]{:S(2)}, u32[]{:S(2)}) collective-permute-start(bf16[160,1280]{1,0:T(8,128)(2,1)S(1)} %collective-permute-done.5.rest_5_), channel_id=1, source_target_pairs={{0,8},{8,0},{16,24},{24,16},{1,9},{9,1},{17,25},{25,17},{2,10},{10... | collective-permute-start | bytes 1228808 | tf_op jit(solution)/shard_map/ppermute | solution.py:91
  58.8 18.1 %collective-permute-start.14 = (bf16[272,1280]{1,0:T(8,128)(2,1)S(1)}, bf16[272,1280]{1,0:T(8,128)(2,1)S(1)}, u32[]{:S(2)}, u32[]{:S(2)}) collective-permute-start(bf16[272,1280]{1,0:T(8,128)(2,1)S(1)} %get-tuple-element.34.rest_1_.rest_4_), channel_id=1, source_target_pairs={{0,8},{8,0},{16,24},{24,16},{1,9},{9,1},{17,25},{25,17},{2,10},{10... | collective-permute-start | bytes 2088968 | tf_op jit(solution)/shard_map/ppermute | solution.py:91
  58.8 19.4 %collective-permute-start.15 = (bf16[272,1280]{1,0:T(8,128)(2,1)S(1)}, bf16[272,1280]{1,0:T(8,128)(2,1)S(1)}, u32[]{:S(2)}, u32[]{:S(2)}) collective-permute-start(bf16[272,1280]{1,0:T(8,128)(2,1)S(1)} %collective-permute-done.11.rest_2_.rest_5_), channel_id=1, source_target_pairs={{0,8},{8,0},{16,24},{24,16},{1,9},{9,1},{17,25},{25,17},{2,10},{10... | collective-permute-start | bytes 2088968 | tf_op jit(solution)/shard_map/ppermute | solution.py:91
  59.4 20.2 %collective-permute-start.16 = (bf16[272,1280]{1,0:T(8,128)(2,1)S(1)}, bf16[272,1280]{1,0:T(8,128)(2,1)S(1)}, u32[]{:S(2)}, u32[]{:S(2)}) collective-permute-start(bf16[272,1280]{1,0:T(8,128)(2,1)S(1)} %collective-permute-done.12.rest_3_.rest_6_), channel_id=1, source_target_pairs={{0,8},{8,0},{16,24},{24,16},{1,9},{9,1},{17,25},{25,17},{2,10},{10... | collective-permute-start | bytes 2088968 | tf_op jit(solution)/shard_map/ppermute | solution.py:91
  71.7 11.7 %collective-permute-start.17 = (bf16[272,1280]{1,0:T(8,128)(2,1)S(1)}, bf16[272,1280]{1,0:T(8,128)(2,1)S(1)}, u32[]{:S(2)}, u32[]{:S(2)}) collective-permute-start(bf16[272,1280]{1,0:T(8,128)(2,1)S(1)} %collective-permute-done.13.rest_4_.rest_7_), channel_id=1, source_target_pairs={{0,8},{8,0},{16,24},{24,16},{1,9},{9,1},{17,25},{25,17},{2,10},{10... | collective-permute-start | bytes 2088968 | tf_op jit(solution)/shard_map/ppermute | solution.py:91
  77.0 22.6 %collective-permute-start.36 = (bf16[128,1280]{1,0:T(8,128)(2,1)S(1)}, bf16[128,1280]{1,0:T(8,128)(2,1)S(1)}, u32[]{:S(2)}, u32[]{:S(2)}) collective-permute-start(bf16[128,1280]{1,0:T(8,128)(2,1)S(1)} %collective-permute-done.32.rest_8_), channel_id=1, source_target_pairs={{2,0},{4,6},{3,1},{5,7},{10,8},{12,14},{11,9},{13,15},{18,16},{20,... | collective-permute-start | bytes 983048 | tf_op jit(solution)/shard_map/ppermute | solution.py:429
  78.3 22.8 %collective-permute-start.37 = (bf16[128,1280]{1,0:T(8,128)(2,1)S(1)}, bf16[128,1280]{1,0:T(8,128)(2,1)S(1)}, u32[]{:S(2)}, u32[]{:S(2)}) collective-permute-start(bf16[128,1280]{1,0:T(8,128)(2,1)S(1)} %collective-permute-done.33.rest_9_), channel_id=1, source_target_pairs={{2,0},{4,6},{3,1},{5,7},{10,8},{12,14},{11,9},{13,15},{18,16},{20,... | collective-permute-start | bytes 983048 | tf_op jit(solution)/shard_map/ppermute | solution.py:429
  79.6 46.7 %collective-permute-start.38 = (bf16[128,1280]{1,0:T(8,128)(2,1)S(1)}, bf16[128,1280]{1,0:T(8,128)(2,1)S(1)}, u32[]{:S(2)}, u32[]{:S(2)}) collective-permute-start(bf16[128,1280]{1,0:T(8,128)(2,1)S(1)} %collective-permute-done.34.rest_10_), channel_id=1, source_target_pairs={{2,0},{4,6},{3,1},{5,7},{10,8},{12,14},{11,9},{13,15},{18,16},{20,... | collective-permute-start | bytes 983048 | tf_op jit(solution)/shard_map/ppermute | solution.py:430
  82.1 44.3 %collective-permute-start.39 = (bf16[128,1280]{1,0:T(8,128)(2,1)S(1)}, bf16[128,1280]{1,0:T(8,128)(2,1)S(1)}, u32[]{:S(2)}, u32[]{:S(2)}) collective-permute-start(bf16[128,1280]{1,0:T(8,128)(2,1)S(1)} %collective-permute-done.35.rest_11_), channel_id=1, source_target_pairs={{2,0},{4,6},{3,1},{5,7},{10,8},{12,14},{11,9},{13,15},{18,16},{20,... | collective-permute-start | bytes 983048 | tf_op jit(solution)/shard_map/ppermute | solution.py:430
  93.1 36.4 %collective-permute-start.24 = (bf16[336,256]{1,0:T(8,128)(2,1)S(1)}, bf16[336,256]{1,0:T(8,128)(2,1)S(1)}, u32[]{:S(2)}, u32[]{:S(2)}) collective-permute-start(bf16[336,256]{1,0:T(8,128)(2,1)S(1)} %get-tuple-element.45), channel_id=1, source_target_pairs={{0,2},{2,0},{4,6},{6,4},{1,3},{3,1},{5,7},{7,5},{8,10},{10,8},{12,... | collective-permute-start | bytes 516104 | tf_op jit(solution)/shard_map/ppermute | solution.py:91
  99.6 18.3 %collective-permute-start.21 = (f32[8,256]{1,0:T(8,128)S(1)}, f32[8,256]{1,0:T(8,128)S(1)}, u32[]{:S(2)}, u32[]{:S(2)}) collective-permute-start(f32[8,256]{1,0:T(8,128)S(1)} %fold_totals.1.rest_0_), channel_id=1, source_target_pairs={{0,2},{2,0},{4,6},{6,4},{1,3},{3,1},{5,7},{7,5},{8,10},{10,8},{12,... | collective-permute-start | bytes 24584 | tf_op jit(solution)/shard_map/ppermute | solution.py:91
  101.1 18.0 %collective-permute-start.22 = (f32[8,256]{1,0:T(8,128)S(1)}, f32[8,256]{1,0:T(8,128)S(1)}, u32[]{:S(2)}, u32[]{:S(2)}) collective-permute-start(f32[8,256]{1,0:T(8,128)S(1)} %fold_totals.1.rest_0_), channel_id=1, source_target_pairs={{0,4},{2,6},{4,0},{6,2},{1,5},{3,7},{5,1},{7,3},{8,12},{10,14},{12... | collective-permute-start | bytes 24584 | tf_op jit(solution)/shard_map/ppermute | solution.py:91
  119.0 15.0 %collective-permute-start.25 = (bf16[336,256]{1,0:T(8,128)(2,1)S(1)}, bf16[336,256]{1,0:T(8,128)(2,1)S(1)}, u32[]{:S(2)}, u32[]{:S(2)}) collective-permute-start(bf16[336,256]{1,0:T(8,128)(2,1)S(1)} %get-tuple-element.46), channel_id=1, source_target_pairs={{0,4},{2,6},{4,0},{6,2},{1,5},{3,7},{5,1},{7,3},{8,12},{10,14},{12... | collective-permute-start | bytes 516104 | tf_op jit(solution)/shard_map/ppermute | solution.py:91
  123.3 10.7 %collective-permute-start.26 = (bf16[336,256]{1,0:T(8,128)(2,1)S(1)}, bf16[336,256]{1,0:T(8,128)(2,1)S(1)}, u32[]{:S(2)}, u32[]{:S(2)}) collective-permute-start(bf16[336,256]{1,0:T(8,128)(2,1)S(1)} %get-tuple-element.47), channel_id=1, source_target_pairs={{0,6},{2,4},{4,2},{6,0},{1,7},{3,5},{5,3},{7,1},{8,14},{10,12},{12... | collective-permute-start | bytes 516104 | tf_op jit(solution)/shard_map/ppermute | solution.py:91
  126.3 12.8 %collective-permute-start.28 = (bf16[176,128]{1,0:T(8,128)(2,1)S(1)}, bf16[176,128]{1,0:T(8,128)(2,1)S(1)}, u32[]{:S(2)}, u32[]{:S(2)}) collective-permute-start(bf16[176,128]{1,0:T(8,128)(2,1)S(1)} %get-tuple-element.49), channel_id=1, source_target_pairs={{0,4},{2,6},{4,0},{6,2},{1,5},{3,7},{5,1},{7,3},{8,12},{10,14},{12... | collective-permute-start | bytes 135176 | tf_op jit(solution)/shard_map/ppermute | solution.py:91
  129.5 9.6 %collective-permute-start.29 = (bf16[176,128]{1,0:T(8,128)(2,1)S(1)}, bf16[176,128]{1,0:T(8,128)(2,1)S(1)}, u32[]{:S(2)}, u32[]{:S(2)}) collective-permute-start(bf16[176,128]{1,0:T(8,128)(2,1)S(1)} %get-tuple-element.50), channel_id=1, source_target_pairs={{0,6},{2,4},{4,2},{6,0},{1,7},{3,5},{5,3},{7,1},{8,14},{10,12},{12... | collective-permute-start | bytes 135176 | tf_op jit(solution)/shard_map/ppermute | solution.py:91
  144.6 11.2 %collective-permute-start.42 = (bf16[400,256]{1,0:T(8,128)(2,1)S(1)}, bf16[400,256]{1,0:T(8,128)(2,1)S(1)}, u32[]{:S(2)}, u32[]{:S(2)}) collective-permute-start(bf16[400,256]{1,0:T(8,128)(2,1)S(1)} %get-tuple-element.55), channel_id=1, source_target_pairs={{0,1},{1,0},{2,3},{3,2},{4,5},{5,4},{6,7},{7,6},{8,9},{9,8},{10,11... | collective-permute-start | bytes 614408 | tf_op jit(solution)/shard_map/ppermute | solution.py:91
  145.1 10.7 %collective-permute-start.43 = (bf16[400,256]{1,0:T(8,128)(2,1)S(1)}, bf16[400,256]{1,0:T(8,128)(2,1)S(1)}, u32[]{:S(2)}, u32[]{:S(2)}) collective-permute-start(bf16[400,256]{1,0:T(8,128)(2,1)S(1)} %get-tuple-element.54), channel_id=1, source_target_pairs={{0,17},{1,16},{8,25},{9,24},{16,1},{17,0},{24,9},{25,8},{2,19},{3,... | collective-permute-start | bytes 614408 | tf_op jit(solution)/shard_map/ppermute | solution.py:416
  (14 other events, 77.2 us)

commit v5 on v4

--- a/solution.py
+++ b/solution.py
@@ -164,17 +164,17 @@
 
 
 def tick_kernel(lab_ref, out_ref):
-    out_ref[...] = lab_ref[:, :128]
+    out_ref[...] = jnp.zeros_like(out_ref)
 
 
 def tick(labels):
     return pl.pallas_call(
         tick_kernel,
         out_shape=sds((1, 128), jnp.int32),
-        in_specs=[VM],
+        in_specs=[HB],
         out_specs=VM,
         compiler_params=params(1),
-    )(labels)
+    )(pltpu.with_memory_space_constraint(labels, pltpu.HBM))
 
 
 def join_kernel(n_cls, *rest):
@@ -512,7 +512,7 @@
         scratch_shapes=[pltpu.SemaphoreType.DMA((2,))],
         compiler_params=params(2),
         name="lift",
-    )(flat_tpl)
+    )(pltpu.with_memory_space_constraint(flat_tpl, pltpu.HBM))
     full, u, rz, local_sum, send_sum = pl.pallas_call(
         functools.partial(text_kernel, places, tpl_count, len(near_tpl)),
         out_shape=(

time: 157 us -> 157 us (level)
  no operation moved by 1% of the time
where the time goes in v5:
time: 157 us
  waiting for transfers between devices  90.3 us (58%)
  starting transfers between devices  49.8 us (32%)
  Pallas kernels  15.7 us (10%)
    ppermute x35, waiting for transfers between devices, swap(): return lax.ppermute(x, axis, [(i, i ^ mask) for i in range(n)])  88.9 us
    ppermute x35, starting transfers between devices, swap(): return lax.ppermute(x, axis, [(i, i ^ mask) for i in range(n)])  40.5 us
  transfers between devices with their start and end apart: 44, of which 19 were waited for; matrix products, arithmetic and copies ran while one was open for 0% of the time, Pallas kernels for 7%

profile of v5, /device:TPU:0, one launch (start us, length us, event | category | flops | bytes accessed | tf_op | source)
XLA Modules:
  0.0 156.7 jit_solution(222933267443142540)
XLA Ops:
  1.7 3.1 %collective-permute-start.30 = (bf16[128,1280]{1,0:T(8,128)(2,1)S(1)}, bf16[128,1280]{1,0:T(8,128)(2,1)S(1)}, u32[]{:S(2)}, u32[]{:S(2)}) collective-permute-start(bf16[128,1280]{1,0:T(8,128)(2,1)S(1)} %get-tuple-element.29.rest_0_), channel_id=1, source_target_pairs={{0,2},{2,0},{4,6},{6,4},{1,3},{3,1},{5,7},{7,5},{8,10},{10,8},{12,... | collective-permute-start | bytes 983048 | tf_op jit(solution)/shard_map/ppermute | solution.py:91
  6.3 3.0 %collective-permute-start.1 = (bf16[160,320]{1,0:T(8,128)(2,1)S(1)}, bf16[160,320]{1,0:T(8,128)(2,1)S(1)}, u32[]{:S(2)}, u32[]{:S(2)}) collective-permute-start(bf16[160,320]{1,0:T(8,128)(2,1)S(1)} %get-tuple-element.31.rest_0_), channel_id=1, source_target_pairs={{0,4},{2,6},{4,0},{6,2},{1,5},{3,7},{5,1},{7,3},{8,12},{10,14},{12... | collective-permute-start | bytes 307208 | tf_op jit(solution)/shard_map/ppermute | solution.py:91
  9.3 1.6 %collective-permute-start.31 = (bf16[128,1280]{1,0:T(8,128)(2,1)S(1)}, bf16[128,1280]{1,0:T(8,128)(2,1)S(1)}, u32[]{:S(2)}, u32[]{:S(2)}) collective-permute-start(bf16[128,1280]{1,0:T(8,128)(2,1)S(1)} %get-tuple-element.30.rest_1_), channel_id=1, source_target_pairs={{0,2},{2,0},{4,6},{6,4},{1,3},{3,1},{5,7},{7,5},{8,10},{10,8},{12,... | collective-permute-start | bytes 983048 | tf_op jit(solution)/shard_map/ppermute | solution.py:91
  11.5 7.1 %collective-permute-done.rest_1_ = bf16[160,320]{1,0:T(8,128)(2,1)S(1)} collective-permute-done((bf16[160,320]{1,0:T(8,128)(2,1)S(1)}, bf16[160,320]{1,0:T(8,128)(2,1)S(1)}, u32[]{:S(2)}, u32[]{:S(2)}) %collective-permute-start) | collective-permute-done | bytes 102432 | tf_op jit(solution)/shard_map/ppermute | solution.py:91
  18.7 4.0 %collective-permute-start.2 = (bf16[160,320]{1,0:T(8,128)(2,1)S(1)}, bf16[160,320]{1,0:T(8,128)(2,1)S(1)}, u32[]{:S(2)}, u32[]{:S(2)}) collective-permute-start(bf16[160,320]{1,0:T(8,128)(2,1)S(1)} %get-tuple-element.31.rest_0_), channel_id=1, source_target_pairs={{0,6},{2,4},{4,2},{6,0},{1,7},{3,5},{5,3},{7,1},{8,14},{10,12},{12... | collective-permute-start | bytes 307208 | tf_op jit(solution)/shard_map/ppermute | solution.py:91
  22.7 1.5 collective-permute-start.12
  24.2 5.5 %collective-permute-done.2.rest_3_ = bf16[160,320]{1,0:T(8,128)(2,1)S(1)} collective-permute-done((bf16[160,320]{1,0:T(8,128)(2,1)S(1)}, bf16[160,320]{1,0:T(8,128)(2,1)S(1)}, u32[]{:S(2)}, u32[]{:S(2)}) %collective-permute-start.2) | collective-permute-done | bytes 102432 | tf_op jit(solution)/shard_map/ppermute | solution.py:91
  31.3 1.6 collective-permute-start.3
  32.9 1.5 collective-permute-start.4
  35.0 8.7 %collective-permute-done.3.rest_3_ = bf16[160,1280]{1,0:T(8,128)(2,1)S(1)} collective-permute-done((bf16[160,1280]{1,0:T(8,128)(2,1)S(1)}, bf16[160,1280]{1,0:T(8,128)(2,1)S(1)}, u32[]{:S(2)}, u32[]{:S(2)}) %collective-permute-start.3) | collective-permute-done | bytes 409632 | tf_op jit(solution)/shard_map/ppermute | solution.py:91
  44.4 2.9 %collective-permute-done.4.rest_4_ = bf16[160,1280]{1,0:T(8,128)(2,1)S(1)} collective-permute-done((bf16[160,1280]{1,0:T(8,128)(2,1)S(1)}, bf16[160,1280]{1,0:T(8,128)(2,1)S(1)}, u32[]{:S(2)}, u32[]{:S(2)}) %collective-permute-start.4) | collective-permute-done | bytes 409632 | tf_op jit(solution)/shard_map/ppermute | solution.py:91
  50.8 4.6 %collective-permute-done.5.rest_5_ = bf16[160,1280]{1,0:T(8,128)(2,1)S(1)} collective-permute-done((bf16[160,1280]{1,0:T(8,128)(2,1)S(1)}, bf16[160,1280]{1,0:T(8,128)(2,1)S(1)}, u32[]{:S(2)}, u32[]{:S(2)}) %collective-permute-start.5) | collective-permute-done | bytes 409632 | tf_op jit(solution)/shard_map/ppermute | solution.py:91
  55.4 3.3 %collective-permute-done.11.rest_2_.rest_5_ = bf16[272,1280]{1,0:T(8,128)(2,1)S(1)} collective-permute-done((bf16[272,1280]{1,0:T(8,128)(2,1)S(1)}, bf16[272,1280]{1,0:T(8,128)(2,1)S(1)}, u32[]{:S(2)}, u32[]{:S(2)}) %collective-permute-start.11) | collective-permute-done | bytes 696352 | tf_op jit(solution)/shard_map/ppermute | solution.py:91
  59.2 12.3 %collective-permute-done.13.rest_4_.rest_7_ = bf16[272,1280]{1,0:T(8,128)(2,1)S(1)} collective-permute-done((bf16[272,1280]{1,0:T(8,128)(2,1)S(1)}, bf16[272,1280]{1,0:T(8,128)(2,1)S(1)}, u32[]{:S(2)}, u32[]{:S(2)}) %collective-permute-start.13) | collective-permute-done | bytes 696352 | tf_op jit(solution)/shard_map/ppermute | solution.py:91
  72.2 3.0 %text.1 = (bf16[4,2,160,1280]{3,2,1,0:T(8,128)(2,1)S(1)}, f32[256,1280]{1,0:T(8,128)S(1)}, f32[256,1]{1,0:T(8,128)S(1)}, f32[64,1280]{1,0:T(8,128)S(1)}, bf16[64,1280]{1,0:T(8,128)(2,1)S(1)}) custom-call(bf16[128,1280]{1,0:T(8,128)(2,1)S(1)} %get-tuple-element.29.rest_0_, bf16[128,1280]{1,0:T(8,128)(2,1)S(1)} %get-tuple-element.30.rest_1_, ...), custom_call_target="tpu_custom_call" | custom-call | tf_op jit(solution)/shard_map/text/pallas_call | solution.py:516
  75.2 1.6 %collective-permute-start.10 = (bf16[64,1280]{1,0:T(8,128)(2,1)S(1)}, bf16[64,1280]{1,0:T(8,128)(2,1)S(1)}, u32[]{:S(2)}, u32[]{:S(2)}) collective-permute-start(bf16[64,1280]{1,0:T(8,128)(2,1)S(1)} %get-tuple-element.33), channel_id=1, source_target_pairs={{0,1},{1,0},{2,3},{3,2},{4,5},{5,4},{6,7},{7,6},{8,9},{9,8},{10,11... | collective-permute-start | bytes 491528 | tf_op jit(solution)/shard_map/ppermute | solution.py:91
  83.1 1.8 %score.1 = (f32[64,1280]{1,0:T(8,128)S(1)}, f32[64,1]{1,0:T(8,128)S(1)}, f32[8,64,256]{2,1,0:T(8,128)S(1)}, f32[8,256]{1,0:T(8,128)S(1)}) custom-call(f32[64,1280]{1,0:T(8,128)S(1)} %get-tuple-element.32.sum_ref, bf16[64,1280]{1,0:T(8,128)(2,1)S(1)} %collective-permute-done.10.rest_0_, bf16[272,1280]{1,0:T(8,128)(2,1)S(1)} %get-tuple-element.34.rest_1_.rest_4_, ...), custom_call_target="tpu_custom_call" | custom-call | tf_op jit(solution)/shard_map/score/pallas_call | solution.py:548
  87.6 2.2 %collective-permute-done.19.rest_1_ = f32[8,256]{1,0:T(8,128)S(1)} collective-permute-done((f32[8,256]{1,0:T(8,128)S(1)}, f32[8,256]{1,0:T(8,128)S(1)}, u32[]{:S(2)}, u32[]{:S(2)}) %collective-permute-start.19) | collective-permute-done | bytes 8224 | tf_op jit(solution)/shard_map/ppermute | solution.py:91
  90.6 2.3 %collective-permute-done.20.rest_2_ = f32[8,256]{1,0:T(8,128)S(1)} collective-permute-done((f32[8,256]{1,0:T(8,128)S(1)}, f32[8,256]{1,0:T(8,128)S(1)}, u32[]{:S(2)}, u32[]{:S(2)}) %collective-permute-start.20) | collective-permute-done | bytes 8224 | tf_op jit(solution)/shard_map/ppermute | solution.py:91
  92.9 6.4 %collective-permute-start.24 = (bf16[336,256]{1,0:T(8,128)(2,1)S(1)}, bf16[336,256]{1,0:T(8,128)(2,1)S(1)}, u32[]{:S(2)}, u32[]{:S(2)}) collective-permute-start(bf16[336,256]{1,0:T(8,128)(2,1)S(1)} %get-tuple-element.45), channel_id=1, source_target_pairs={{0,2},{2,0},{4,6},{6,4},{1,3},{3,1},{5,7},{7,5},{8,10},{10,8},{12,... | collective-permute-start | bytes 516104 | tf_op jit(solution)/shard_map/ppermute | solution.py:91
  101.2 16.4 %collective-permute-done.21.rest_1_ = f32[8,256]{1,0:T(8,128)S(1)} collective-permute-done((f32[8,256]{1,0:T(8,128)S(1)}, f32[8,256]{1,0:T(8,128)S(1)}, u32[]{:S(2)}, u32[]{:S(2)}) %collective-permute-start.21) | collective-permute-done | bytes 8224 | tf_op jit(solution)/shard_map/ppermute | solution.py:91
  118.8 4.3 %collective-permute-done.23.rest_3_ = f32[8,256]{1,0:T(8,128)S(1)} collective-permute-done((f32[8,256]{1,0:T(8,128)S(1)}, f32[8,256]{1,0:T(8,128)S(1)}, u32[]{:S(2)}, u32[]{:S(2)}) %collective-permute-start.23) | collective-permute-done | bytes 8224 | tf_op jit(solution)/shard_map/ppermute | solution.py:91
  124.2 1.8 %grad.1 = (bf16[256,1280]{1,0:T(8,128)(2,1)S(1)}, bf16[176,128]{1,0:T(8,128)(2,1)S(1)}, bf16[176,128]{1,0:T(8,128)(2,1)S(1)}, bf16[176,128]{1,0:T(8,128)(2,1)S(1)}, bf16[176,128]{1,0:T(8,128)(2,1)S(1)}) custom-call(f32[8,256]{1,0:T(8,128)S(1)} %fold_totals.1.rest_0_, f32[8,256]{1,0:T(8,128)S(1)} %collective-permute-done.21.rest_1_, ...), custom_call_target="tpu_custom_call" | custom-call | tf_op jit(solution)/shard_map/grad/pallas_call | solution.py:572
  126.1 3.2 %collective-permute-start.28 = (bf16[176,128]{1,0:T(8,128)(2,1)S(1)}, bf16[176,128]{1,0:T(8,128)(2,1)S(1)}, u32[]{:S(2)}, u32[]{:S(2)}) collective-permute-start(bf16[176,128]{1,0:T(8,128)(2,1)S(1)} %get-tuple-element.49), channel_id=1, source_target_pairs={{0,4},{2,6},{4,0},{6,2},{1,5},{3,7},{5,1},{7,3},{8,12},{10,14},{12... | collective-permute-start | bytes 135176 | tf_op jit(solution)/shard_map/ppermute | solution.py:91
  131.0 2.8 %collective-permute-done.25.rest_1_ = bf16[336,256]{1,0:T(8,128)(2,1)S(1)} collective-permute-done((bf16[336,256]{1,0:T(8,128)(2,1)S(1)}, bf16[336,256]{1,0:T(8,128)(2,1)S(1)}, u32[]{:S(2)}, u32[]{:S(2)}) %collective-permute-start.25) | collective-permute-done | bytes 172064 | tf_op jit(solution)/shard_map/ppermute | solution.py:91
  133.8 5.1 %collective-permute-done.28.rest_4_ = bf16[176,128]{1,0:T(8,128)(2,1)S(1)} collective-permute-done((bf16[176,128]{1,0:T(8,128)(2,1)S(1)}, bf16[176,128]{1,0:T(8,128)(2,1)S(1)}, u32[]{:S(2)}, u32[]{:S(2)}) %collective-permute-start.28) | collective-permute-done | bytes 45088 | tf_op jit(solution)/shard_map/ppermute | solution.py:91
  138.9 2.0 %outer.1 = (f32[2,400,256]{2,1,0:T(8,128)S(1)}, bf16[2,400,256]{2,1,0:T(8,128)(2,1)S(1)}) custom-call(f32[320,1280]{1,0:T(8,128)S(1)} %outer_own.1.first_ref, bf16[336,256]{1,0:T(8,128)(2,1)S(1)} %collective-permute-done.24.rest_0_, bf16[336,256]{1,0:T(8,128)(2,1)S(1)} %collective-permute-done.25.rest_1_, ...), custom_call_target="tpu_custom_call" | custom-call | tf_op jit(solution)/shard_map/outer/pallas_call | solution.py:610
  141.0 1.7 %collective-permute-done.40.recv_ref = bf16[2,400,256]{2,1,0:T(8,128)(2,1)S(1)} collective-permute-done((bf16[2,400,256]{2,1,0:T(8,128)(2,1)S(1)}, bf16[2,400,256]{2,1,0:T(8,128)(2,1)S(1)}, u32[]{:S(2)}, u32[]{:S(2)}) %collective-permute-start.40) | collective-permute-done | bytes 409632 | tf_op jit(solution)/shard_map/ppermute | solution.py:91
  142.8 1.6 collective-permute-start.41
  146.4 1.9 %back.1 = bf16[256,1280]{1,0:T(8,128)(2,1)} custom-call(bf16[256,1280]{1,0:T(8,128)(2,1)S(1)} %get-tuple-element.41.gz_ref, bf16[1280,1280]{1,0:T(8,128)(2,1)S(1)} %bitcast.4, s32[1,128]{1,0:T(1,128)S(1)} %shard_map.59.rest_0_.rest_1_.rest_2_.rest_3_.rest_4_.rest_5_.rest_6_, s32[1,128]{1,0:T(1,128)S(1)} %shard_map.59.rest_0_.rest_1_.rest_2_.rest_3_.rest_4_.rest_5_.rest_6_, ...), custom_call_target="tpu_custom_call" | custom-call | flops 838860800 | bytes 4587520 | tf_op jit(solution)/shard_map/back/pallas_call | solution.py:595
  148.3 2.6 %collective-permute-done.41.rest_0_ = bf16[400,256]{1,0:T(8,128)(2,1)S(1)} collective-permute-done((bf16[400,256]{1,0:T(8,128)(2,1)S(1)}, bf16[400,256]{1,0:T(8,128)(2,1)S(1)}, u32[]{:S(2)}, u32[]{:S(2)}) %collective-permute-start.41) | collective-permute-done | bytes 204832 | tf_op jit(solution)/shard_map/ppermute | solution.py:91
  150.9 4.8 %collective-permute-done.42.rest_1_ = bf16[400,256]{1,0:T(8,128)(2,1)S(1)} collective-permute-done((bf16[400,256]{1,0:T(8,128)(2,1)S(1)}, bf16[400,256]{1,0:T(8,128)(2,1)S(1)}, u32[]{:S(2)}, u32[]{:S(2)}) %collective-permute-start.42) | collective-permute-done | bytes 204832 | tf_op jit(solution)/shard_map/ppermute | solution.py:91
  (70 shorter events, 29.8 us)
Async XLA Ops:
  1.7 29.6 %collective-permute-start.30 = (bf16[128,1280]{1,0:T(8,128)(2,1)S(1)}, bf16[128,1280]{1,0:T(8,128)(2,1)S(1)}, u32[]{:S(2)}, u32[]{:S(2)}) collective-permute-start(bf16[128,1280]{1,0:T(8,128)(2,1)S(1)} %get-tuple-element.29.rest_0_), channel_id=1, source_target_pairs={{0,2},{2,0},{4,6},{6,4},{1,3},{3,1},{5,7},{7,5},{8,10},{10,8},{12,... | collective-permute-start | bytes 983048 | tf_op jit(solution)/shard_map/ppermute | solution.py:91
  6.2 12.5 %collective-permute-start = (bf16[160,320]{1,0:T(8,128)(2,1)S(1)}, bf16[160,320]{1,0:T(8,128)(2,1)S(1)}, u32[]{:S(2)}, u32[]{:S(2)}) collective-permute-start(bf16[160,320]{1,0:T(8,128)(2,1)S(1)} %get-tuple-element.31.rest_0_), channel_id=1, source_target_pairs={{0,2},{2,0},{4,6},{6,4},{1,3},{3,1},{5,7},{7,5},{8,10},{10,8},{12,... | collective-permute-start | bytes 307208 | tf_op jit(solution)/shard_map/ppermute | solution.py:91
  6.3 16.5 %collective-permute-start.1 = (bf16[160,320]{1,0:T(8,128)(2,1)S(1)}, bf16[160,320]{1,0:T(8,128)(2,1)S(1)}, u32[]{:S(2)}, u32[]{:S(2)}) collective-permute-start(bf16[160,320]{1,0:T(8,128)(2,1)S(1)} %get-tuple-element.31.rest_0_), channel_id=1, source_target_pairs={{0,4},{2,6},{4,0},{6,2},{1,5},{3,7},{5,1},{7,3},{8,12},{10,14},{12... | collective-permute-start | bytes 307208 | tf_op jit(solution)/shard_map/ppermute | solution.py:91
  9.3 23.6 %collective-permute-start.31 = (bf16[128,1280]{1,0:T(8,128)(2,1)S(1)}, bf16[128,1280]{1,0:T(8,128)(2,1)S(1)}, u32[]{:S(2)}, u32[]{:S(2)}) collective-permute-start(bf16[128,1280]{1,0:T(8,128)(2,1)S(1)} %get-tuple-element.30.rest_1_), channel_id=1, source_target_pairs={{0,2},{2,0},{4,6},{6,4},{1,3},{3,1},{5,7},{7,5},{8,10},{10,8},{12,... | collective-permute-start | bytes 983048 | tf_op jit(solution)/shard_map/ppermute | solution.py:91
  10.9 23.5 %collective-permute-start.32 = (bf16[128,1280]{1,0:T(8,128)(2,1)S(1)}, bf16[128,1280]{1,0:T(8,128)(2,1)S(1)}, u32[]{:S(2)}, u32[]{:S(2)}) collective-permute-start(bf16[128,1280]{1,0:T(8,128)(2,1)S(1)} %get-tuple-element.29.rest_0_), channel_id=1, source_target_pairs={{2,4},{4,2},{3,5},{5,3},{10,12},{12,10},{11,13},{13,11},{18,20},{2... | collective-permute-start | bytes 983048 | tf_op jit(solution)/shard_map/ppermute | solution.py:427
  18.7 11.1 %collective-permute-start.2 = (bf16[160,320]{1,0:T(8,128)(2,1)S(1)}, bf16[160,320]{1,0:T(8,128)(2,1)S(1)}, u32[]{:S(2)}, u32[]{:S(2)}) collective-permute-start(bf16[160,320]{1,0:T(8,128)(2,1)S(1)} %get-tuple-element.31.rest_0_), channel_id=1, source_target_pairs={{0,6},{2,4},{4,2},{6,0},{1,7},{3,5},{5,3},{7,1},{8,14},{10,12},{12... | collective-permute-start | bytes 307208 | tf_op jit(solution)/shard_map/ppermute | solution.py:91
  22.7 26.1 %collective-permute-start.12 = (bf16[272,1280]{1,0:T(8,128)(2,1)S(1)}, bf16[272,1280]{1,0:T(8,128)(2,1)S(1)}, u32[]{:S(2)}, u32[]{:S(2)}) collective-permute-start(bf16[272,1280]{1,0:T(8,128)(2,1)S(1)} %get-tuple-element.34.rest_1_.rest_4_), channel_id=1, source_target_pairs={{0,1},{1,0},{2,3},{3,2},{4,5},{5,4},{6,7},{7,6},{8,9},{9,8},{10,11... | collective-permute-start | bytes 2088968 | tf_op jit(solution)/shard_map/ppermute | solution.py:91
  31.3 12.4 %collective-permute-start.3 = (bf16[160,1280]{1,0:T(8,128)(2,1)S(1)}, bf16[160,1280]{1,0:T(8,128)(2,1)S(1)}, u32[]{:S(2)}, u32[]{:S(2)}) collective-permute-start(bf16[160,1280]{1,0:T(8,128)(2,1)S(1)} %join.1.rest_2_), channel_id=1, source_target_pairs={{0,16},{8,24},{16,0},{24,8},{1,17},{9,25},{17,1},{25,9},{2,18},{10... | collective-permute-start | bytes 1228808 | tf_op jit(solution)/shard_map/ppermute | solution.py:91
  32.9 14.4 %collective-permute-start.4 = (bf16[160,1280]{1,0:T(8,128)(2,1)S(1)}, bf16[160,1280]{1,0:T(8,128)(2,1)S(1)}, u32[]{:S(2)}, u32[]{:S(2)}) collective-permute-start(bf16[160,1280]{1,0:T(8,128)(2,1)S(1)} %join.1.rest_2_), channel_id=1, source_target_pairs={{0,1},{1,0},{2,3},{3,2},{4,5},{5,4},{6,7},{7,6},{8,9},{9,8},{10,11... | collective-permute-start | bytes 1228808 | tf_op jit(solution)/shard_map/ppermute | solution.py:91
  34.4 15.9 %collective-permute-start.6 = (bf16[160,1280]{1,0:T(8,128)(2,1)S(1)}, bf16[160,1280]{1,0:T(8,128)(2,1)S(1)}, u32[]{:S(2)}, u32[]{:S(2)}) collective-permute-start(bf16[160,1280]{1,0:T(8,128)(2,1)S(1)} %join.1.rest_2_), channel_id=1, source_target_pairs={{0,8},{8,0},{16,24},{24,16},{1,9},{9,1},{17,25},{25,17},{2,10},{10... | collective-permute-start | bytes 1228808 | tf_op jit(solution)/shard_map/ppermute | solution.py:91
  34.4 24.2 %collective-permute-start.11 = (bf16[272,1280]{1,0:T(8,128)(2,1)S(1)}, bf16[272,1280]{1,0:T(8,128)(2,1)S(1)}, u32[]{:S(2)}, u32[]{:S(2)}) collective-permute-start(bf16[272,1280]{1,0:T(8,128)(2,1)S(1)} %get-tuple-element.34.rest_1_.rest_4_), channel_id=1, source_target_pairs={{0,16},{8,24},{16,0},{24,8},{1,17},{9,25},{17,1},{25,9},{2,18},{10... | collective-permute-start | bytes 2088968 | tf_op jit(solution)/shard_map/ppermute | solution.py:91
  48.8 22.7 %collective-permute-start.13 = (bf16[272,1280]{1,0:T(8,128)(2,1)S(1)}, bf16[272,1280]{1,0:T(8,128)(2,1)S(1)}, u32[]{:S(2)}, u32[]{:S(2)}) collective-permute-start(bf16[272,1280]{1,0:T(8,128)(2,1)S(1)} %collective-permute-done.12.rest_3_.rest_6_), channel_id=1, source_target_pairs={{0,16},{8,24},{16,0},{24,8},{1,17},{9,25},{17,1},{25,9},{2,18},{10... | collective-permute-start | bytes 2088968 | tf_op jit(solution)/shard_map/ppermute | solution.py:91
  50.3 8.3 %collective-permute-start.7 = (bf16[160,1280]{1,0:T(8,128)(2,1)S(1)}, bf16[160,1280]{1,0:T(8,128)(2,1)S(1)}, u32[]{:S(2)}, u32[]{:S(2)}) collective-permute-start(bf16[160,1280]{1,0:T(8,128)(2,1)S(1)} %collective-permute-done.3.rest_3_), channel_id=1, source_target_pairs={{0,8},{8,0},{16,24},{24,16},{1,9},{9,1},{17,25},{25,17},{2,10},{10... | collective-permute-start | bytes 1228808 | tf_op jit(solution)/shard_map/ppermute | solution.py:91
  50.3 8.8 %collective-permute-start.8 = (bf16[160,1280]{1,0:T(8,128)(2,1)S(1)}, bf16[160,1280]{1,0:T(8,128)(2,1)S(1)}, u32[]{:S(2)}, u32[]{:S(2)}) collective-permute-start(bf16[160,1280]{1,0:T(8,128)(2,1)S(1)} %collective-permute-done.4.rest_4_), channel_id=1, source_target_pairs={{0,8},{8,0},{16,24},{24,16},{1,9},{9,1},{17,25},{25,17},{2,10},{10... | collective-permute-start | bytes 1228808 | tf_op jit(solution)/shard_map/ppermute | solution.py:91
  55.4 16.1 %collective-permute-start.9 = (bf16[160,1280]{1,0:T(8,128)(2,1)S(1)}, bf16[160,1280]{1,0:T(8,128)(2,1)S(1)}, u32[]{:S(2)}, u32[]{:S(2)}) collective-permute-start(bf16[160,1280]{1,0:T(8,128)(2,1)S(1)} %collective-permute-done.5.rest_5_), channel_id=1, source_target_pairs={{0,8},{8,0},{16,24},{24,16},{1,9},{9,1},{17,25},{25,17},{2,10},{10... | collective-permute-start | bytes 1228808 | tf_op jit(solution)/shard_map/ppermute | solution.py:91
  58.6 18.1 %collective-permute-start.14 = (bf16[272,1280]{1,0:T(8,128)(2,1)S(1)}, bf16[272,1280]{1,0:T(8,128)(2,1)S(1)}, u32[]{:S(2)}, u32[]{:S(2)}) collective-permute-start(bf16[272,1280]{1,0:T(8,128)(2,1)S(1)} %get-tuple-element.34.rest_1_.rest_4_), channel_id=1, source_target_pairs={{0,8},{8,0},{16,24},{24,16},{1,9},{9,1},{17,25},{25,17},{2,10},{10... | collective-permute-start | bytes 2088968 | tf_op jit(solution)/shard_map/ppermute | solution.py:91
  58.6 19.4 %collective-permute-start.15 = (bf16[272,1280]{1,0:T(8,128)(2,1)S(1)}, bf16[272,1280]{1,0:T(8,128)(2,1)S(1)}, u32[]{:S(2)}, u32[]{:S(2)}) collective-permute-start(bf16[272,1280]{1,0:T(8,128)(2,1)S(1)} %collective-permute-done.11.rest_2_.rest_5_), channel_id=1, source_target_pairs={{0,8},{8,0},{16,24},{24,16},{1,9},{9,1},{17,25},{25,17},{2,10},{10... | collective-permute-start | bytes 2088968 | tf_op jit(solution)/shard_map/ppermute | solution.py:91
  59.1 20.2 %collective-permute-start.16 = (bf16[272,1280]{1,0:T(8,128)(2,1)S(1)}, bf16[272,1280]{1,0:T(8,128)(2,1)S(1)}, u32[]{:S(2)}, u32[]{:S(2)}) collective-permute-start(bf16[272,1280]{1,0:T(8,128)(2,1)S(1)} %collective-permute-done.12.rest_3_.rest_6_), channel_id=1, source_target_pairs={{0,8},{8,0},{16,24},{24,16},{1,9},{9,1},{17,25},{25,17},{2,10},{10... | collective-permute-start | bytes 2088968 | tf_op jit(solution)/shard_map/ppermute | solution.py:91
  71.5 11.7 %collective-permute-start.17 = (bf16[272,1280]{1,0:T(8,128)(2,1)S(1)}, bf16[272,1280]{1,0:T(8,128)(2,1)S(1)}, u32[]{:S(2)}, u32[]{:S(2)}) collective-permute-start(bf16[272,1280]{1,0:T(8,128)(2,1)S(1)} %collective-permute-done.13.rest_4_.rest_7_), channel_id=1, source_target_pairs={{0,8},{8,0},{16,24},{24,16},{1,9},{9,1},{17,25},{25,17},{2,10},{10... | collective-permute-start | bytes 2088968 | tf_op jit(solution)/shard_map/ppermute | solution.py:91
  76.7 22.6 %collective-permute-start.36 = (bf16[128,1280]{1,0:T(8,128)(2,1)S(1)}, bf16[128,1280]{1,0:T(8,128)(2,1)S(1)}, u32[]{:S(2)}, u32[]{:S(2)}) collective-permute-start(bf16[128,1280]{1,0:T(8,128)(2,1)S(1)} %collective-permute-done.32.rest_8_), channel_id=1, source_target_pairs={{2,0},{4,6},{3,1},{5,7},{10,8},{12,14},{11,9},{13,15},{18,16},{20,... | collective-permute-start | bytes 983048 | tf_op jit(solution)/shard_map/ppermute | solution.py:429
  78.0 22.8 %collective-permute-start.37 = (bf16[128,1280]{1,0:T(8,128)(2,1)S(1)}, bf16[128,1280]{1,0:T(8,128)(2,1)S(1)}, u32[]{:S(2)}, u32[]{:S(2)}) collective-permute-start(bf16[128,1280]{1,0:T(8,128)(2,1)S(1)} %collective-permute-done.33.rest_9_), channel_id=1, source_target_pairs={{2,0},{4,6},{3,1},{5,7},{10,8},{12,14},{11,9},{13,15},{18,16},{20,... | collective-permute-start | bytes 983048 | tf_op jit(solution)/shard_map/ppermute | solution.py:429
  79.4 46.7 %collective-permute-start.38 = (bf16[128,1280]{1,0:T(8,128)(2,1)S(1)}, bf16[128,1280]{1,0:T(8,128)(2,1)S(1)}, u32[]{:S(2)}, u32[]{:S(2)}) collective-permute-start(bf16[128,1280]{1,0:T(8,128)(2,1)S(1)} %collective-permute-done.34.rest_10_), channel_id=1, source_target_pairs={{2,0},{4,6},{3,1},{5,7},{10,8},{12,14},{11,9},{13,15},{18,16},{20,... | collective-permute-start | bytes 983048 | tf_op jit(solution)/shard_map/ppermute | solution.py:430
  81.8 44.3 %collective-permute-start.39 = (bf16[128,1280]{1,0:T(8,128)(2,1)S(1)}, bf16[128,1280]{1,0:T(8,128)(2,1)S(1)}, u32[]{:S(2)}, u32[]{:S(2)}) collective-permute-start(bf16[128,1280]{1,0:T(8,128)(2,1)S(1)} %collective-permute-done.35.rest_11_), channel_id=1, source_target_pairs={{2,0},{4,6},{3,1},{5,7},{10,8},{12,14},{11,9},{13,15},{18,16},{20,... | collective-permute-start | bytes 983048 | tf_op jit(solution)/shard_map/ppermute | solution.py:430
  92.9 36.4 %collective-permute-start.24 = (bf16[336,256]{1,0:T(8,128)(2,1)S(1)}, bf16[336,256]{1,0:T(8,128)(2,1)S(1)}, u32[]{:S(2)}, u32[]{:S(2)}) collective-permute-start(bf16[336,256]{1,0:T(8,128)(2,1)S(1)} %get-tuple-element.45), channel_id=1, source_target_pairs={{0,2},{2,0},{4,6},{6,4},{1,3},{3,1},{5,7},{7,5},{8,10},{10,8},{12,... | collective-permute-start | bytes 516104 | tf_op jit(solution)/shard_map/ppermute | solution.py:91
  99.3 18.3 %collective-permute-start.21 = (f32[8,256]{1,0:T(8,128)S(1)}, f32[8,256]{1,0:T(8,128)S(1)}, u32[]{:S(2)}, u32[]{:S(2)}) collective-permute-start(f32[8,256]{1,0:T(8,128)S(1)} %fold_totals.1.rest_0_), channel_id=1, source_target_pairs={{0,2},{2,0},{4,6},{6,4},{1,3},{3,1},{5,7},{7,5},{8,10},{10,8},{12,... | collective-permute-start | bytes 24584 | tf_op jit(solution)/shard_map/ppermute | solution.py:91
  100.8 18.0 %collective-permute-start.22 = (f32[8,256]{1,0:T(8,128)S(1)}, f32[8,256]{1,0:T(8,128)S(1)}, u32[]{:S(2)}, u32[]{:S(2)}) collective-permute-start(f32[8,256]{1,0:T(8,128)S(1)} %fold_totals.1.rest_0_), channel_id=1, source_target_pairs={{0,4},{2,6},{4,0},{6,2},{1,5},{3,7},{5,1},{7,3},{8,12},{10,14},{12... | collective-permute-start | bytes 24584 | tf_op jit(solution)/shard_map/ppermute | solution.py:91
  118.8 15.0 %collective-permute-start.25 = (bf16[336,256]{1,0:T(8,128)(2,1)S(1)}, bf16[336,256]{1,0:T(8,128)(2,1)S(1)}, u32[]{:S(2)}, u32[]{:S(2)}) collective-permute-start(bf16[336,256]{1,0:T(8,128)(2,1)S(1)} %get-tuple-element.46), channel_id=1, source_target_pairs={{0,4},{2,6},{4,0},{6,2},{1,5},{3,7},{5,1},{7,3},{8,12},{10,14},{12... | collective-permute-start | bytes 516104 | tf_op jit(solution)/shard_map/ppermute | solution.py:91
  123.0 10.7 %collective-permute-start.26 = (bf16[336,256]{1,0:T(8,128)(2,1)S(1)}, bf16[336,256]{1,0:T(8,128)(2,1)S(1)}, u32[]{:S(2)}, u32[]{:S(2)}) collective-permute-start(bf16[336,256]{1,0:T(8,128)(2,1)S(1)} %get-tuple-element.47), channel_id=1, source_target_pairs={{0,6},{2,4},{4,2},{6,0},{1,7},{3,5},{5,3},{7,1},{8,14},{10,12},{12... | collective-permute-start | bytes 516104 | tf_op jit(solution)/shard_map/ppermute | solution.py:91
  126.1 12.8 %collective-permute-start.28 = (bf16[176,128]{1,0:T(8,128)(2,1)S(1)}, bf16[176,128]{1,0:T(8,128)(2,1)S(1)}, u32[]{:S(2)}, u32[]{:S(2)}) collective-permute-start(bf16[176,128]{1,0:T(8,128)(2,1)S(1)} %get-tuple-element.49), channel_id=1, source_target_pairs={{0,4},{2,6},{4,0},{6,2},{1,5},{3,7},{5,1},{7,3},{8,12},{10,14},{12... | collective-permute-start | bytes 135176 | tf_op jit(solution)/shard_map/ppermute | solution.py:91
  129.3 9.6 %collective-permute-start.29 = (bf16[176,128]{1,0:T(8,128)(2,1)S(1)}, bf16[176,128]{1,0:T(8,128)(2,1)S(1)}, u32[]{:S(2)}, u32[]{:S(2)}) collective-permute-start(bf16[176,128]{1,0:T(8,128)(2,1)S(1)} %get-tuple-element.50), channel_id=1, source_target_pairs={{0,6},{2,4},{4,2},{6,0},{1,7},{3,5},{5,3},{7,1},{8,14},{10,12},{12... | collective-permute-start | bytes 135176 | tf_op jit(solution)/shard_map/ppermute | solution.py:91
  144.4 11.2 %collective-permute-start.42 = (bf16[400,256]{1,0:T(8,128)(2,1)S(1)}, bf16[400,256]{1,0:T(8,128)(2,1)S(1)}, u32[]{:S(2)}, u32[]{:S(2)}) collective-permute-start(bf16[400,256]{1,0:T(8,128)(2,1)S(1)} %get-tuple-element.55), channel_id=1, source_target_pairs={{0,1},{1,0},{2,3},{3,2},{4,5},{5,4},{6,7},{7,6},{8,9},{9,8},{10,11... | collective-permute-start | bytes 614408 | tf_op jit(solution)/shard_map/ppermute | solution.py:91
  144.9 10.7 %collective-permute-start.43 = (bf16[400,256]{1,0:T(8,128)(2,1)S(1)}, bf16[400,256]{1,0:T(8,128)(2,1)S(1)}, u32[]{:S(2)}, u32[]{:S(2)}) collective-permute-start(bf16[400,256]{1,0:T(8,128)(2,1)S(1)} %get-tuple-element.54), channel_id=1, source_target_pairs={{0,17},{1,16},{8,25},{9,24},{16,1},{17,0},{24,9},{25,8},{2,19},{3,... | collective-permute-start | bytes 614408 | tf_op jit(solution)/shard_map/ppermute | solution.py:416
  (12 other events, 60.7 us)
